TPU v7x, 32 devices: a whole 2x2x4 slice. The times are simulated.
32 devices in a mesh: rep: 2 (over x), fsdp: 16 (over z, y, core).
Axes of the slice: x: 2, y: 2, z: 4, core: 2. Of those that a mesh axis runs over, the one named last changes fastest.
Arguments:
- prompt_rows: bfloat16 [8192, 1024], P(('rep', 'fsdp')), may hold values from -12 to 12
- suffix_rows: bfloat16 [8192, 1024], P(('rep', 'fsdp')), may hold values from -12 to 12
- assignment: int32 [2, 32], P('rep', 'fsdp'), may hold values from 0 to 31, each once within a row
- lengths: int32 [2, 32], P('rep', 'fsdp'), may hold values from 1 to 128, 3072 in all within a row
- attention_gain: bfloat16 [1024], P('fsdp'), may hold values from 0.5 to 1.5
- query_weight: bfloat16 [1024, 2048], P('fsdp'), may hold values from -0.1875 to 0.1875
- key_matrix: bfloat16 [1024, 1024], P('fsdp'), may hold values from -0.1875 to 0.1875
- value_matrix: bfloat16 [1024, 1024], P('fsdp'), may hold values from -0.1875 to 0.1875
- query_gain: bfloat16 [128], P('fsdp'), may hold values from 0.5 to 1.5
- key_norm_gain: bfloat16 [128], P('fsdp'), may hold values from 0.5 to 1.5
- out_weight: bfloat16 [2048, 1024], P('fsdp'), may hold values from -2 to 2
- mlp_gain: bfloat16 [1024], P('fsdp'), may hold values from 0.5 to 1.5
- gate_weight: bfloat16 [1024, 3072], P('fsdp'), may hold values from -0.1875 to 0.1875
- up_weight: bfloat16 [1024, 3072], P('fsdp'), may hold values from -0.1875 to 0.1875
- down_weight: bfloat16 [3072, 1024], P('fsdp'), may hold values from -0.109375 to 0.109375
- prompt_cotangent: bfloat16 [8192, 1024], P(('rep', 'fsdp')), may hold values from -18 to 18
- suffix_cotangent: bfloat16 [8192, 1024], P(('rep', 'fsdp')), may hold values from -18 to 18
Outputs:
- prompt_mixed: bfloat16 [8192, 1024], P(('rep', 'fsdp'))
- suffix_mixed: bfloat16 [8192, 1024], P(('rep', 'fsdp'))
- prompt_grad: float32 [8192, 1024], P(('rep', 'fsdp'))
- suffix_grad: float32 [8192, 1024], P(('rep', 'fsdp'))
- grad_attention_gain: float32 [1024], P('fsdp')
- grad_query_weight: float32 [1024, 2048], P('fsdp')
- grad_key_weight: float32 [1024, 1024], P('fsdp')
- grad_value_weight: float32 [1024, 1024], P('fsdp')
- grad_query_gain: float32 [128], P('fsdp')
- grad_key_gain: float32 [128], P('fsdp')
- grad_out_weight: float32 [2048, 1024], P('fsdp')
- grad_mlp_gain: float32 [1024], P('fsdp')
- grad_gate_weight: float32 [1024, 3072], P('fsdp')
- grad_up_weight: float32 [1024, 3072], P('fsdp')
- grad_down_weight: float32 [3072, 1024], P('fsdp')
- token_norms: float32 [3], replicated
Inputs may be any that keep to these rules, and one draw needn't show every extreme that they name: Each row of assignment is a permutation; so every prompt has exactly 8 continuation slots. Each row of lengths sums to 3072 and holds 128 at least once.
All inputs are finite; a program needn't handle non-finite values. No bound on the sum of `lengths` on one device may be relied on, other than what follows from the above.
Results may differ from a plain program's by a relative error of at most 0.024.
Values may be sent and summed in bfloat16 or wider, within the bound.
A program may use at most 256 MiB of HBM per device.

v0:
```python
from functools import partial

import jax
import jax.numpy as jnp
from jax import lax
from jax.experimental import pallas as pl
from jax.experimental.pallas import tpu as pltpu
from jax.sharding import PartitionSpec as P

MODEL_WIDTH = 1024
QUERY_HEADS = 16
KEY_VALUE_HEADS = 8
HEAD_SIZE = 128
PROMPT_LENGTH = 1024
CONT = 8
CONTINUATION_LEN = 128

norm_epsilon = 1e-06
rope_theta = 1000000.0
masked_score = -1e30
MESH = pl.DeviceIdType.MESH
bf16 = jnp.bfloat16
f32 = jnp.float32

def position(n):
    rep = lax.axis_index("rep")
    rank = lax.axis_index("fsdp")
    return rep, rank // 4, (rank // 2) % 2, rank % 2


def meet(peers):
    barrier = pltpu.get_barrier_semaphore()
    for p in peers:
        pl.semaphore_signal(barrier, inc=1, device_id=p, device_id_type=MESH)
    pl.semaphore_wait(barrier, len(peers))


def remote(src, dst, send, recv, to):
    return pltpu.make_async_remote_copy(src, dst, send, recv, device_id=to, device_id_type=MESH)


def gather_kernel(n, m, k, *refs):
    A = n // 4
    it = iter(refs)
    take = lambda count: [next(it) for _ in range(count)]
    own, (tile,), pieces = take(m), take(1), take(k)
    full, (tiles,), staged = take(m), take(1), take(k)
    zs, zr, s2s, s2r, s3s, s3r, cs, cr, ls, ts, tr, ps, pr, pls = take(14)
    rep, a, b, c = position(n)
    me = (a * 2 + b) * 2 + c
    h = rep % 2
    mate = rep + 1 - 2 * h

    def dev(r, a, b, c):
        return (r, (a * 2 + b) * 2 + c)

    meet([(rep, (me + d) % n) for d in range(1, n)] + [dev(mate, a, b, c)])
    ydev, xdev, cdev = dev(rep, a, 1 - b, c), dev(mate, a, b, c), dev(rep, a, b, 1 - c)

    def local(i):
        return pltpu.make_async_copy(own[i].at[:, h], full[i].at[a, b, c, :, h], ls.at[i])

    def along(i, d):
        return remote(own[i].at[:, h], full[i].at[a, b, c, :, h], zs.at[i, d - 1], zr.at[i, d - 1], dev(rep, (a + d) % A, b, c))

    def s2(i):
        y, x = full[i].at[:, b, c, 0, h], full[i].at[:, b, c, 1, h]
        return [remote(y, y, s2s.at[i, 0], s2r.at[i, 0], ydev), remote(x, x, s2s.at[i, 1], s2r.at[i, 1], xdev)]

    def s3(i):
        x, y = full[i].at[:, :, c, 0, h], full[i].at[:, b, c, 1]
        return [remote(x, x, s3s.at[i, 0], s3r.at[i, 0], xdev), remote(y, y, s3s.at[i, 1], s3r.at[i, 1], ydev)]

    def s4(i):
        both = full[i].at[:, :, c]
        return [remote(both, both, cs.at[i], cr.at[i], cdev)]

    def share(d):
        return remote(tile, tiles.at[me], ts.at[d - 1], tr.at[d - 1], (rep, (me + d) % n))

    def piece(i, d):
        to = (me + d) % n
        return remote(pieces[i].at[:, to], staged[i].at[me], ps.at[i, d - 1], pr.at[i, d - 1], (rep, to))

    def own_piece(i):
        return pltpu.make_async_copy(pieces[i].at[:, me], staged[i].at[me], pls.at[i])

    for d in range(1, n):
        share(d).start()
    tiles[me] = tile[...]
    for i in range(k):
        own_piece(i).start()
        for d in range(1, n):
            piece(i, d).start()
    for i in range(m):
        local(i).start()
        for d in range(1, A):
            along(i, d).start()
    for t in range(m + 3):
        if t < m:
            local(t).wait()
            for d in range(1, A):
                along(t, d).wait_recv()
            for q in s2(t):
                q.start()
        if 0 <= t - 1 < m:
            for q in s2(t - 1):
                q.wait_recv()
            for q in s3(t - 1):
                q.start()
        if 0 <= t - 2 < m:
            for q in s3(t - 2):
                q.wait_recv()
            for q in s4(t - 2):
                q.start()
        if 0 <= t - 3 < m:
            for q in s4(t - 3):
                q.wait_recv()
    for d in range(1, n):
        share(d).wait()
    for i in range(k):
        own_piece(i).wait()
        for d in range(1, n):
            piece(i, d).wait()
    for t in range(m):
        for d in range(1, A):
            along(t, d).wait_send()
        for q in s2(t) + s3(t) + s4(t):
            q.wait_send()


def gather(shards, tile, slots, n, cid):
    m, k, A = len(shards), len(slots), n // 4
    views = [s.reshape(2, 2, s.shape[0] // 4, s.shape[1]) for s in shards]
    outs = [jax.ShapeDtypeStruct((A, 2, 2) + v.shape, v.dtype) for v in views]
    outs += [jax.ShapeDtypeStruct((n,) + tile.shape, tile.dtype)]
    outs += [jax.ShapeDtypeStruct((n, s.shape[0]) + s.shape[2:], s.dtype) for s in slots]
    D = pltpu.SemaphoreType.DMA
    vm, hbm = pl.BlockSpec(memory_space=pltpu.VMEM), pl.BlockSpec(memory_space=pl.ANY)
    res = pl.pallas_call(
        partial(gather_kernel, n, m, k),
        out_shape=outs,
        in_specs=[vm] * (m + 1 + k),
        out_specs=[hbm] * m + [vm] + [hbm] * k,
        scratch_shapes=[D((m, A - 1))] * 2 + [D((m, 2))] * 4 + [D((m,))] * 3 + [D((n - 1,))] * 2 + [D((max(k, 1), n - 1))] * 2 + [D((max(k, 1),))],
        compiler_params=pltpu.CompilerParams(collective_id=cid, has_side_effects=True),
        name="gather",
    )(*views, tile, *slots)
    return [f.reshape(-1, s.shape[1]) for f, s in zip(res, shards)], res[m], res[m + 1:]


def spread_kernel(n, k, *refs):
    it = iter(refs)
    take = lambda count: [next(it) for _ in range(count)]
    pieces, staged, (ps, pr, pls) = take(k), take(k), take(3)
    rep, a, b, c = position(n)
    me = (a * 2 + b) * 2 + c
    meet([(rep, (me + d) % n) for d in range(1, n)])

    def piece(i, d):
        to = (me + d) % n
        return remote(pieces[i].at[:, to], staged[i].at[me], ps.at[i, d - 1], pr.at[i, d - 1], (rep, to))

    def own_piece(i):
        return pltpu.make_async_copy(pieces[i].at[:, me], staged[i].at[me], pls.at[i])

    for i in range(k):
        own_piece(i).start()
        for d in range(1, n):
            piece(i, d).start()
    for i in range(k):
        own_piece(i).wait()
        for d in range(1, n):
            piece(i, d).wait()


def spread(slots, n, cid):
    k = len(slots)
    D = pltpu.SemaphoreType.DMA
    vm, hbm = pl.BlockSpec(memory_space=pltpu.VMEM), pl.BlockSpec(memory_space=pl.ANY)
    return pl.pallas_call(
        partial(spread_kernel, n, k),
        out_shape=[jax.ShapeDtypeStruct((n, s.shape[0]) + s.shape[2:], s.dtype) for s in slots],
        in_specs=[vm] * k,
        out_specs=[hbm] * k,
        scratch_shapes=[D((k, n - 1))] * 2 + [D((k,))],
        compiler_params=pltpu.CompilerParams(collective_id=cid, has_side_effects=True),
        name="spread",
    )(*slots)


def collect_kernel(n, k, *refs):
    it = iter(refs)
    take = lambda count: [next(it) for _ in range(count)]
    (index,), staged, final, ordered, (ps, pr, pls) = take(1), take(k), take(k), take(k), take(3)
    rep, a, b, c = position(n)
    me = (a * 2 + b) * 2 + c
    meet([(rep, (me + d) % n) for d in range(1, n)])
    S = ordered[0].shape[1]
    for i in range(k):
        def place(j, _):
            ordered[i][j // S, j % S] = staged[i][index[j]]
            return 0
        lax.fori_loop(0, n * S, place, 0)

    def piece(i, d):
        to = (me + d) % n
        return remote(ordered[i].at[to], final[i].at[:, me], ps.at[i, d - 1], pr.at[i, d - 1], (rep, to))

    def own_piece(i):
        return pltpu.make_async_copy(ordered[i].at[me], final[i].at[:, me], pls.at[i])

    for i in range(k):
        own_piece(i).start()
        for d in range(1, n):
            piece(i, d).start()
    for i in range(k):
        own_piece(i).wait()
        for d in range(1, n):
            piece(i, d).wait()


def collect(index, staged, n, cid):
    k = len(staged)
    flat = [s.reshape((-1,) + s.shape[2:]) for s in staged]
    D = pltpu.SemaphoreType.DMA
    vm, hbm, sm = pl.BlockSpec(memory_space=pltpu.VMEM), pl.BlockSpec(memory_space=pl.ANY), pl.BlockSpec(memory_space=pltpu.SMEM)
    return pl.pallas_call(
        partial(collect_kernel, n, k),
        out_shape=[jax.ShapeDtypeStruct((s.shape[1], n) + s.shape[2:], s.dtype) for s in staged],
        in_specs=[sm] + [vm] * k,
        out_specs=[hbm] * k,
        scratch_shapes=[pltpu.VMEM(s.shape, s.dtype) for s in staged] + [D((k, n - 1))] * 2 + [D((k,))],
        compiler_params=pltpu.CompilerParams(collective_id=cid, has_side_effects=True),
        name="collect",
    )(index, *flat)


def add_rows(count, out, first, second, step=None):
    def one(j, _):
        o = out(j)
        total = first(j)[...].astype(jnp.float32)
        for s in second:
            total = total + s(j)[...].astype(jnp.float32)
        o[...] = total.astype(o.dtype)
        return 0
    lax.fori_loop(0, count, one, 0)

def scatter_kernel(n, R, m, has_vec, *refs):
    A = n // 4
    bits = R.bit_length() - 1
    it = iter(refs)
    take = lambda k: [next(it) for _ in range(k)]
    grads = take(m)
    vec = next(it) if has_vec else None
    outs = take(m)
    vout = next(it) if has_vec else None
    own, b1, b2y, b2x, b3, b4, b5 = [take(m) for _ in range(7)]
    s4 = take(m)
    vb = next(it) if has_vec else None
    vz = next(it) if has_vec else None
    ls, s1s, s1r, s2s, s2r, s3s, s3r, s4s, s4r, s5s, s5r, ws = take(12)
    if has_vec:
        vs, vr = take(2)
    rep, a, b, c = position(n)
    h = rep % 2
    mate = rep + 1 - 2 * h
    def dev(r, a, b, c):
        return (r, (a * 2 + b) * 2 + c)
    ydev, xdev, cdev = dev(rep, a, 1 - b, c), dev(mate, a, b, c), dev(rep, a, b, 1 - c)
    zdev = lambda d: dev(rep, (a + d) % A, b, c)
    def flip(bit):
        w = 1 << bit
        return dev(rep + w - 2 * w * ((rep // w) % 2), a, b, c)
    barrier = pltpu.get_barrier_semaphore()
    peers = [zdev(d) for d in range(1, A)] + [ydev, xdev, cdev] + [flip(k) for k in range(1, bits)]
    for p in peers:
        pl.semaphore_signal(barrier, inc=1, device_id=p, device_id_type=MESH)
    pl.semaphore_wait(barrier, len(peers))
    def rc(src, dst, ss, rs, to):
        return pltpu.make_async_remote_copy(src, dst, ss, rs, device_id=to, device_id_type=MESH)
    def load(i): return pltpu.make_async_copy(grads[i].at[:, :, c], own[i], ls.at[i])
    def S1(i): return [rc(grads[i].at[:, :, 1 - c], b1[i], s1s.at[i], s1r.at[i], cdev)]
    def S2(i): return [rc(b1[i].at[:, 1 - b, 0], b2y[i], s2s.at[i, 0], s2r.at[i, 0], ydev),
                       rc(b1[i].at[:, :, 1, 1 - h], b2x[i], s2s.at[i, 1], s2r.at[i, 1], xdev)]
    def S3(i): return [rc(b2y[i].at[:, 1 - h], b3[i].at[0], s3s.at[i, 0], s3r.at[i, 0], xdev),
                       rc(b2x[i].at[:, 1 - b], b3[i].at[1], s3s.at[i, 1], s3r.at[i, 1], ydev)]
    def S4(i): return [rc(b3[i].at[:, (a + d) % A], b4[i].at[d - 1], s4s.at[i, d - 1], s4r.at[i, d - 1], zdev(d)) for d in range(1, A)]
    def S5(i, k): return rc(s4[i].at[0] if k == bits - 1 else s4[i].at[k], b5[i].at[k], s5s.at[i, k], s5r.at[i, k], xdev if k == bits - 1 else flip(k + 1))
    def put(i, k): return pltpu.make_async_copy((s4[i].at[0] if bits == 1 else s4[i].at[bits - 1]) if k == 0 else b5[i].at[bits - 1], outs[i].at[:, h if k == 0 else 1 - h], ws.at[i, k])
    for i in range(m):
        load(i).start()
        for q in S1(i): q.start()
    if has_vec:
        rounds = [cdev, ydev, xdev] + [flip(k) for k in range(1, bits)]
        vb[0] = vec[...]
        for k, to in enumerate(rounds):
            q = rc(vb.at[2 * k], vb.at[2 * k + 1], vs.at[k], vr.at[k], to)
            q.start(); q.wait()
            vb[2 * k + 2] = vb[2 * k] + vb[2 * k + 1]
        last = 2 * len(rounds)
        nr = len(rounds)
        qs = [rc(vb.at[last], vz.at[a], vs.at[nr + d - 1], vr.at[nr + d - 1], zdev(d)) for d in range(1, A)]
        for q in qs: q.start()
        vz[a] = vb[last]
        for q in qs: q.wait()
        total = vz[0]
        for k in range(1, A):
            total = total + vz[k]
        vout[...] = total
    for t in range(m + 4):
        i = t
        if t < m:
            load(i).wait()
            for q in S1(i): q.wait_recv()
            add_rows(A * 2 * 4, lambda j, i=i: b1[i].at[j // 8, (j // 4) % 2, (j // 2) % 2, j % 2],
                     lambda j, i=i: b1[i].at[j // 8, (j // 4) % 2, (j // 2) % 2, j % 2],
                     [lambda j, i=i: own[i].at[j // 8, (j // 4) % 2, (j // 2) % 2, j % 2]])
            for q in S2(i): q.start()
        i = t - 1
        if 0 <= i < m:
            for q in S2(i): q.wait_recv()
            add_rows(A * 2, lambda j, i=i: b2y[i].at[j // 2, j % 2], lambda j, i=i: b2y[i].at[j // 2, j % 2],
                     [lambda j, i=i: b1[i].at[j // 2, b, 0, j % 2]])
            add_rows(A * 2, lambda j, i=i: b2x[i].at[j // 2, j % 2], lambda j, i=i: b2x[i].at[j // 2, j % 2],
                     [lambda j, i=i: b1[i].at[j // 2, j % 2, 1, h]])
            for q in S3(i): q.start()
        i = t - 2
        if 0 <= i < m:
            for q in S3(i): q.wait_recv()
            add_rows(A, lambda j, i=i: b3[i].at[0, j], lambda j, i=i: b3[i].at[0, j], [lambda j, i=i: b2y[i].at[j, h]])
            add_rows(A, lambda j, i=i: b3[i].at[1, j], lambda j, i=i: b3[i].at[1, j], [lambda j, i=i: b2x[i].at[j, b]])
            for q in S4(i): q.start()
        i = t - 3
        if 0 <= i < m:
            for q in S4(i): q.wait_recv()
            add_rows(2, lambda j, i=i: s4[i].at[0, j], lambda j, i=i: b3[i].at[j, a], [lambda j, i=i, d=d: b4[i].at[d, j] for d in range(A - 1)])
            for k in range(bits - 1):
                q = S5(i, k); q.start(); q.wait()
                add_rows(2, lambda j, i=i, k=k: s4[i].at[k + 1, j], lambda j, i=i, k=k: s4[i].at[k, j], [lambda j, i=i, k=k: b5[i].at[k, j]])
            rc(s4[i].at[bits - 1], b5[i].at[bits - 1], s5s.at[i, bits - 1], s5r.at[i, bits - 1], xdev).start()
            put(i, 0).start()
        i = t - 4
        if 0 <= i < m:
            rc(s4[i].at[bits - 1], b5[i].at[bits - 1], s5s.at[i, bits - 1], s5r.at[i, bits - 1], xdev).wait_recv()
            put(i, 1).start()
    for i in range(m):
        for q in S1(i) + S2(i) + S3(i) + S4(i): q.wait_send()
        rc(s4[i].at[bits - 1], b5[i].at[bits - 1], s5s.at[i, bits - 1], s5r.at[i, bits - 1], xdev).wait_send()
        put(i, 0).wait(); put(i, 1).wait()

def scatter(grads, n, R, cid, vec=None):
    m, A, bits = len(grads), n // 4, R.bit_length() - 1
    views = [g.reshape(A, 2, 2, 2, 2, g.shape[0] // (4 * n), g.shape[1]) for g in grads]
    sub = [v.shape[-2:] for v in views]
    bf = jnp.bfloat16
    V, D = pltpu.VMEM, pltpu.SemaphoreType.DMA
    scratch = ([V((A, 2, 2, 2) + s, bf) for s in sub] * 2 + [V((A, 2) + s, bf) for s in sub] * 2 + [V((2, A) + s, bf) for s in sub]
        + [V((A - 1, 2) + s, bf) for s in sub] + [V((bits, 2) + s, bf) for s in sub] + [V((bits, 2) + s, bf) for s in sub])
    ins, ispec = list(views), [pl.BlockSpec(memory_space=pl.ANY)] * m
    outs, ospec = [jax.ShapeDtypeStruct((2, 2) + s, bf) for s in sub], [pl.BlockSpec(memory_space=pl.ANY)] * m
    sems = [D((m,)), D((m,)), D((m,)), D((m, 2)), D((m, 2)), D((m, 2)), D((m, 2)), D((m, A - 1)), D((m, A - 1)), D((m, bits)), D((m, bits)), D((m, 2))]
    if vec is not None:
        ins.append(vec); ispec.append(pl.BlockSpec(memory_space=pltpu.VMEM))
        outs.append(jax.ShapeDtypeStruct(vec.shape, vec.dtype)); ospec.append(pl.BlockSpec(memory_space=pltpu.VMEM))
        scratch += [V((2 * (2 + bits) + 1,) + vec.shape, vec.dtype), V((A,) + vec.shape, vec.dtype)]
        sems += [D((2 + bits + A - 1,))] * 2
    res = pl.pallas_call(partial(scatter_kernel, n, R, m, vec is not None), out_shape=outs, in_specs=ispec, out_specs=ospec,
        scratch_shapes=scratch + sems,
        compiler_params=pltpu.CompilerParams(collective_id=cid, has_side_effects=True, vmem_limit_bytes=60 << 20),
        name="scatter")(*ins)
    shards = [r.reshape(-1, r.shape[-1]) for r in res[:m]]
    return (shards, res[m]) if vec is not None else shards


LOG2E = 1.4426950408889634


def mm(x, y, cx, cy):
    return lax.dot_general(x, y, (((cx,), (cy,)), ((), ())), preferred_element_type=f32)


def keys_kernel(n, group, k_pre, v, gain, cos, sin, k_out, ks, vs, fs, fr, gs, gr, ls):
    rows = ks.shape[2]
    half = group // 2
    rep, a, b, c = position(n)
    me = (a * 2 + b) * 2 + c
    first = (me // group) * half
    slot = (me // 2) % half

    def at(s, c):
        return (rep, (first + s) * 2 + c)

    others = [(slot + d) % half for d in range(1, half)]
    meet([at(s, c) for s in others] + [at(slot, 1 - c)])

    def head(j, _):
        lanes = pl.ds(pl.multiple_of(j * HEAD_SIZE, HEAD_SIZE), HEAD_SIZE)
        x = k_pre[:, lanes]
        x = x * lax.rsqrt(jnp.mean(x * x, axis=-1, keepdims=True) + norm_epsilon) * gain[...]
        k_out[:, lanes] = (x * cos[...] + pltpu.roll(x, HEAD_SIZE // 2, 1) * sin[...]).astype(bf16)
        return 0

    lax.fori_loop(0, KEY_VALUE_HEADS, head, 0)
    parts = [(k_out, ks), (v, vs)]

    def local(i):
        return pltpu.make_async_copy(parts[i][0].at[pl.ds(0, rows)], parts[i][1].at[slot, c], ls.at[i])

    def across(i, d):
        return remote(parts[i][0].at[pl.ds(0, rows)], parts[i][1].at[slot, c], fs.at[i, d - 1], fr.at[i, d - 1], at((slot + d) % half, c))

    def sibling(i, d):
        if d == 0:
            return remote(parts[i][0].at[pl.ds(0, rows)], parts[i][1].at[slot, c], gs.at[i, d], gr.at[i, d], at(slot, 1 - c))
        there = parts[i][1].at[(slot + half - d) % half, c]
        return remote(there, there, gs.at[i, d], gr.at[i, d], at(slot, 1 - c))

    for i in range(2):
        for d in range(1, half):
            across(i, d).start()
        sibling(i, 0).start()
        local(i).start()
    for i in range(2):
        for d in range(1, half):
            across(i, d).wait_recv()
            sibling(i, d).start()
    for i in range(2):
        local(i).wait()
        sibling(i, 0).wait()
        for d in range(1, half):
            across(i, d).wait_send()
            sibling(i, d).wait()


def gather_keys(k_pre, v, gain, cos, sin, rows, n, cid):
    group = PROMPT_LENGTH // rows
    half = group // 2
    width = k_pre.shape[1]
    D = pltpu.SemaphoreType.DMA
    vm, hbm = pl.BlockSpec(memory_space=pltpu.VMEM), pl.BlockSpec(memory_space=pl.ANY)
    wide = jax.ShapeDtypeStruct((half, 2, rows, width), bf16)
    k_rot, ks, vs = pl.pallas_call(
        partial(keys_kernel, n, group),
        out_shape=[jax.ShapeDtypeStruct(k_pre.shape, bf16), wide, wide],
        in_specs=[vm] * 5,
        out_specs=[vm, hbm, hbm],
        scratch_shapes=[D((2, max(half - 1, 1)))] * 2 + [D((2, half))] * 2 + [D((2,))],
        compiler_params=pltpu.CompilerParams(collective_id=cid, has_side_effects=True),
        name="prompt_keys",
    )(k_pre, v, gain, cos, sin)
    return k_rot, ks.reshape(PROMPT_LENGTH, width), vs.reshape(PROMPT_LENGTH, width)


def key_grads_kernel(n, group, dk, dv, dks, dvs, k_pre, gain, cos, sin, dk_out, dv_out, g_out, s1, r1, s2, r2, dk_rot, gs, gr, fs, fr):
    rows = dk.shape[2]
    half = group // 2
    rep, a, b, c = position(n)
    me = (a * 2 + b) * 2 + c
    first = (me // group) * half
    slot = (me // 2) % half

    def at(s, c):
        return (rep, (first + s) * 2 + c)

    meet([at((slot + d) % half, c) for d in range(1, half)] + [at(slot, 1 - c)])
    parts = [dk, dv]

    def to_sibling(i, d):
        s = (slot + d) % half
        return remote(parts[i].at[s, 1 - c], r1.at[i, d], gs.at[i, d], gr.at[i, d], at(slot, 1 - c))

    def across(i, d):
        return remote(s1.at[i, d], r2.at[i, d - 1], fs.at[i, d - 1], fr.at[i, d - 1], at((slot + d) % half, c))

    order = list(range(1, half)) + [0]
    for d in order:
        for i in range(2):
            to_sibling(i, d).start()
    for d in order:
        for i in range(2):
            to_sibling(i, d).wait_recv()
            s1[i, d] = (parts[i][(slot + d) % half, c].astype(f32) + r1[i, d].astype(f32)).astype(bf16)
            if d:
                across(i, d).start()
    for i in range(2):
        for d in range(1, half):
            across(i, d).wait_recv()

    def total(i):
        t = s1[i, 0].astype(f32)
        for d in range(1, half):
            t = t + r2[i, d - 1].astype(f32)
        return t

    dv_out[pl.ds(0, rows), :] = total(1).astype(bf16)
    dv_out[pl.ds(rows, dvs.shape[0]), :] = dvs[...].astype(bf16)
    dk_rot[pl.ds(0, rows), :] = total(0)
    dk_rot[pl.ds(rows, dks.shape[0]), :] = dks[...].astype(f32)
    g_out[...] = jnp.zeros_like(g_out)

    def head(j, _):
        lanes = pl.ds(pl.multiple_of(j * HEAD_SIZE, HEAD_SIZE), HEAD_SIZE)
        x = k_pre[:, lanes]
        rs = lax.rsqrt(jnp.mean(x * x, axis=-1, keepdims=True) + norm_epsilon)
        unit = x * rs
        dy = dk_rot[:, lanes]
        dy = dy * cos[...] - pltpu.roll(dy, HEAD_SIZE // 2, 1) * sin[...]
        g_out[0:1, :] += jnp.sum(dy * unit, axis=0, keepdims=True)
        dy = dy * gain[...]
        dk_out[:, lanes] = (rs * (dy - unit * jnp.mean(dy * unit, axis=-1, keepdims=True))).astype(bf16)
        return 0

    lax.fori_loop(0, KEY_VALUE_HEADS, head, 0)
    for i in range(2):
        for d in range(half):
            to_sibling(i, d).wait_send()
            if d:
                across(i, d).wait_send()


def key_grads(dk, dv, dks, dvs, k_pre, gain, cos, sin, rows, n, cid):
    group = PROMPT_LENGTH // rows
    half = group // 2
    width = k_pre.shape[1]
    D = pltpu.SemaphoreType.DMA
    vm = pl.BlockSpec(memory_space=pltpu.VMEM)
    V = pltpu.VMEM
    block = (rows, width)
    return pl.pallas_call(
        partial(key_grads_kernel, n, group),
        out_shape=[jax.ShapeDtypeStruct(k_pre.shape, bf16), jax.ShapeDtypeStruct(k_pre.shape, bf16), jax.ShapeDtypeStruct((8, HEAD_SIZE), f32)],
        in_specs=[vm] * 8,
        out_specs=[vm] * 3,
        scratch_shapes=[V((2, half) + block, bf16), V((2, half) + block, bf16), V((1, 8, 128), bf16), V((2, max(half - 1, 1)) + block, bf16), V(k_pre.shape, f32)]
        + [D((2, half))] * 2 + [D((2, max(half - 1, 1)))] * 2,
        compiler_params=pltpu.CompilerParams(collective_id=cid, has_side_effects=True, vmem_limit_bytes=60 << 20),
        name="prompt_key_grads",
    )(dk.reshape(half, 2, rows, width), dv.reshape(half, 2, rows, width), dks, dvs, k_pre, gain, cos, sin)


def attend_kernel(rows, q_pre, ks, vs, k_own, v_own, gain, cos, sin, past, inside, out, q_out, lse_out, rs_out):
    scale = HEAD_SIZE ** -0.5 * LOG2E
    for g in range(QUERY_HEADS // KEY_VALUE_HEADS):
        lanes = slice(g * HEAD_SIZE, (g + 1) * HEAD_SIZE)
        q = q_pre[:, lanes].T
        rs = lax.rsqrt(jnp.mean(q * q, axis=0, keepdims=True) + norm_epsilon)
        rs_out[0, g:g + 1, :] = rs
        q = q * rs * gain[:, 0:1]
        lo, hi = q[:HEAD_SIZE // 2], q[HEAD_SIZE // 2:]
        q = jnp.concatenate([lo * cos[...] - hi * sin[...], hi * cos[...] + lo * sin[...]], axis=0).astype(bf16)
        q_out[lanes, :] = q
        p = jnp.exp2(mm(ks[...], q[:, :rows], 1, 0) * scale + past[...])
        total = jnp.sum(p, axis=0, keepdims=True)
        o = mm(vs[...], p.astype(bf16), 0, 0) / total
        out[:rows, lanes] = o.T.astype(bf16)
        lse_out[0, g:g + 1, :rows] = jnp.log2(total)
        p = jnp.exp2(mm(ks[...], q[:, rows:], 1, 0) * scale)
        r = jnp.exp2(mm(k_own[rows:, :], q[:, rows:], 1, 0) * scale + inside[...])
        total = jnp.sum(p, axis=0, keepdims=True) + jnp.sum(r, axis=0, keepdims=True)
        o = (mm(vs[...], p.astype(bf16), 0, 0) + mm(v_own[rows:, :], r.astype(bf16), 0, 0)) / total
        out[rows:, lanes] = o.T.astype(bf16)
        lse_out[0, g:g + 1, rows:] = jnp.log2(total)


def attend(q_pre, ks, vs, k_own, v_own, gain, cos, sin, past, inside, rows):
    total = q_pre.shape[0]
    pair = 2 * HEAD_SIZE
    whole = lambda x: pl.BlockSpec(x.shape, lambda j: (0,) * x.ndim)
    col = lambda r, w: pl.BlockSpec((r, w), lambda j: (0, j))
    small = pl.BlockSpec((1, 2, total), lambda j: (j, 0, 0))
    return pl.pallas_call(
        partial(attend_kernel, rows),
        grid=(KEY_VALUE_HEADS,),
        in_specs=[col(total, pair), col(PROMPT_LENGTH, HEAD_SIZE), col(PROMPT_LENGTH, HEAD_SIZE), col(total, HEAD_SIZE), col(total, HEAD_SIZE),
                  whole(gain), whole(cos), whole(sin), whole(past), whole(inside)],
        out_specs=[col(total, pair), pl.BlockSpec((pair, total), lambda j: (j, 0)), small, small],
        out_shape=[jax.ShapeDtypeStruct((total, QUERY_HEADS * HEAD_SIZE), bf16), jax.ShapeDtypeStruct((QUERY_HEADS * HEAD_SIZE, total), bf16),
                   jax.ShapeDtypeStruct((KEY_VALUE_HEADS, 2, total), f32), jax.ShapeDtypeStruct((KEY_VALUE_HEADS, 2, total), f32)],
        compiler_params=pltpu.CompilerParams(vmem_limit_bytes=60 << 20),
        name="attend",
    )(q_pre, ks, vs, k_own, v_own, gain, cos, sin, past, inside)


def attend_back_kernel(rows, q_rot, ks, vs, k_own, v_own, d_out, out, lse, rs_in, gain, cos, sin, past, inside, dq_out, dk_out, dv_out, dks_out, dvs_out, g_out):
    scale = HEAD_SIZE ** -0.5
    dk = dv = dks = dvs = None
    plus = lambda x, y: y if x is None else x + y
    gain_grad = None
    for g in range(QUERY_HEADS // KEY_VALUE_HEADS):
        lanes = slice(g * HEAD_SIZE, (g + 1) * HEAD_SIZE)
        q = q_rot[lanes, :]
        do = d_out[:, lanes]
        delta = jnp.sum((do.astype(f32) * out[:, lanes].astype(f32)).T, axis=0, keepdims=True)
        log_total = lse[0, g:g + 1, :]
        dq = []
        for suffix in range(2):
            part = slice(rows, None) if suffix else slice(0, rows)
            qp, dop, lp, dp = q[:, part], do[part], log_total[:, part], delta[:, part]
            blocks = [(ks[...], vs[...], None if suffix else past[...])]
            if suffix:
                blocks.append((k_own[rows:, :], v_own[rows:, :], inside[...]))
            dqp = None
            for i, (kb, vb, bias) in enumerate(blocks):
                s = mm(kb, qp, 1, 0) * (scale * LOG2E) - lp
                p = jnp.exp2(s if bias is None else s + bias)
                ds = (p * (mm(vb, dop, 1, 1) - dp)).astype(bf16)
                dvp = mm(p.astype(bf16), dop, 1, 0)
                dkp = mm(ds, qp, 1, 1)
                dqp = plus(dqp, mm(kb, ds, 0, 0))
                if i:
                    dks, dvs = plus(dks, dkp), plus(dvs, dvp)
                else:
                    dk, dv = plus(dk, dkp), plus(dv, dvp)
            dq.append(dqp)
        dq = jnp.concatenate(dq, axis=1) * scale
        half = HEAD_SIZE // 2
        c, s = cos[...], sin[...]
        dy = jnp.concatenate([dq[:half] * c + dq[half:] * s, dq[half:] * c - dq[:half] * s], axis=0)
        qf = q.astype(f32)
        unit = jnp.concatenate([qf[:half] * c + qf[half:] * s, qf[half:] * c - qf[:half] * s], axis=0) / gain[:, 0:1]
        gg = dy * unit
        for t in range(gg.shape[1] // 128):
            gain_grad = plus(gain_grad, gg[:, t * 128:(t + 1) * 128])
        dy = dy * gain[:, 0:1]
        dx = rs_in[0, g:g + 1, :] * (dy - unit * jnp.mean(dy * unit, axis=0, keepdims=True))
        dq_out[:, lanes] = dx.T.astype(bf16)
    dk_out[...] = (dk * scale).astype(bf16)
    dv_out[...] = dv.astype(bf16)
    dks_out[...] = (dks * scale).astype(bf16)
    dvs_out[...] = dvs.astype(bf16)

    @pl.when(pl.program_id(0) == 0)
    def _():
        g_out[...] = gain_grad

    @pl.when(pl.program_id(0) > 0)
    def _():
        g_out[...] += gain_grad


def attend_back(q_rot, ks, vs, k_own, v_own, d_out, out, lse, rs, gain, cos, sin, past, inside, rows):
    total = k_own.shape[0]
    pair = 2 * HEAD_SIZE
    whole = lambda x: pl.BlockSpec(x.shape, lambda j: (0,) * x.ndim)
    col = lambda r, w: pl.BlockSpec((r, w), lambda j: (0, j))
    small = pl.BlockSpec((1, 2, total), lambda j: (j, 0, 0))
    width = KEY_VALUE_HEADS * HEAD_SIZE
    kv, own = jax.ShapeDtypeStruct((PROMPT_LENGTH, width), bf16), jax.ShapeDtypeStruct((total - rows, width), bf16)
    return pl.pallas_call(
        partial(attend_back_kernel, rows),
        grid=(KEY_VALUE_HEADS,),
        in_specs=[pl.BlockSpec((pair, total), lambda j: (j, 0)), col(PROMPT_LENGTH, HEAD_SIZE), col(PROMPT_LENGTH, HEAD_SIZE), col(total, HEAD_SIZE),
                  col(total, HEAD_SIZE), col(total, pair), col(total, pair), small, small, whole(gain), whole(cos), whole(sin), whole(past), whole(inside)],
        out_specs=[col(total, pair), col(PROMPT_LENGTH, HEAD_SIZE), col(PROMPT_LENGTH, HEAD_SIZE), col(total - rows, HEAD_SIZE), col(total - rows, HEAD_SIZE),
                   pl.BlockSpec((HEAD_SIZE, 128), lambda j: (0, 0))],
        out_shape=[jax.ShapeDtypeStruct((total, QUERY_HEADS * HEAD_SIZE), bf16), kv, kv, own, own, jax.ShapeDtypeStruct((HEAD_SIZE, 128), f32)],
        compiler_params=pltpu.CompilerParams(vmem_limit_bytes=60 << 20),
        name="attend_back",
    )(q_rot, ks, vs, k_own, v_own, d_out, out, lse, rs, gain, cos, sin, past, inside)


class Ring:
    def __init__(self, n, own, full, cols, sems, i):
        zs, zr, ss, sr, ls = sems
        A = n // 4
        rep, a, b, c = position(n)
        h = rep % 2
        rh = own.shape[1]
        k0 = rh * 3 // 4 if (rh * 3 // 4) % 8 == 0 else rh // 2
        lo, hi, every = pl.ds(0, k0), pl.ds(k0, rh - k0), slice(None)
        at = lambda *ix: full.at[(*ix, cols)]
        rank = lambda a, b, c: (a * 2 + b) * 2 + c
        ydev, xdev, cdev = (rep, rank(a, 1 - b, c)), (rep + 1 - 2 * h, rank(a, b, c)), (rep, rank(a, b, 1 - c))
        same = lambda ref, k, to: remote(ref, ref, ss.at[i, k], sr.at[i, k], to)
        mine = own.at[h, :, cols]
        self.local = lambda: [pltpu.make_async_copy(mine, at(a, b, c, h, every), ls.at[i])]
        self.along = lambda: [remote(mine, at(a, b, c, h, every), zs.at[i, d - 1], zr.at[i, d - 1], (rep, rank((a + d) % A, b, c))) for d in range(1, A)]
        self.second = lambda: [same(at(every, b, c, h, lo), 0, ydev), same(at(every, b, c, h, hi), 1, xdev)]
        self.third = lambda: [same(at(every, every, c, h, lo), 2, xdev), same(at(every, b, c, every, hi), 3, ydev)]
        self.last = lambda: [same(at(every, every, c, every, every), 4, cdev)]

    def begin(self):
        for q in self.local() + self.along():
            q.start()

    def turn(self, arrived, started):
        for q in arrived():
            q.wait_recv()
        for q in started():
            q.start()

    def step(self, k):
        if k == 0:
            for q in self.local():
                q.wait()
            self.turn(self.along, self.second)
        elif k == 1:
            self.turn(self.second, self.third)
        elif k == 2:
            self.turn(self.third, self.last)
        else:
            for q in self.last():
                q.wait_recv()

    def end(self):
        for q in self.along() + self.second() + self.third() + self.last():
            q.wait_send()


def forward_kernel(n, group, *refs):
    it = iter(refs)
    take = lambda count: [next(it) for _ in range(count)]
    index, x, hidden, wk, wv, wq, so, sg, su, sd, k_gain, q_gain, cos_r, sin_r, cos, sin, past, inside, valid, gain2, staged = take(21)
    wo, wg, wu, wd, moved, attended, q_out, lse_out, rs_out, k_pre, k_out, v, ks, vs, resid, h2, act, gate, up, mixed, stats = take(21)
    ordered, o_buf, g_buf, u_buf, d_buf, g_st, u_st = take(7)
    zs, zr, ss, sr, ls, lds, fs, fr, gs, gr, kls, ps, pr, pls, gos = take(15)
    rows = ks.shape[2]
    T = x.shape[0]
    half = group // 2
    rep, a, b, c = position(n)
    me = (a * 2 + b) * 2 + c
    first, slot = (me // group) * half, (me // 2) % half
    h = rep % 2
    meet([(rep, (me + d) % n) for d in range(1, n)] + [(rep + 1 - 2 * h, me)])

    OB, GB = o_buf.shape[-1], g_buf.shape[-1]
    n_out, n_mlp = wo.shape[-1] // OB, wg.shape[-1] // GB
    blocks = [(so, wo, pl.ds(q * OB, OB), o_buf.at[q]) for q in range(n_out)]
    for q in range(n_mlp):
        blocks += [(sg, wg, pl.ds(q * GB, GB), g_buf.at[q % 2]), (su, wu, pl.ds(q * GB, GB), u_buf.at[q % 2])]
    blocks += [(sd, wd, pl.ds(q * OB, OB), d_buf.at[q]) for q in range(n_out)]
    m = len(blocks)
    rings = [Ring(n, own, full, cols, (zs, zr, ss, sr, ls), i) for i, (own, full, cols, _) in enumerate(blocks)]

    def load(i):
        _, full, cols, buf = blocks[i]
        return pltpu.make_async_copy(full.at[:, :, :, :, :, cols], buf, lds.at[i])

    def tick(t):
        for k in range(4):
            if 0 <= t - k < m:
                rings[t - k].step(k)
                if k == 3:
                    load(t - k).start()

    S = ordered.shape[1]

    def put(j, _):
        ordered[j // S, j % S] = staged[index[j]]
        return 0

    lax.fori_loop(0, n * S, put, 0)
    pieces = [remote(ordered.at[(me + d) % n], moved.at[:, me], ps.at[d - 1], pr.at[d - 1], (rep, (me + d) % n)) for d in range(1, n)]
    own_piece = pltpu.make_async_copy(ordered.at[me], moved.at[:, me], pls.at[0])
    for r in rings[:2]:
        r.begin()
    own_piece.start()
    for q in pieces:
        q.start()
    for r in rings[2:]:
        r.begin()

    lane = lambda j, w: pl.ds(pl.multiple_of(j * w, w), w)
    heads = QUERY_HEADS // KEY_VALUE_HEADS
    pair = heads * HEAD_SIZE

    def kv_tile(j, _):
        kp = mm(hidden[...], wk[:, lane(j, 256)], 1, 0)
        k_pre[:, lane(j, 256)] = kp
        for g in range(2):
            y = kp[:, g * HEAD_SIZE:(g + 1) * HEAD_SIZE]
            y = y * lax.rsqrt(jnp.mean(y * y, axis=-1, keepdims=True) + norm_epsilon) * k_gain[...]
            k_out[:, lane(2 * j + g, HEAD_SIZE)] = (y * cos_r[...] + pltpu.roll(y, HEAD_SIZE // 2, 1) * sin_r[...]).astype(bf16)
        v[:, lane(j, 256)] = mm(hidden[...], wv[:, lane(j, 256)], 1, 0).astype(bf16)
        return 0

    lax.fori_loop(0, wk.shape[1] // 256, kv_tile, 0)
    parts = [(k_out, ks), (v, vs)]
    at = lambda s, c: (rep, (first + s) * 2 + c)
    mine = lambda i: parts[i][0].at[pl.ds(0, rows)]
    klocal = [pltpu.make_async_copy(mine(i), parts[i][1].at[slot, c], kls.at[i]) for i in range(2)]
    across = [remote(mine(i), parts[i][1].at[slot, c], fs.at[i, d - 1], fr.at[i, d - 1], at((slot + d) % half, c)) for i in range(2) for d in range(1, half)]
    sibling = [remote(mine(i), parts[i][1].at[slot, c], gs.at[i, 0], gr.at[i, 0], at(slot, 1 - c)) for i in range(2)]
    onward = []
    for i in range(2):
        for d in range(1, half):
            there = parts[i][1].at[(slot + half - d) % half, c]
            onward.append(remote(there, there, gs.at[i, d], gr.at[i, d], at(slot, 1 - c)))
    for q in across + sibling + klocal:
        q.start()
    tick(0)

    def q_tile(j, _):
        qp = mm(hidden[...], wq[:, lane(j, pair)], 1, 0)
        for g in range(heads):
            y = qp[:, g * HEAD_SIZE:(g + 1) * HEAD_SIZE].T
            rs = lax.rsqrt(jnp.mean(y * y, axis=0, keepdims=True) + norm_epsilon)
            rs_out[j, g:g + 1, :] = rs
            y = y * rs * q_gain[:, 0:1]
            lo, hi = y[:HEAD_SIZE // 2], y[HEAD_SIZE // 2:]
            y = jnp.concatenate([lo * cos[...] - hi * sin[...], hi * cos[...] + lo * sin[...]], axis=0)
            q_out[lane(j * heads + g, HEAD_SIZE), :] = y.astype(bf16)
        for when, t in ((3, 1), (7, 2)):
            pl.when(j == when)(partial(tick, t))
        return 0

    lax.fori_loop(0, KEY_VALUE_HEADS, q_tile, 0)
    for q in across:
        q.wait_recv()
    for q in onward:
        q.start()
    tick(3)
    for q in klocal:
        q.wait()
    for q in sibling + onward:
        q.wait_recv()

    scale = HEAD_SIZE ** -0.5 * LOG2E

    def attend_head(j, _):
        kl = lane(j, HEAD_SIZE)
        kb = ks[:, :, :, kl].reshape(PROMPT_LENGTH, HEAD_SIZE)
        vb = vs[:, :, :, kl].reshape(PROMPT_LENGTH, HEAD_SIZE)
        for g in range(heads):
            ql = lane(j * heads + g, HEAD_SIZE)
            q = q_out[ql, :]
            p = jnp.exp2(mm(kb, q[:, :rows], 1, 0) * scale + past[...])
            total = jnp.sum(p, axis=0, keepdims=True)
            o = mm(vb, p.astype(bf16), 0, 0) / total
            attended[:rows, ql] = o.T.astype(bf16)
            lse_out[j, g:g + 1, :rows] = jnp.log2(total)
            p = jnp.exp2(mm(kb, q[:, rows:], 1, 0) * scale)
            r = jnp.exp2(mm(k_out[rows:, kl], q[:, rows:], 1, 0) * scale + inside[...])
            total = jnp.sum(p, axis=0, keepdims=True) + jnp.sum(r, axis=0, keepdims=True)
            o = (mm(vb, p.astype(bf16), 0, 0) + mm(v[rows:, kl], r.astype(bf16), 0, 0)) / total
            attended[rows:, ql] = o.T.astype(bf16)
            lse_out[j, g:g + 1, rows:] = jnp.log2(total)
        for when, t in ((2, 4), (5, 5)):
            pl.when(j == when)(partial(tick, t))
        return 0

    lax.fori_loop(0, KEY_VALUE_HEADS, attend_head, 0)

    stats[...] = jnp.zeros_like(stats)
    for q in range(n_out):
        load(q).wait()

        def out_tile(j, _):
            cols = lane(q * (OB // 256) + j, 256)
            w = o_buf[q, :, :, :, :, :, lane(j, 256)].reshape(-1, 256)
            y = x[:, cols].astype(f32) + mm(attended[...], w, 1, 0)
            resid[:, cols] = y
            stats[1:2, :] += jnp.sum(valid[...] * y * y, axis=0, keepdims=True)
            return 0

        lax.fori_loop(0, OB // 256, out_tile, 0)
    RB = 32

    def norm_rows(j, _):
        y = resid[pl.ds(pl.multiple_of(j * RB, RB), RB), :]
        y = y * lax.rsqrt(jnp.mean(y * y, axis=-1, keepdims=True) + norm_epsilon) * gain2[...]
        h2[pl.ds(pl.multiple_of(j * RB, RB), RB), :] = y.astype(bf16)
        return 0

    lax.fori_loop(0, T // RB, norm_rows, 0)
    done = 6
    saved = lambda q: [pltpu.make_async_copy(g_st.at[q % 2], gate.at[:, pl.ds(q * GB, GB)], gos.at[q % 2, 0]),
                       pltpu.make_async_copy(u_st.at[q % 2], up.at[:, pl.ds(q * GB, GB)], gos.at[q % 2, 1])]
    for q in range(n_mlp):
        need = n_out + 2 * q + 1 + 3
        while done <= need:
            tick(done)
            done += 1
        load(n_out + 2 * q).wait()
        load(n_out + 2 * q + 1).wait()
        if q >= 2:
            for s in saved(q - 2):
                s.wait()

        def mlp_tile(j, _):
            g = mm(h2[...], g_buf[q % 2, :, :, :, :, :, lane(j, 256)].reshape(-1, 256), 1, 0)
            u = mm(h2[...], u_buf[q % 2, :, :, :, :, :, lane(j, 256)].reshape(-1, 256), 1, 0)
            g_st[q % 2, :, lane(j, 256)] = g.astype(bf16)
            u_st[q % 2, :, lane(j, 256)] = u.astype(bf16)
            act[:, lane(q * (GB // 256) + j, 256)] = (g / (1.0 + jnp.exp(-g)) * u).astype(bf16)
            return 0

        lax.fori_loop(0, GB // 256, mlp_tile, 0)
        for s in saved(q):
            s.start()
    for q in range(n_out):
        need = n_out + 2 * n_mlp + q + 3
        while done <= need:
            tick(done)
            done += 1
        load(n_out + 2 * n_mlp + q).wait()

        def down_tile(j, _):
            cols = lane(q * (OB // 256) + j, 256)
            w = d_buf[q, :, :, :, :, :, lane(j, 256)].reshape(-1, 256)
            y = resid[:, cols] + mm(act[...], w, 1, 0)
            mixed[:, cols] = y.astype(bf16)
            stats[0:1, :] += jnp.sum(valid[...] * y * y, axis=0, keepdims=True)
            return 0

        lax.fori_loop(0, OB // 256, down_tile, 0)
    for q in range(max(0, n_mlp - 2), n_mlp):
        for s in saved(q):
            s.wait()
    own_piece.wait()
    for q in pieces:
        q.wait()
    for q in across + sibling + onward:
        q.wait_send()
    for r in rings:
        r.end()


def forward(index, x, hidden, wk, wv, wq, shards, k_gain, q_gain, cos_r, sin_r, cos, sin, past, inside, valid, gain2, staged, rows, n, cid):
    group = PROMPT_LENGTH // rows
    half, A, T, W = group // 2, n // 4, x.shape[0], x.shape[1]
    S = staged.shape[1]
    halves = [s.reshape(2, s.shape[0] // 2, s.shape[1]) for s in shards]
    fulls = [jax.ShapeDtypeStruct((A, 2, 2) + s.shape, bf16) for s in halves]
    flat = staged.reshape((-1,) + staged.shape[2:])
    QW, KW, FW = wq.shape[1], wk.shape[1], shards[1].shape[1]
    sd_ = jax.ShapeDtypeStruct
    small = sd_((KEY_VALUE_HEADS, 2, T), f32)
    keys = sd_((half, 2, rows, KW), bf16)
    out_shape = fulls + [sd_((S, n) + staged.shape[2:], bf16), sd_((T, QW), bf16), sd_((QW, T), bf16), small, small, sd_((T, KW), f32),
        sd_((T, KW), bf16), sd_((T, KW), bf16), keys, keys, sd_((T, W), f32), sd_((T, W), bf16), sd_((T, FW), bf16),
        sd_((T, FW), bf16), sd_((T, FW), bf16), sd_((T, W), bf16), sd_((8, 256), f32)]
    vm, hbm, sm = pl.BlockSpec(memory_space=pltpu.VMEM), pl.BlockSpec(memory_space=pl.ANY), pl.BlockSpec(memory_space=pltpu.SMEM)
    D, V = pltpu.SemaphoreType.DMA, pltpu.VMEM
    OB, GB = 512, 768
    n_out, n_mlp = W // OB, FW // GB
    m = 2 * n_out + 2 * n_mlp
    buf = lambda i, k, w: V((k, A, 2, 2) + halves[i].shape[:2] + (w,), bf16)
    res = pl.pallas_call(
        partial(forward_kernel, n, group),
        out_shape=out_shape,
        in_specs=[sm] + [vm] * 20,
        out_specs=[hbm] * 5 + [vm] * 12 + [hbm] * 2 + [vm] * 2,
        scratch_shapes=[V(staged.shape, bf16), buf(0, n_out, OB), buf(1, 2, GB), buf(2, 2, GB), buf(3, n_out, OB), V((2, T, GB), bf16), V((2, T, GB), bf16)]
        + [D((m, A - 1))] * 2 + [D((m, 5))] * 2 + [D((m,))] * 2 + [D((2, max(half - 1, 1)))] * 2 + [D((2, half))] * 2 + [D((2,))]
        + [D((n - 1,))] * 2 + [D((1,))] + [D((2, 2))],
        compiler_params=pltpu.CompilerParams(collective_id=cid, has_side_effects=True, vmem_limit_bytes=63 << 20),
        name="forward",
    )(index, x, hidden, wk, wv, wq, *halves, k_gain, q_gain, cos_r, sin_r, cos, sin, past, inside, valid, gain2, flat)
    res = list(res)
    for i, s in enumerate(shards):
        res[i] = res[i].reshape(-1, s.shape[1])
    res[12], res[13] = res[12].reshape(PROMPT_LENGTH, KW), res[13].reshape(PROMPT_LENGTH, KW)
    return res


MLP_TICKS = (1, 2, 2, 2, 2, 2)
OUT_TICKS = 1
HEAD_TICKS = (1, 1, 1)
BACK_TICKS = (1, 1, 1, 1)


class Fold:
    def __init__(self, n, R, where, g, bufs, out, cols, sems, i):
        self.bufs, self.k, self.landing = bufs
        self.waited = set()
        self.g, self.out, self.cols, self.i, self.sems = g, out, cols, i, sems
        self.A, self.bits = n // 4, R.bit_length() - 1
        self.rep, self.a, self.b, self.c, self.h = where
        self.rh = self.bufs[0].shape[-2]
        self.k0 = fold_split(self.rh)

    b1 = property(lambda self: self.bufs[0].at[self.landing])
    b2y, b2x, b3, b4, s4, b5 = [property(lambda self, j=j: self.bufs[j].at[self.k]) for j in range(1, 7)]

    def device(self, da=0, db=0, dc=0, bit=None):
        rep, a, b, c = self.rep, self.a, self.b, self.c
        if bit is not None:
            rep = rep + (1 << bit) - 2 * (1 << bit) * ((rep // (1 << bit)) % 2)
        return (rep, (((a + da) % self.A) * 2 + (1 - b if db else b)) * 2 + (1 - c if dc else c))

    @property
    def ydev(self):
        return self.device(db=1)

    @property
    def xdev(self):
        return self.device(bit=0)

    @property
    def cdev(self):
        return self.device(dc=1)

    def zdev(self, d):
        return self.device(da=d)

    def flip(self, bit):
        return self.device(bit=bit)

    def hop(self, k):
        i, a, b, c, h, k0, rh = self.i, self.a, self.b, self.c, self.h, self.k0, self.rh
        s1s, s1r, s2s, s2r, s3s, s3r, s4s, s4r, s5s, s5r, _ = self.sems
        lo, hi = pl.ds(0, k0), pl.ds(k0, rh - k0)
        if k == 1:
            return [remote(self.g.at[:, :, 1 - c], self.b1, s1s.at[i], s1r.at[i], self.cdev)]
        if k == 2:
            q = [remote(self.b1.at[:, 1 - b, :, lo], self.b2y, s2s.at[i, 0], s2r.at[i, 0], self.ydev)]
            if k0 < rh:
                q.append(remote(self.b1.at[:, :, 1 - h, hi], self.b2x, s2s.at[i, 1], s2r.at[i, 1], self.xdev))
            return q
        if k == 3:
            q = [remote(self.b2y.at[:, 1 - h], self.b3.at[:, lo], s3s.at[i, 0], s3r.at[i, 0], self.xdev)]
            if k0 < rh:
                q.append(remote(self.b2x.at[:, 1 - b], self.b3.at[:, hi], s3s.at[i, 1], s3r.at[i, 1], self.ydev))
            return q
        if k == 4:
            return [remote(self.b3.at[(a + d) % self.A], self.b4.at[d - 1], s4s.at[i, d - 1], s4r.at[i, d - 1], self.zdev(d)) for d in range(1, self.A)]
        last = self.bits - 1
        return [remote(self.s4.at[last], self.b5.at[last], s5s.at[i, last], s5r.at[i, last], self.xdev)]

    def put(self, k):
        last = self.bits - 1
        half = self.h if k == 0 else 1 - self.h
        return pltpu.make_async_copy((self.s4 if k == 0 else self.b5).at[last], self.out.at[half, :, self.cols], self.sems[-1].at[self.i, k])

    def begin(self):
        for q in self.hop(1):
            q.start()

    def arrive(self, k):
        for q in self.hop(k):
            q.wait_recv()

    def go(self, k):
        for q in self.hop(k):
            q.start()

    def step(self, k):
        a, b, c, h, k0, rh = self.a, self.b, self.c, self.h, self.k0, self.rh
        self.arrive(k)
        lo, hi = pl.ds(0, k0), pl.ds(k0, rh - k0)
        if k == 1:
            for q in self.hop(1):
                q.wait_send()
            view = lambda ref: lambda j: ref.at[j // 4, (j // 2) % 2, j % 2]
            add_rows(self.A * 4, view(self.b1), view(self.b1), [lambda j: self.g.at[j // 4, (j // 2) % 2, c, j % 2]])
        elif k == 2:
            view = lambda ref: lambda j: ref.at[j // 2, j % 2]
            add_rows(self.A * 2, view(self.b2y), view(self.b2y), [lambda j: self.b1.at[j // 2, b, j % 2, lo]])
            if k0 < rh:
                add_rows(self.A * 2, view(self.b2x), view(self.b2x), [lambda j: self.b1.at[j // 2, j % 2, h, hi]])
        elif k == 3:
            view = lambda part: lambda j: self.b3.at[j, part]
            add_rows(self.A, view(lo), view(lo), [lambda j: self.b2y.at[j, h]])
            if k0 < rh:
                add_rows(self.A, view(hi), view(hi), [lambda j: self.b2x.at[j, b]])
        elif k == 4:
            add_rows(1, lambda j: self.s4.at[0], lambda j: self.b3.at[a], [lambda j, d=d: self.b4.at[d] for d in range(self.A - 1)])
            s5s, s5r = self.sems[8:10]
            for r in range(self.bits - 1):
                q = remote(self.s4.at[r], self.b5.at[r], s5s.at[self.i, r], s5r.at[self.i, r], self.flip(r + 1))
                q.start()
                q.wait()
                add_rows(1, lambda j, r=r: self.s4.at[r + 1], lambda j, r=r: self.s4.at[r], [lambda j, r=r: self.b5.at[r]])
            self.put(0).start()
        else:
            self.put(1).start()
            return
        self.go(k + 1)

    def sent(self, k):
        if k not in self.waited:
            self.waited.add(k)
            for q in self.hop(k):
                q.wait_send()

    def end(self):
        for k in range(2, 6):
            self.sent(k)
        self.put(0).wait()
        self.put(1).wait()


def fold_split(rh):
    if (rh // 2) % 16 == 0:
        return rh // 2
    return rh // 32 * 16 if rh >= 32 else rh


def backward_kernel(n, R, group, UD, UF, UO, *refs):
    it = iter(refs)
    take = lambda count: [next(it) for _ in range(count)]
    index, mixed, dm, h2, act, gate, up, resid, wd, wg, wu, wo, attended, q_rot, lse, rs_q, ks, vs, k_rot, v, k_pre, wq, wk, wv, hidden, x = take(26)
    k_gain, q_gain, cos_r, sin_r, cos, sin, past, inside, valid, gain1, gain2, sums = take(12)
    outs = take(7)
    vec, d_prompt, mixed_out, grad_out = take(4)
    classes = [take(7) for _ in range(3)]
    r1, r2, mixed_in, turned, grad_src, grad_in, vb, vz, dres = take(9)
    fold_sems = take(11)
    lds, hs, gs, gr, fs, fr, a2s, a2r, a2l, vs_, vr_, free = take(12)
    A, T, W = n // 4, dm.shape[0], dm.shape[1]
    half, rows, KW = group // 2, r1.shape[2], k_rot.shape[1]
    FW, QW = act.shape[1], attended.shape[1]
    bits = R.bit_length() - 1
    rep, a, b, c = position(n)
    h = rep % 2
    rank = lambda a, b, c: (a * 2 + b) * 2 + c
    me = rank(a, b, c)
    first, slot = (me // group) * half, (me // 2) % half
    flip = lambda bit: (rep + (1 << bit) - 2 * (1 << bit) * ((rep // (1 << bit)) % 2), me)
    meet([(rep, (me + d) % n) for d in range(1, n)] + [flip(k) for k in range(bits)])

    lane = lambda j, w: pl.ds(pl.multiple_of(j * w, w), w)
    heads = QUERY_HEADS // KEY_VALUE_HEADS
    loads = iter(range(lds.shape[0]))

    def fetch(src, dst):
        q = pltpu.make_async_copy(src, dst, lds.at[next(loads)])
        q.start()
        return q

    S = turned.shape[1]

    def spread_copies(src, dst, k):
        own = pltpu.make_async_copy(src.at[:, me], dst.at[me], a2l.at[k])
        return own, [remote(src.at[:, (me + d) % n], dst.at[me], a2s.at[k, d - 1], a2r.at[k, d - 1], (rep, (me + d) % n)) for d in range(1, n)]

    def collect_copies(src, dst, k):
        own = pltpu.make_async_copy(src.at[me], dst.at[:, me], a2l.at[k])
        return own, [remote(src.at[(me + d) % n], dst.at[:, me], a2s.at[k, d - 1], a2r.at[k, d - 1], (rep, (me + d) % n)) for d in range(1, n)]

    def begin_all(pair):
        pair[0].start()
        for q in pair[1]:
            q.start()

    def wait_all(pair):
        pair[0].wait()
        for q in pair[1]:
            q.wait()

    def reorder(src, dst):
        def put(j, _):
            s = index[j]
            dst[j // S, j % S] = src[s // S, s % S]
            return 0

        lax.fori_loop(0, n * S, put, 0)

    mixed_spread = spread_copies(mixed, mixed_in, 0)

    units = []

    def unit(cls, k, g, out, cols, landing=None):
        units.append(Fold(n, R, (rep, a, b, c, h), g, (classes[cls], k, k if landing is None else landing), outs[out], cols, fold_sems, len(units)))
        return units[-1]

    state = {"e1": 0, "tick": 0}

    def e1():
        units[state["e1"]].step(1)
        state["e1"] += 1

    def tick(count=1):
        for _ in range(count):
            t = state["tick"]
            for k in range(4):
                if 0 <= t - k < len(units) and (k or t < state["e1"]):
                    units[t - k].step(k + 2)
            state["tick"] += 1

    n_down, n_ff, n_out = W // UD, FW // UF, W // UO
    V = pltpu.VMEM
    rh = lambda k: classes[k][0].shape[-2]
    AT, QT = FW // A, QW // A

    def down(act_c, act_t, g_down, dm_v):
        got = fetch(dm, dm_v)
        pieces = [fetch(act.at[:, pl.ds(0, AT)], act_c.at[0])]
        begin_all(mixed_spread)
        got.wait()
        for i in range(A):
            if i + 1 < A:
                pieces.append(fetch(act.at[:, pl.ds((i + 1) * AT, AT)], act_c.at[(i + 1) % 2]))
            pieces[i].wait()
            act_t[...] = act_c[i % 2].T

            def down_tile(j, _):
                y = mm(act_t[...], dm_v[:, lane(j, UD)], 1, 0).astype(bf16)
                g_down[j, i] = y.reshape(g_down.shape[2:])
                return 0

            lax.fori_loop(0, n_down, down_tile, 0)
        for u in range(n_down):
            unit(0, u, g_down.at[u], 0, pl.ds(u * UD, UD)).begin()
        for u in range(n_down):
            e1()

    pl.run_scoped(down, V((2, T, AT), bf16), V((AT, T), bf16), V((n_down, A, 2, 2, 2, rh(0), UD), bf16), V((T, W), bf16))
    tick()
    RB = 32
    block = lambda j: pl.ds(pl.multiple_of(j * RB, RB), RB)

    def norm_back(value, gain, grad):
        r = lax.rsqrt(jnp.mean(value * value, axis=-1, keepdims=True) + norm_epsilon)
        u = value * r
        t = grad * gain
        return r * (t - u * jnp.mean(t * u, axis=-1, keepdims=True)), jnp.sum(grad * u, axis=0, keepdims=True)

    def persistent(dq, dkr, dvl):
        def after_mlp(drl):
            pl.run_scoped(partial(mlp, drl), V((4, A, 2, 2, 2, rh(1), UF), bf16), V((2, UF, W), bf16), V((2, W, UF), bf16), V((2, W, UF), bf16), V((2, T, UF), bf16),
                          V((2, T, UF), bf16), V((T, UF), bf16), V((T, UF), bf16), V((W, T), bf16), V((T, W), bf16), V((T, W), bf16), V((T, W), f32))
            pl.run_scoped(partial(out_grad, drl), V((2, T, QT), bf16), V((QT, T), bf16), V((n_out, A, 2, 2, 2, rh(2), UO), bf16))
            wait_all(mixed_spread)
            reorder(mixed_in, turned)
            mixed_collect = collect_copies(turned, mixed_out, 1)
            begin_all(mixed_collect)
            pl.run_scoped(partial(attention, drl, dq, dkr, dvl), V((half, 2, rows, KW), bf16), V((half, 2, rows, KW), bf16), V((2, PROMPT_LENGTH, HEAD_SIZE), bf16),
                          V((2, PROMPT_LENGTH, HEAD_SIZE), bf16), V((2, heads * HEAD_SIZE, T), bf16), V((2, T, heads * HEAD_SIZE), bf16), V((2, heads * HEAD_SIZE, W), bf16),
                          V((T, KW), bf16), V((T, KW), bf16))
            wait_all(mixed_collect)

        pl.run_scoped(after_mlp, V((T, W), bf16))
        pl.run_scoped(partial(weights_back, dq, dkr, dvl), V((2, 256, QW), bf16), V((2, 256, KW), bf16), V((2, 256, KW), bf16), V((T, W), bf16), V((W, T), bf16),
                      V((T, KW), f32), V((T, KW), bf16), V((4, A, 2, 2, 2, rh(1), UF), bf16), V((T, W), f32))

    def mlp(drl, g_ff, wd_c, wg_c, wu_c, gate_c, up_c, dg_c, du_c, h2_t, h2_v, dm_v, dhid):
        got = [fetch(h2, h2_v), fetch(dm, dm_v)]

        def fetch_ff(q):
            cols, s = pl.ds(q * UF, UF), q % 2
            return [fetch(wd.at[cols], wd_c.at[s]), fetch(gate.at[:, cols], gate_c.at[s]), fetch(up.at[:, cols], up_c.at[s]),
                    fetch(wg.at[:, cols], wg_c.at[s]), fetch(wu.at[:, cols], wu_c.at[s])]

        ff = [fetch_ff(0)]
        got_resid = fetch(resid, dres)
        for f in got:
            f.wait()
        h2_t[...] = h2_v[...].T
        for q in range(n_ff):
            s = q % 2
            if q + 1 < n_ff:
                ff.append(fetch_ff(q + 1))
            for f in ff[q]:
                f.wait()

            def act_tile(j, _):
                cols = lane(j, 256)
                g, u = gate_c[s, :, cols].astype(f32), up_c[s, :, cols].astype(f32)
                da = mm(dm_v[...], wd_c[s, lane(j, 256), :], 1, 1)
                sg = 1.0 / (1.0 + jnp.exp(-g))
                du_c[:, cols] = (da * (g * sg)).astype(bf16)
                dg_c[:, cols] = (da * u * (sg * (1.0 + g * (1.0 - sg)))).astype(bf16)
                return 0

            lax.fori_loop(0, UF // 256, act_tile, 0)
            for k, d in enumerate((dg_c, du_c)):
                while state["e1"] < len(units) - 1:
                    e1()

                def ff_tile(j, _):
                    y = mm(h2_t[...], d[:, lane(j, 256)], 1, 0).astype(bf16)
                    g_ff[(2 * q + k) % 4, :, :, :, :, :, lane(j, 256)] = y.reshape(g_ff.shape[1:6] + (256,))
                    return 0

                lax.fori_loop(0, UF // 256, ff_tile, 0)
                unit(1, 2 * q + k, g_ff.at[(2 * q + k) % 4], 1 + k, pl.ds(q * UF, UF)).begin()

            def hid_tile(j, _):
                cols = lane(j, 256)
                y = mm(dg_c[...], wg_c[s, cols, :], 1, 1) + mm(du_c[...], wu_c[s, cols, :], 1, 1)
                dhid[:, cols] = y if q == 0 else dhid[:, cols] + y
                return 0

            lax.fori_loop(0, W // 256, hid_tile, 0)
            for _ in range(MLP_TICKS[q % len(MLP_TICKS)]):
                tick()
        while state["e1"] < len(units):
            e1()
        got_resid.wait()

        def second_norm(j, total):
            d, gg = norm_back(dres[block(j), :], gain2[...], dhid[block(j), :])
            d = dm_v[block(j), :].astype(f32) + d
            dres[block(j), :] = d
            drl[block(j), :] = d.astype(bf16)
            return total + gg

        g2 = lax.fori_loop(0, T // RB, second_norm, jnp.zeros((1, W), f32))
        for k in range(W // 128):
            vec[W // 128 + k:W // 128 + k + 1, :] = g2[:, k * 128:(k + 1) * 128]

    def out_grad(drl, att_c, att_t, g_out):
        pieces = [fetch(attended.at[:, pl.ds(0, QT)], att_c.at[0])]
        for i in range(A):
            if i + 1 < A:
                pieces.append(fetch(attended.at[:, pl.ds((i + 1) * QT, QT)], att_c.at[(i + 1) % 2]))
            pieces[i].wait()
            att_t[...] = att_c[i % 2].T

            def out_tile(j, _):
                y = mm(att_t[...], drl[:, lane(j, UO)], 1, 0).astype(bf16)
                g_out[j, i] = y.reshape(g_out.shape[2:])
                return 0

            lax.fori_loop(0, n_out, out_tile, 0)
        for u in range(n_out):
            unit(2, u, g_out.at[u], 3, pl.ds(u * UO, UO)).begin()
        tick(OUT_TICKS)
        while state["e1"] < len(units):
            e1()

    def attention(drl, dq, dkr, dvl, dk, dv, ks_c, vs_c, q_c, att_c, wo_c, kr_v, v_v):
        others = [fetch(k_rot, kr_v), fetch(v, v_v)]
        pair = lambda j: lane(j, heads * HEAD_SIZE)

        def head_copies(j):
            s = j % 2
            moves = [(ks.at[:, lane(j, HEAD_SIZE)], ks_c), (vs.at[:, lane(j, HEAD_SIZE)], vs_c), (q_rot.at[pair(j), :], q_c),
                     (attended.at[:, pair(j)], att_c), (wo.at[pair(j), :], wo_c)]
            return [pltpu.make_async_copy(src, dst.at[s], hs.at[s, k]) for k, (src, dst) in enumerate(moves)]

        for q in head_copies(jnp.int32(0)):
            q.start()
        for q in others:
            q.wait()
        scale = HEAD_SIZE ** -0.5
        plus = lambda p, q: q if p is None else p + q

        def head(j, gain_grad):
            @pl.when(j + 1 < KEY_VALUE_HEADS)
            def _():
                for q in head_copies(j + 1):
                    q.start()

            for q in head_copies(j):
                q.wait()
            at = j % 2
            kl = lane(j, HEAD_SIZE)
            kb, vb_ = ks_c[at], vs_c[at]
            dkp = dvp = dks = dvs = None
            do_pair = mm(drl[...], wo_c[at], 1, 1)
            out_pair = att_c[at].astype(f32)
            for g in range(heads):
                sl = slice(g * HEAD_SIZE, (g + 1) * HEAD_SIZE)
                q = q_c[at, sl, :]
                do = do_pair[:, sl].astype(bf16)
                delta = jnp.sum((do.astype(f32) * out_pair[:, sl]).T, axis=0, keepdims=True)
                log_total = lse[j, g:g + 1, :]
                parts = []
                for suffix in range(2):
                    part = slice(rows, None) if suffix else slice(0, rows)
                    qp, dop, lp, dp = q[:, part], do[part], log_total[:, part], delta[:, part]
                    pieces = [(kb, vb_, None if suffix else past[...])]
                    if suffix:
                        pieces.append((kr_v[rows:, kl], v_v[rows:, kl], inside[...]))
                    total = None
                    for i, (kk, vv, bias) in enumerate(pieces):
                        s = mm(kk, qp, 1, 0) * (scale * LOG2E) - lp
                        p = jnp.exp2(s if bias is None else s + bias)
                        ds = (p * (mm(vv, dop, 1, 1) - dp)).astype(bf16)
                        gv, gk = mm(p.astype(bf16), dop, 1, 0), mm(ds, qp, 1, 1)
                        total = plus(total, mm(kk, ds, 0, 0))
                        if i:
                            dks, dvs = plus(dks, gk), plus(dvs, gv)
                        else:
                            dkp, dvp = plus(dkp, gk), plus(dvp, gv)
                    parts.append(total)
                d = jnp.concatenate(parts, axis=1) * scale
                m = HEAD_SIZE // 2
                cs, sn = cos[...], sin[...]
                dy = jnp.concatenate([d[:m] * cs + d[m:] * sn, d[m:] * cs - d[:m] * sn], axis=0)
                qf = q.astype(f32)
                u = jnp.concatenate([qf[:m] * cs + qf[m:] * sn, qf[m:] * cs - qf[:m] * sn], axis=0) / q_gain[:, 0:1]
                gg = dy * u
                for t in range(T // 128):
                    gain_grad = gain_grad + gg[:, t * 128:(t + 1) * 128]
                dy = dy * q_gain[:, 0:1]
                dx = rs_q[j, g:g + 1, :] * (dy - u * jnp.mean(dy * u, axis=0, keepdims=True))
                dq[:, lane(j * heads + g, HEAD_SIZE)] = dx.T.astype(bf16)
            dk[:, :, :, kl] = (dkp * scale).astype(bf16).reshape(half, 2, rows, HEAD_SIZE)
            dv[:, :, :, kl] = dvp.astype(bf16).reshape(half, 2, rows, HEAD_SIZE)
            dkr[rows:, kl] = dks * scale
            dvl[rows:, kl] = dvs.astype(bf16)
            return gain_grad

        gain_grad = jnp.zeros((HEAD_SIZE, 128), f32)
        for part in range(4):
            gain_grad = lax.fori_loop(2 * part, 2 * part + 2, head, gain_grad)
            if part < 3:
                tick(HEAD_TICKS[part])
        vec[2 * W // 128:2 * W // 128 + 1, :] = jnp.sum(gain_grad.T, axis=0, keepdims=True)
        grads = [dk, dv]
        home = lambda s, c: (rep, (first + s) * 2 + c)

        def to_sibling(i, d):
            return remote(grads[i].at[(slot + d) % half, 1 - c], r1.at[i, d], gs.at[i, d], gr.at[i, d], home(slot, 1 - c))

        order = list(range(1, half)) + [0]
        for d in order:
            for i in range(2):
                to_sibling(i, d).start()
        for d in order:
            for i in range(2):
                to_sibling(i, d).wait_recv()

                def one(j, _):
                    r1[i, d, block(j)] = (grads[i][(slot + d) % half, c, block(j)].astype(f32) + r1[i, d, block(j)].astype(f32)).astype(bf16)
                    return 0

                lax.fori_loop(0, rows // RB, one, 0)
                if d:
                    across(i, d).start()
        for d in order:
            for i in range(2):
                to_sibling(i, d).wait_send()

    def across(i, d):
        return remote(r1.at[i, d], r2.at[i, d - 1], fs.at[i, d - 1], fr.at[i, d - 1], (rep, (first + (slot + d) % half) * 2 + c))

    def weights_back(dq, dkr, dvl, wq_c, wk_c, wv_c, hid_v, hid_t, kp_v, dkl, g_qkv, dhid):
        got = [fetch(hidden, hid_v), fetch(k_pre, kp_v)]
        tiles = W // 256
        fetch_q = lambda j: fetch(wq.at[pl.ds(j * 256, 256)], wq_c.at[j % 2])
        fetch_kv = lambda j: [fetch(wk.at[pl.ds(j * 256, 256)], wk_c.at[j % 2]), fetch(wv.at[pl.ds(j * 256, 256)], wv_c.at[j % 2])]
        q_tiles, kv_tiles = [fetch_q(0), fetch_q(1)], [fetch_kv(0), fetch_kv(1)]
        got[0].wait()
        hid_t[...] = hid_v[...].T
        got_x = fetch(x, hid_v)
        count = [0]
        first_ff = n_down
        assert state["tick"] > first_ff + (QW + 2 * KW) // UF - 1
        for f in units[first_ff:first_ff + (QW + 2 * KW) // UF]:
            f.sent(2)
        pl.semaphore_signal(free, inc=1, device_id=(rep, rank(a, b, 1 - c)), device_id_type=MESH)
        pl.semaphore_wait(free, 1)

        def grad_unit(d, out, cols):
            k = count[0]
            count[0] += 1
            start = cols * UF

            def tile(j, _):
                y = mm(hid_t[...], d[:, pl.ds(pl.multiple_of(start + j * 256, 256), 256)], 1, 0).astype(bf16)
                g_qkv[k % 4, :, :, :, :, :, lane(j, 256)] = y.reshape(g_qkv.shape[1:6] + (256,))
                return 0

            lax.fori_loop(0, UF // 256, tile, 0)
            unit(1, 2 * n_ff + k, g_qkv.at[k % 4], out, pl.ds(start, UF), k).begin()

        for u in range(QW // UF):
            grad_unit(dq, 4, u)
        for u in range(QW // UF):
            e1()
        tick(BACK_TICKS[0])
        for j in range(tiles):
            q_tiles[j].wait()
            dhid[:, j * 256:(j + 1) * 256] = mm(dq[...], wq_c[j % 2], 1, 1)
            if j + 2 < tiles:
                q_tiles.append(fetch_q(j + 2))
        tick(BACK_TICKS[1])
        for i in range(2):
            for d in range(1, half):
                across(i, d).wait_recv()

        def own_keys(j, _):
            t, u = r1[0, 0, block(j)].astype(f32), r1[1, 0, block(j)].astype(f32)
            for d in range(1, half):
                t, u = t + r2[0, d - 1, block(j)].astype(f32), u + r2[1, d - 1, block(j)].astype(f32)
            dkr[block(j), :] = t
            dvl[block(j), :] = u.astype(bf16)
            return 0

        lax.fori_loop(0, rows // RB, own_keys, 0)
        for u in range(KW // UF):
            grad_unit(dvl, 6, u)
        got[1].wait()

        def key_head(j, total):
            lanes = lane(j, HEAD_SIZE)
            y = kp_v[:, lanes]
            r = lax.rsqrt(jnp.mean(y * y, axis=-1, keepdims=True) + norm_epsilon)
            u = y * r
            dy = dkr[:, lanes]
            dy = dy * cos_r[...] - pltpu.roll(dy, HEAD_SIZE // 2, 1) * sin_r[...]
            total = total + jnp.sum(dy * u, axis=0, keepdims=True)
            dy = dy * k_gain[...]
            dkl[:, lanes] = (r * (dy - u * jnp.mean(dy * u, axis=-1, keepdims=True))).astype(bf16)
            return total

        gk = lax.fori_loop(0, KEY_VALUE_HEADS, key_head, jnp.zeros((1, HEAD_SIZE), f32))
        vec[2 * W // 128 + 1:2 * W // 128 + 2, :] = gk
        for u in range(KW // UF):
            grad_unit(dkl, 5, u)
        while state["e1"] < len(units):
            e1()
        tick(BACK_TICKS[2])
        for j in range(tiles):
            for f in kv_tiles[j]:
                f.wait()
            dhid[:, j * 256:(j + 1) * 256] += mm(dkl[...], wk_c[j % 2], 1, 1) + mm(dvl[...], wv_c[j % 2], 1, 1)
            if j + 2 < tiles:
                kv_tiles.append(fetch_kv(j + 2))
        tick(BACK_TICKS[3])
        got_x.wait()

        def first_norm(j, carry):
            total, square = carry
            d, gg = norm_back(hid_v[block(j), :].astype(f32), gain1[...], dhid[block(j), :])
            d = dres[block(j), :] + d
            dres[block(j), :] = d
            return total + gg, square + jnp.sum(valid[block(j), :] * d * d, axis=0, keepdims=True)

        g1, square = lax.fori_loop(0, T // RB, first_norm, (jnp.zeros((1, W), f32), jnp.zeros((1, W), f32)))
        for k in range(W // 128):
            vec[k:k + 1, :] = g1[:, k * 128:(k + 1) * 128]
        place = lax.broadcasted_iota(jnp.int32, (1, 128), 1)
        row = jnp.zeros((1, 128), f32)
        whole = lambda y: jnp.sum(jnp.sum(y, axis=0, keepdims=True), axis=1, keepdims=True)
        for k, y in enumerate((sums[0:1, :], sums[1:2, :], square, valid[...])):
            row = jnp.where(place == k, whole(y), row)
        vec[2 * W // 128 + 2:2 * W // 128 + 3, :] = row
        vec[2 * W // 128 + 3:, :] = jnp.zeros((vec.shape[0] - 2 * W // 128 - 3, 128), f32)

    pl.run_scoped(persistent, V((T, QW), bf16), V((T, KW), f32), V((T, KW), bf16))
    for i in range(2):
        for d in range(1, half):
            across(i, d).wait_send()

    width = CONTINUATION_LEN // n

    step = max(width, 8)

    def pack(j, _):
        y = dres[pl.ds(pl.multiple_of(rows + j * step, step), step), :].astype(bf16)
        for k in range(step // width):
            i = j * (step // width) + k
            grad_src[i // n, i % n] = y[k * width:(k + 1) * width]
        return 0

    lax.fori_loop(0, S * CONTINUATION_LEN // step, pack, 0)
    grad_spread = spread_copies(grad_src, grad_in, 2)
    begin_all(grad_spread)
    prompt_out = fetch(dres.at[pl.ds(0, rows)], d_prompt)
    tick()
    rounds = [(rep, rank(a, b, 1 - c)), (rep, rank(a, 1 - b, c))] + [flip(k) for k in range(bits)]
    vb[0] = vec[...]
    for k, to in enumerate(rounds):
        q = remote(vb.at[2 * k], vb.at[2 * k + 1], vs_.at[k], vr_.at[k], to)
        q.start()
        q.wait()
        vb[2 * k + 2] = vb[2 * k] + vb[2 * k + 1]
        if k in (0, 1, 2):
            tick()
    last, nr = 2 * len(rounds), len(rounds)
    zs = [remote(vb.at[last], vz.at[a], vs_.at[nr + d - 1], vr_.at[nr + d - 1], (rep, rank((a + d) % A, b, c))) for d in range(1, A)]
    for q in zs:
        q.start()
    vz[a] = vb[last]
    wait_all(grad_spread)
    reorder(grad_in, turned)
    grad_collect = collect_copies(turned, grad_out, 3)
    begin_all(grad_collect)
    for q in zs:
        q.wait()
    total = vz[0]
    for k in range(1, A):
        total = total + vz[k]
    vec[...] = total
    while state["tick"] < len(units) + 3:
        tick()
    wait_all(grad_collect)
    prompt_out.wait()
    for f in units:
        f.end()


def backward(index, mixed, dm, h2, act, gate, up, resid, wd, wg, wu, wo, attended, q_rot, lse, rs_q, ks, vs, k_rot, v, k_pre, wq, wk, wv, hidden, x,
             k_gain, q_gain, cos_r, sin_r, cos, sin, past, inside, valid, gain1, gain2, sums, rows, n, R, cid):
    group = PROMPT_LENGTH // rows
    half, A, (T, W), bits = group // 2, n // 4, dm.shape, R.bit_length() - 1
    FW, QW, KW = act.shape[1], attended.shape[1], k_rot.shape[1]
    UD, UF, UO = 256, 512, 512
    S = mixed.shape[0]
    V, D = pltpu.VMEM, pltpu.SemaphoreType.DMA
    shape = jax.ShapeDtypeStruct
    vm, hbm, sm = pl.BlockSpec(memory_space=pltpu.VMEM), pl.BlockSpec(memory_space=pl.ANY), pl.BlockSpec(memory_space=pltpu.SMEM)
    rh = lambda w: w.shape[0] // (2 * n)
    out_shape = [shape((2, rh(w), w.shape[1]), bf16) for w in (wd, wg, wu, wo, wq, wk, wv)]
    vec_rows = 2 * W // 128 + 8
    out_shape += [shape((vec_rows, 128), f32), shape((rows, W), f32), shape(mixed.shape, bf16), shape(mixed.shape, bf16)]
    scratch = []
    for count, r, w in ((W // UD, rh(wd), UD), (2 * (FW // UF) + (QW + 2 * KW) // UF, rh(wg), UF), (W // UO, rh(wo), UO)):
        k0 = fold_split(r)
        k1 = max(r - k0, 8)
        landing = 2 * (FW // UF) if w == UF and r == rh(wg) else count
        scratch += [V((landing, A, 2, 2, r, w), bf16), V((count, A, 2, k0, w), bf16), V((count, A, 2, k1, w) if k0 < r else (1, 1, 1, 8, 128), bf16), V((count, A, r, w), bf16),
                    V((count, A - 1, r, w), bf16), V((count, bits, r, w), bf16), V((count, bits, r, w), bf16)]
    m = W // UD + 2 * (FW // UF) + (QW + 2 * KW) // UF + W // UO
    turned = (n, S) + mixed.shape[2:]
    kv = (2, half, rows, KW)
    scratch += [V(kv, bf16), V((2, max(half - 1, 1), rows, KW), bf16), V(turned, bf16), V(turned, bf16), V(mixed.shape, bf16), V(turned, bf16),
                V((2 * (2 + bits) + 1, vec_rows, 128), f32), V((A, vec_rows, 128), f32), V((T, W), f32)]
    scratch += [D((m,)), D((m,)), D((m, 2)), D((m, 2)), D((m, 2)), D((m, 2)), D((m, A - 1)), D((m, A - 1)), D((m, bits)), D((m, bits)), D((m, 2))]
    scratch += [D((2 * A + 5 * (FW // UF) + 32,)), D((2, 5)), D((2, half)), D((2, half)), D((2, max(half - 1, 1))), D((2, max(half - 1, 1))), D((4, n - 1)), D((4, n - 1)), D((4,)),
                D((2 + bits + A - 1,)), D((2 + bits + A - 1,)), pltpu.SemaphoreType.REGULAR]
    hbm_in = [mixed, dm, h2, act, gate, up, resid, wd, wg, wu, wo, attended, q_rot, lse, rs_q, ks, vs, k_rot, v, k_pre, wq, wk, wv, hidden, x]
    in_vmem = {13, 14}
    res = pl.pallas_call(
        partial(backward_kernel, n, R, group, UD, UF, UO),
        out_shape=out_shape,
        in_specs=[sm] + [vm if k in in_vmem else hbm for k in range(len(hbm_in))] + [vm] * 12,
        out_specs=[hbm] * 7 + [vm] + [hbm] * 3,
        scratch_shapes=scratch,
        compiler_params=pltpu.CompilerParams(collective_id=cid, has_side_effects=True, vmem_limit_bytes=63 << 20),
        name="backward",
    )(index, *hbm_in, k_gain, q_gain, cos_r, sin_r, cos, sin, past, inside, valid, gain1, gain2, sums)
    return [r.reshape(-1, r.shape[-1]) for r in res[:7]], res[7], res[8], res[9], res[10]


def root_mean_scale(values, gain_vector):
    return (
        values
        * lax.rsqrt(jnp.mean(values * values, axis=-1, keepdims=True) + norm_epsilon)
        * gain_vector
    )


def swiglu(gate_pre, up_pre):
    return jax.nn.silu(gate_pre) * up_pre


def dot(x, y):
    return jnp.dot(x, y, preferred_element_type=f32)


def dot_tn(x, y):
    return jnp.einsum("ra,rb->ab", x, y, preferred_element_type=f32)


def dot_nt(x, y):
    return jnp.einsum("ra,ba->rb", x, y, preferred_element_type=f32)


def per_device(
    prompt_rows,
    suffix_rows,
    assignment,
    lengths,
    attention_gain,
    query_weight,
    key_matrix,
    value_matrix,
    query_gain,
    key_norm_gain,
    out_weight,
    mlp_gain,
    gate_weight,
    up_weight,
    down_weight,
    prompt_cotangent,
    suffix_cotangent,
):
    n, R = lax.axis_size("fsdp"), lax.axis_size("rep")
    rank = lax.axis_index("fsdp")
    rows = prompt_rows.shape[0]
    suffix = suffix_rows.shape[0]
    S = suffix // CONTINUATION_LEN
    total = rows + suffix
    width = MODEL_WIDTH

    pad = lambda v: jnp.pad(v.astype(f32).reshape(-1), (0, 128 - v.size))
    tile = jnp.stack([pad(v) for v in (attention_gain, mlp_gain, query_gain, key_norm_gain, assignment, lengths)])
    tile = jnp.pad(tile, ((0, 2), (0, 0)))
    cut = lambda v: v.reshape(S, n, CONTINUATION_LEN // n, width)
    (w_key, w_value, w_query), tiles, (staged_rows, staged_cotangent) = gather(
        [key_matrix, value_matrix, query_weight], tile, [cut(suffix_rows), cut(suffix_cotangent)], n, 0
    )
    gain_first = tiles[:, 0, : attention_gain.size].reshape(-1)
    gain_second = tiles[:, 1, : mlp_gain.size].reshape(-1)
    query_scale = tiles[:, 2, : query_gain.size].reshape(-1)
    key_scale = tiles[:, 3, : key_norm_gain.size].reshape(-1)

    owner = tiles[:, 4, :S].reshape(-1).astype(jnp.int32) // CONT
    slot_count = n * S
    ids = jnp.arange(slot_count, dtype=jnp.int32)
    ahead = (owner[None, :] < owner[:, None]) | ((owner[None, :] == owner[:, None]) & (ids[None, :] < ids[:, None]))
    place = jnp.sum(ahead.astype(jnp.int32), axis=1)
    hits = place[None, :] == ids[:, None]
    order = jnp.sum(jnp.where(hits, ids[None, :], 0), axis=1)
    slot_lengths = jnp.sum(jnp.where(hits, tiles[:, 5, :S].reshape(-1).astype(jnp.int32)[None, :], 0), axis=1)
    own_lengths = lax.dynamic_slice_in_dim(slot_lengths, rank * S, S)

    moved_rows = collect(order, [staged_rows], n, 1)[0].reshape(suffix, width)

    prompt_place = (rank * rows) % PROMPT_LENGTH + jnp.arange(rows, dtype=jnp.int32)
    suffix_place = jnp.arange(suffix, dtype=jnp.int32) % CONTINUATION_LEN
    suffix_slot = jnp.arange(suffix, dtype=jnp.int32) // CONTINUATION_LEN
    length_rows = jnp.repeat(own_lengths, CONTINUATION_LEN)
    suffix_valid = suffix_place < length_rows
    valid_rows = jnp.concatenate([jnp.ones((rows,), f32), suffix_valid.astype(f32)])
    token_positions = jnp.concatenate([prompt_place, PROMPT_LENGTH + suffix_place]).astype(f32)
    half = HEAD_SIZE // 2
    inverse = rope_theta ** (jnp.arange(half, dtype=f32) * (-2.0 / HEAD_SIZE))
    angles_t = inverse[:, None] * token_positions[None, :]
    cos_t, sin_t = jnp.cos(angles_t), jnp.sin(angles_t)
    cos_r, sin_r = cos_t.T, sin_t.T
    cos_rows = jnp.concatenate([cos_r, cos_r], axis=1)
    sin_rows = jnp.concatenate([-sin_r, sin_r], axis=1)
    past = jnp.where(jnp.arange(PROMPT_LENGTH, dtype=jnp.int32)[:, None] <= prompt_place[None, :], 0.0, masked_score).astype(f32)
    inside = jnp.where(
        (suffix_slot[:, None] == suffix_slot[None, :]) & (suffix_place[:, None] <= suffix_place[None, :]) & suffix_valid[:, None], 0.0, masked_score
    ).astype(f32)

    rows_low = jnp.concatenate([prompt_rows, moved_rows], 0)
    hidden = root_mean_scale(rows_low.astype(f32), gain_first).astype(bf16)
    key_gain_row = key_scale.reshape(1, HEAD_SIZE)
    query_gain_col = jnp.broadcast_to(query_scale[:, None], (HEAD_SIZE, 128))
    (
        w_out, w_gate, w_up, w_down, moved_cotangent, attended, query_rot, lse, query_rs, key_pre, key_rot, values,
        prompt_keys, prompt_values, residual, hidden_two, act, gate_low, up_low, mixed_low, sums,
    ) = forward(
        order, rows_low, hidden, w_key, w_value, w_query, [out_weight, gate_weight, up_weight, down_weight], key_gain_row, query_gain_col,
        cos_rows, sin_rows, cos_t, sin_t, past, inside, valid_rows[:, None], gain_second[None, :], staged_cotangent, rows, n, 2,
    )
    moved_cotangent = moved_cotangent.reshape(suffix, width)
    d_mixed_low = jnp.concatenate([prompt_cotangent, moved_cotangent], 0) * valid_rows[:, None].astype(bf16)
    shards, vec_sum, prompt_grad, suffix_mixed, suffix_grad = backward(
        place, cut(mixed_low[rows:]), d_mixed_low, hidden_two, act, gate_low, up_low, residual, w_down, w_gate, w_up, w_out, attended, query_rot, lse, query_rs,
        prompt_keys, prompt_values, key_rot, values, key_pre, w_query, w_key, w_value, hidden, rows_low, key_gain_row, query_gain_col,
        cos_rows, sin_rows, cos_t, sin_t, past, inside, valid_rows[:, None], gain_first[None, :], gain_second[None, :], sums, rows, n, R, 3,
    )
    suffix_mixed, suffix_grad = suffix_mixed.reshape(suffix, width), suffix_grad.reshape(suffix, width)
    g_down, g_gate, g_up, g_out, g_query, g_key, g_value = [g.astype(f32) for g in shards]
    flat = vec_sum.reshape(-1)

    def mine(first, size, part):
        return lax.dynamic_slice_in_dim(flat[first : first + size], rank * part, part)

    g_first = mine(0, width, attention_gain.size)
    g_second = mine(width, width, mlp_gain.size)
    g_query_gain = mine(2 * width, HEAD_SIZE, query_gain.size)
    g_key_gain = mine(2 * width + HEAD_SIZE, HEAD_SIZE, key_norm_gain.size)
    stat_sums = flat[2 * width + 2 * HEAD_SIZE : 2 * width + 2 * HEAD_SIZE + 4]
    token_norms = jnp.sqrt(stat_sums[:3] / (stat_sums[3] * width))
    return (
        mixed_low[:rows],
        suffix_mixed,
        prompt_grad,
        suffix_grad.astype(f32),
        g_first,
        g_query,
        g_key,
        g_value,
        g_query_gain,
        g_key_gain,
        g_out,
        g_second,
        g_gate,
        g_up,
        g_down,
        token_norms,
    )


def solution(mesh):
    placed = (
        P(("rep", "fsdp"), None),
        P(("rep", "fsdp"), None),
        P("rep", "fsdp"),
        P("rep", "fsdp"),
        P("fsdp"),
        P("fsdp", None),
        P("fsdp", None),
        P("fsdp", None),
        P("fsdp"),
        P("fsdp"),
        P("fsdp", None),
        P("fsdp"),
        P("fsdp", None),
        P("fsdp", None),
        P("fsdp", None),
        P(("rep", "fsdp"), None),
        P(("rep", "fsdp"), None),
    )
    return jax.shard_map(
        per_device,
        mesh=mesh,
        in_specs=placed,
        out_specs=(
            P(("rep", "fsdp"), None),
            P(("rep", "fsdp"), None),
            P(("rep", "fsdp"), None),
            P(("rep", "fsdp"), None),
            P("fsdp"),
            P("fsdp", None),
            P("fsdp", None),
            P("fsdp", None),
            P("fsdp"),
            P("fsdp"),
            P("fsdp", None),
            P("fsdp"),
            P("fsdp", None),
            P("fsdp", None),
            P("fsdp", None),
            P(),
        ),
        check_vma=False,
    )
```

profile of v0, /device:TPU:0, one launch (start us, length us, event | category | flops | bytes accessed | tf_op | source)
XLA Modules:
  0.0 593.8 jit_solution(18123719463710561244)
XLA Ops:
  0.7 0.7 bitcast_convert_fusion.10
  4.0 88.0 %gather.1 = (bf16[4,2,2,2,2,16,1024]{6,5,4,3,2,1,0:T(8,128)(2,1)}, bf16[4,2,2,2,2,16,1024]{6,5,4,3,2,1,0:T(8,128)(2,1)}, bf16[4,2,2,2,2,16,2048]{6,5,4,3,2,1,0:T...) custom-call(bf16[2,2,16,1024]{3,2,1,0:T(8,128)(2,1)} %bitcast.109, ...), custom_call_target="tpu_custom_call" | custom-call | tf_op jit(solution)/shard_map/gather/pallas_call | solution.py:140
  92.1 1.0 convert_reduce_fusion.1
  94.1 14.8 %collect.1 = bf16[2,16,8,1024]{3,2,1,0:T(8,128)(2,1)} custom-call(s32[32]{0:T(128)} %get-tuple-element.99.refs_0_, bf16[32,8,1024]{2,1,0:T(8,128)(2,1)} %bitcast.102), custom_call_target="tpu_custom_call" | custom-call | tf_op jit(solution)/shard_map/collect/pallas_call | solution.py:228
  108.9 2.1 pad_maximum_fusion.refs_1_.refs_25_
  111.4 1.3 fusion.2.refs_2_.refs_24_
  113.5 0.7 broadcast_in_dim.42.refs_11_.refs_27_
  114.2 1.0 fusion.4
  115.2 0.8 pad_maximum_fusion.1.refs_12_.refs_28_
  116.0 0.8 pad_maximum_fusion.2.refs_13_.refs_29_
  116.9 1.2 multiply_sine_fusion.1
  118.1 1.1 fusion.3.refs_16_.refs_32_
  119.4 0.9 and_select_fusion.refs_17_.refs_33_
  120.3 0.9 copy.35.refs_18_.refs_34_
  121.8 176.9 %forward.1 = (bf16[4,2,2,2,64,1024]{5,4,3,2,1,0:T(8,128)(2,1)}, bf16[4,2,2,2,32,3072]{5,4,3,2,1,0:T(8,128)(2,1)}, bf16[4,2,2,2,32,3072]{5,4,3,2,1,0:T(8,128)(2,1...) custom-call(s32[32]{0:T(128)} %get-tuple-element.99.refs_0_, ...), custom_call_target="tpu_custom_call" | custom-call | tf_op jit(solution)/shard_map/forward/pallas_call | solution.py:940
  298.7 2.3 fusion.10
  301.0 1.2 maximum_multiply_fusion.refs_2_
  302.9 272.5 %backward.1 = (bf16[2,96,1024]{2,1,0:T(8,128)(2,1)}, bf16[2,32,3072]{2,1,0:T(8,128)(2,1)}, bf16[2,32,3072]{2,1,0:T(8,128)(2,1)}, bf16[2,64,1024]{2,1,0:T(8,128)(...) custom-call(s32[32]{0:T(128)} %copy-done.13, ...), custom_call_target="tpu_custom_call" | custom-call | tf_op jit(solution)/shard_map/backward/pallas_call | solution.py:1611
  575.5 2.2 bitcast_convert_fusion
  577.7 0.7 slice_bitcast_fusion
  579.0 1.8 bitcast_convert_fusion.5
  580.8 0.7 bitcast_convert_fusion.7
  581.5 0.7 bitcast_convert_fusion.6
  582.2 0.8 fusion.11
  584.2 0.9 bitcast_convert_fusion.4
  585.6 1.0 bitcast_convert_fusion.3
  586.6 1.0 bitcast_convert_fusion.2
  587.5 1.0 bitcast_convert_fusion.1
  588.5 1.3 slice.70
  590.4 1.2 fusion.9
  591.6 0.8 copy.39
  592.4 1.0 copy.40
  (59 shorter events, 8.7 us)
Async XLA Ops:
  0.6 108.2 %copy-start.1 = (bf16[256,1024]{1,0:T(8,128)(2,1)S(1)}, bf16[256,1024]{1,0:T(8,128)(2,1)}, u32[]{:S(2)}) copy-start(bf16[256,1024]{1,0:T(8,128)(2,1)} %param.17) | copy-start | bytes 1572868
  92.1 18.9 %copy-start.12 = (f32[16,8,128]{2,1,0:T(8,128)S(1)}, f32[16,8,128]{2,1,0:T(8,128)}, u32[]{:S(2)}) copy-start(f32[16,8,128]{2,1,0:T(8,128)} %get-tuple-element.54) | copy-start | bytes 196612
  93.4 18.0 %copy-start.13 = (s32[32]{0:T(128)}, s32[32]{0:T(128)S(1)}, u32[]{:S(2)}) copy-start(s32[32]{0:T(128)S(1)} %convert_reduce_fusion.refs_0_) | copy-start | bytes 388
  108.8 2.3 copy-start
  298.7 2.3 copy-start.4
  298.7 2.3 copy-start.5
  575.4 5.3 copy-start.11
  575.4 6.1 %copy-start.10 = (bf16[2,32,1024]{2,1,0:T(8,128)(2,1)S(1)}, bf16[2,32,1024]{2,1,0:T(8,128)(2,1)}, u32[]{:S(2)}) copy-start(bf16[2,32,1024]{2,1,0:T(8,128)(2,1)} %get-tuple-element.87) | copy-start | bytes 393220
  575.4 8.7 %copy-start.9 = (bf16[2,64,1024]{2,1,0:T(8,128)(2,1)S(1)}, bf16[2,64,1024]{2,1,0:T(8,128)(2,1)}, u32[]{:S(2)}) copy-start(bf16[2,64,1024]{2,1,0:T(8,128)(2,1)} %get-tuple-element.88) | copy-start | bytes 786436
  575.4 10.2 %copy-start.8 = (bf16[2,32,3072]{2,1,0:T(8,128)(2,1)S(1)}, bf16[2,32,3072]{2,1,0:T(8,128)(2,1)}, u32[]{:S(2)}) copy-start(bf16[2,32,3072]{2,1,0:T(8,128)(2,1)} %get-tuple-element.89) | copy-start | bytes 1179652
  577.7 8.9 %copy-start.7 = (bf16[2,32,3072]{2,1,0:T(8,128)(2,1)S(1)}, bf16[2,32,3072]{2,1,0:T(8,128)(2,1)}, u32[]{:S(2)}) copy-start(bf16[2,32,3072]{2,1,0:T(8,128)(2,1)} %get-tuple-element.90) | copy-start | bytes 1179652
  580.8 6.8 %copy-start.6 = (bf16[2,96,1024]{2,1,0:T(8,128)(2,1)S(1)}, bf16[2,96,1024]{2,1,0:T(8,128)(2,1)}, u32[]{:S(2)}) copy-start(bf16[2,96,1024]{2,1,0:T(8,128)(2,1)} %get-tuple-element.91) | copy-start | bytes 1179652
  584.1 7.5 %copy-start.3 = (bf16[2,16,8,1024]{3,2,1,0:T(8,128)(2,1)S(1)}, bf16[2,16,8,1024]{3,2,1,0:T(8,128)(2,1)}, u32[]{:S(2)}) copy-start(bf16[2,16,8,1024]{3,2,1,0:T(8,128)(2,1)} %get-tuple-element.81) | copy-start | bytes 1572868
  585.6 6.8 %copy-start.2 = (f32[256,1024]{1,0:T(8,128)S(1)}, f32[256,1024]{1,0:T(8,128)}, u32[]{:S(2)}) copy-start(f32[256,1024]{1,0:T(8,128)} %get-tuple-element.142) | copy-start | bytes 3145732
where the time goes:
time: 604 us; the launch traced here: 594 us
  Pallas kernels  552 us (91%)
  other arithmetic  25.9 us (4%)
  local copies, waits for them, and re-layouts  13.9 us (2%)
    pallas_call x1, Pallas kernels, backward(): pl.pallas_call(partial(backward_kernel, n, R, group, UD, UF, UO), out_sha...  272 us
    pallas_call x1, Pallas kernels, forward(): pl.pallas_call(partial(forward_kernel, n, group), out_shape=out_shape, in...  177 us
    pallas_call x1, Pallas kernels, gather(): pl.pallas_call(partial(gather_kernel, n, m, k), out_shape=outs, in_specs=...  88 us
    pallas_call x1, Pallas kernels, collect(): pl.pallas_call(partial(collect_kernel, n, k), out_shape=[jax.ShapeDtypeSt...  14.8 us

commit v1 on v0

v1 whole, which is shorter than its diff:
```python
from functools import partial

import jax
import jax.numpy as jnp
from jax import lax
from jax.experimental import pallas as pl
from jax.experimental.pallas import tpu as pltpu
from jax.sharding import PartitionSpec as P

MODEL_WIDTH = 1024
QUERY_HEADS = 16
KEY_VALUE_HEADS = 8
HEAD_SIZE = 128
PROMPT_LENGTH = 1024
CONT = 8
CONTINUATION_LEN = 128

norm_epsilon = 1e-06
rope_theta = 1000000.0
masked_score = -1e30
MESH = pl.DeviceIdType.MESH
bf16 = jnp.bfloat16
f32 = jnp.float32

def position(n):
    rep = lax.axis_index("rep")
    rank = lax.axis_index("fsdp")
    return rep, rank // 4, (rank // 2) % 2, rank % 2


def meet(peers):
    barrier = pltpu.get_barrier_semaphore()
    for p in peers:
        pl.semaphore_signal(barrier, inc=1, device_id=p, device_id_type=MESH)
    pl.semaphore_wait(barrier, len(peers))


def remote(src, dst, send, recv, to):
    return pltpu.make_async_remote_copy(src, dst, send, recv, device_id=to, device_id_type=MESH)


def add_rows(count, out, first, second, step=None):
    def one(j, _):
        o = out(j)
        total = first(j)[...].astype(jnp.float32)
        for s in second:
            total = total + s(j)[...].astype(jnp.float32)
        o[...] = total.astype(o.dtype)
        return 0
    lax.fori_loop(0, count, one, 0)


LOG2E = 1.4426950408889634


def mm(x, y, cx, cy):
    return lax.dot_general(x, y, (((cx,), (cy,)), ((), ())), preferred_element_type=f32)


class Ring:
    def __init__(self, n, own, full, cols, sems, i, x_first):
        zs, zr, ss, sr, ls = sems
        A = n // 4
        rep, a, b, c = position(n)
        h = rep % 2
        every = slice(None)
        at = lambda *ix: full.at[(*ix, every, cols)]
        rank = lambda a, b, c: (a * 2 + b) * 2 + c
        ydev, xdev, cdev = (rep, rank(a, 1 - b, c)), (rep + 1 - 2 * h, rank(a, b, c)), (rep, rank(a, b, 1 - c))
        same = lambda ref, k, to: remote(ref, ref, ss.at[i, k], sr.at[i, k], to)
        mine = own.at[h, :, cols]
        self.local = lambda: [pltpu.make_async_copy(mine, at(a, b, c, h), ls.at[i])]
        self.along = lambda: [remote(mine, at(a, b, c, h), zs.at[i, d - 1], zr.at[i, d - 1], (rep, rank((a + d) % A, b, c))) for d in range(1, A)]
        self.second = lambda: [same(at(every, b, c, h), 0, xdev if x_first else ydev)]
        self.third = lambda: [same(at(every, b, c, every), 1, ydev) if x_first else same(at(every, every, c, h), 1, xdev)]
        self.last = lambda: [same(at(every, every, c, every), 2, cdev)]

    def begin(self):
        for q in self.local() + self.along():
            q.start()

    def turn(self, arrived, started):
        for q in arrived():
            q.wait_recv()
        for q in started():
            q.start()

    def step(self, k):
        if k == 0:
            for q in self.local():
                q.wait()
            self.turn(self.along, self.second)
        elif k == 1:
            self.turn(self.second, self.third)
        elif k == 2:
            self.turn(self.third, self.last)
        else:
            for q in self.last():
                q.wait_recv()

    def end(self):
        for q in self.along() + self.second() + self.third() + self.last():
            q.wait_send()


class Ticker:
    def __init__(self, rings, arrived=lambda i: None):
        self.rings, self.arrived, self.done = rings, arrived, [0] * 5

    def begin(self, count):
        for r in self.rings[self.done[0]:self.done[0] + count]:
            r.begin()
            self.done[0] += 1

    def __call__(self, count=1, lag=1):
        for _ in range(count):
            before = list(self.done)
            for k in range(1, 5):
                i = self.done[k]
                if i < len(self.rings) and before[k - 1] - i >= lag:
                    self.rings[i].step(k - 1)
                    self.done[k] += 1
                    if k == 1:
                        self.begin(self.done[1] + ALONG - self.done[0])
                    if k == 4:
                        self.arrived(i)

    def until(self, count):
        while self.done[4] < count:
            self()


ALONG = 2


def slot_spread(n, src, dst, sems, k, where):
    s, r, l = sems
    rep, me = where
    own = pltpu.make_async_copy(src.at[:, me], dst.at[me], l.at[k])
    return own, [remote(src.at[:, (me + d) % n], dst.at[me], s.at[k, d - 1], r.at[k, d - 1], (rep, (me + d) % n)) for d in range(1, n)]


def slot_collect(n, src, dst, sems, k, where):
    s, r, l = sems
    rep, me = where
    own = pltpu.make_async_copy(src.at[me], dst.at[:, me], l.at[k])
    return own, [remote(src.at[(me + d) % n], dst.at[:, me], s.at[k, d - 1], r.at[k, d - 1], (rep, (me + d) % n)) for d in range(1, n)]


def begin_all(pair):
    pair[0].start()
    for q in pair[1]:
        q.start()


def wait_all(pair):
    pair[0].wait()
    for q in pair[1]:
        q.wait()


def gather_kernel(n, CB, *refs):
    so, sk, sv, tile, pieces, wq, wk, wv, tiles, staged, zs, zr, ss, sr, ls, ts, tr, ps, pr, pls = refs
    rep, a, b, c = position(n)
    me = (a * 2 + b) * 2 + c
    h = rep % 2
    meet([(rep, (me + d) % n) for d in range(1, n)] + [(rep + 1 - 2 * h, me)])
    blocks = []
    for own, full in ((sk, wk), (sv, wv), (so, wq)):
        blocks += [(own, full, pl.ds(q * CB, CB)) for q in range(full.shape[-1] // CB)]
    rings = [Ring(n, own, full, cols, (zs, zr, ss, sr, ls), i, i % 2 == 0) for i, (own, full, cols) in enumerate(blocks)]
    tick = Ticker(rings)
    share = [remote(tile, tiles.at[me], ts.at[d - 1], tr.at[d - 1], (rep, (me + d) % n)) for d in range(1, n)]
    rows = slot_spread(n, pieces, staged, (ps, pr, pls), 0, (rep, me))
    for q in share:
        q.start()
    tiles[me] = tile[...]
    tick.begin(ALONG)
    begin_all(rows)
    tick.until(len(rings))
    for q in share:
        q.wait()
    wait_all(rows)
    for r in rings:
        r.end()


def gather(wk, wv, wq, tile, slots, n, cid):
    A, CB = n // 4, 512
    halves = [w.reshape(2, w.shape[0] // 2, w.shape[1]) for w in (wq, wk, wv)]
    m = sum(w.shape[1] for w in (wk, wv, wq)) // CB
    D = pltpu.SemaphoreType.DMA
    vm, hbm = pl.BlockSpec(memory_space=pltpu.VMEM), pl.BlockSpec(memory_space=pl.ANY)
    shape = jax.ShapeDtypeStruct
    res = pl.pallas_call(
        partial(gather_kernel, n, CB),
        out_shape=[shape((A, 2, 2) + w.shape, bf16) for w in halves] + [shape((n,) + tile.shape, f32), shape((n, slots.shape[0]) + slots.shape[2:], bf16)],
        in_specs=[hbm] * 3 + [vm] + [hbm],
        out_specs=[hbm] * 3 + [vm, hbm],
        scratch_shapes=[D((m, A - 1))] * 2 + [D((m, 3))] * 2 + [D((m,))] + [D((n - 1,))] * 2 + [D((1, n - 1))] * 2 + [D((1,))],
        compiler_params=pltpu.CompilerParams(collective_id=cid, has_side_effects=True),
        name="gather",
    )(*halves, tile, slots)
    w_query, w_key, w_value = [f.reshape(-1, f.shape[-1]) for f in res[:3]]
    return w_key, w_value, w_query, res[3], res[4]


def forward_kernel(n, group, *refs):
    it = iter(refs)
    take = lambda count: [next(it) for _ in range(count)]
    index, prompt, staged, cot, wk_h, wv_h, wq_h, so, sg, su, sd, k_gain, q_gain, cos_r, sin_r, cos, sin, past, inside, valid, gain1, gain2 = take(22)
    wo, wg, wu, wd, moved, gate, up = take(7)
    outs = take(13)
    lse_out, rs_out, stats = take(3)
    x, hidden, attended, q_out, k_pre, k_out, v, ks, vs, resid, h2, act, mixed = bufs = take(13)
    wk, wv, wq, ordered, landed, cot_in, o_buf, g_buf, u_buf, d_buf, g_st, u_st = take(12)
    zs, zr, ss, sr, ls, lds, fs, fr, gs, gr, kls, ps, pr, pls, gos, outs_sem, ins_sem = take(17)
    rows = ks.shape[2]
    T, W = x.shape
    half = group // 2
    rep, a, b, c = position(n)
    me = (a * 2 + b) * 2 + c
    first, slot = (me // group) * half, (me // 2) % half
    h = rep % 2
    ins = [pltpu.make_async_copy(src, dst, ins_sem.at[k]) for k, (src, dst) in enumerate(((wk_h, wk), (wv_h, wv), (wq_h, wq)))]
    for q in ins:
        q.start()
    meet([(rep, (me + d) % n) for d in range(1, n)] + [(rep + 1 - 2 * h, me)])
    saves = {id(buf): pltpu.make_async_copy(buf, out, outs_sem.at[k]) for k, (buf, out) in enumerate(zip(bufs, outs))}

    def save(*which):
        for buf in which:
            saves[id(buf)].start()

    OB, GB = o_buf.shape[-1], g_buf.shape[-1]
    n_out, n_mlp = wo.shape[-1] // OB, wg.shape[-1] // GB
    blocks = [(so, wo, pl.ds(q * OB, OB), o_buf.at[q]) for q in range(n_out)]
    for q in range(n_mlp):
        blocks += [(sg, wg, pl.ds(q * GB, GB), g_buf.at[q % 2]), (su, wu, pl.ds(q * GB, GB), u_buf.at[q % 2])]
    blocks += [(sd, wd, pl.ds(q * OB, OB), d_buf.at[q]) for q in range(n_out)]
    m = len(blocks)
    rings = [Ring(n, own, full, cols, (zs, zr, ss, sr, ls), i, i < X_FIRST) for i, (own, full, cols, _) in enumerate(blocks)]

    def load(i):
        _, full, cols, buf = blocks[i]
        return pltpu.make_async_copy(full.at[:, :, :, :, :, cols], buf, lds.at[i])

    used, late = [0], []

    def arrived(i):
        q = (i - n_out) // 2 if n_out <= i < n_out + 2 * n_mlp else 0
        if q < used[0] + 2:
            load(i).start()
        else:
            late.append(i)

    def release():
        used[0] += 1
        now, late[:] = [i for i in late if (i - n_out) // 2 < used[0] + 2], [i for i in late if (i - n_out) // 2 >= used[0] + 2]
        for i in now:
            load(i).start()

    tick = Ticker(rings, arrived)
    S = ordered.shape[1]

    def reorder(src, flat):
        def put(j, _):
            s = index[j]
            ordered[j // S, j % S] = src[s] if flat else src[s // S, s % S]
            return 0

        lax.fori_loop(0, n * S, put, 0)

    sems = (ps, pr, pls)
    reorder(staged, True)
    rows_in = slot_collect(n, ordered, landed, sems, 0, (rep, me))
    cot_spread = slot_spread(n, cot, cot_in, sems, 1, (rep, me))
    cot_collect = slot_collect(n, ordered, moved, sems, 2, (rep, me))
    begin_all(rows_in)
    tick.begin(ALONG)

    lane = lambda j, w: pl.ds(pl.multiple_of(j * w, w), w)
    heads = QUERY_HEADS // KEY_VALUE_HEADS
    pair = heads * HEAD_SIZE
    RB = 32
    block = lambda j: pl.ds(pl.multiple_of(j * RB, RB), RB)

    def norm(y, gain):
        return (y * lax.rsqrt(jnp.mean(y * y, axis=-1, keepdims=True) + norm_epsilon) * gain[...]).astype(bf16)

    def prompt_rows(j, _):
        y = prompt[block(j), :]
        x[block(j), :] = y
        hidden[block(j), :] = norm(y.astype(f32), gain1)
        return 0

    def kv_tile(part, j, _):
        kp = mm(hidden[part, :], wk[:, lane(j, 256)], 1, 0)
        k_pre[part, lane(j, 256)] = kp
        for g in range(2):
            y = kp[:, g * HEAD_SIZE:(g + 1) * HEAD_SIZE]
            y = y * lax.rsqrt(jnp.mean(y * y, axis=-1, keepdims=True) + norm_epsilon) * k_gain[...]
            k_out[part, lane(2 * j + g, HEAD_SIZE)] = (y * cos_r[part, :] + pltpu.roll(y, HEAD_SIZE // 2, 1) * sin_r[part, :]).astype(bf16)
        v[part, lane(j, 256)] = mm(hidden[part, :], wv[:, lane(j, 256)], 1, 0).astype(bf16)
        return 0

    lax.fori_loop(0, rows // RB, prompt_rows, 0)
    ins[0].wait()
    ins[1].wait()
    lax.fori_loop(0, wk.shape[1] // 256, partial(kv_tile, pl.ds(0, rows)), 0)
    parts = [(k_out, ks), (v, vs)]
    at = lambda s, c: (rep, (first + s) * 2 + c)
    mine = lambda i: parts[i][0].at[pl.ds(0, rows)]
    klocal = [pltpu.make_async_copy(mine(i), parts[i][1].at[slot, c], kls.at[i]) for i in range(2)]
    across = [remote(mine(i), parts[i][1].at[slot, c], fs.at[i, d - 1], fr.at[i, d - 1], at((slot + d) % half, c)) for i in range(2) for d in range(1, half)]
    sibling = [remote(mine(i), parts[i][1].at[slot, c], gs.at[i, 0], gr.at[i, 0], at(slot, 1 - c)) for i in range(2)]
    onward = []
    for i in range(2):
        for d in range(1, half):
            there = parts[i][1].at[(slot + half - d) % half, c]
            onward.append(remote(there, there, gs.at[i, d], gr.at[i, d], at(slot, 1 - c)))
    for q in across + sibling + klocal:
        q.start()
    tick()
    wait_all(rows_in)
    width = landed.shape[2]

    def slot_rows(j, _):
        s, p = j // (n * width // RB), j % (n * width // RB)
        k = RB // width
        if width % 8 == 0:
            y = landed[s, pl.ds(p * k, k)].astype(f32).reshape(RB, W)
        else:
            y = jnp.concatenate([landed[s, p * k + i].astype(f32) for i in range(k)], axis=0)
        at = pl.ds(pl.multiple_of(rows + j * RB, RB), RB)
        x[at, :] = y.astype(bf16)
        hidden[at, :] = norm(y, gain1)
        return 0

    lax.fori_loop(0, (T - rows) // RB, slot_rows, 0)
    lax.fori_loop(0, wk.shape[1] // 256, partial(kv_tile, pl.ds(rows, T - rows)), 0)
    tick()
    save(x, hidden, k_pre, k_out, v)
    ins[2].wait()

    def q_tile(j, _):
        qp = mm(hidden[...], wq[:, lane(j, pair)], 1, 0)
        for g in range(heads):
            y = qp[:, g * HEAD_SIZE:(g + 1) * HEAD_SIZE].T
            rs = lax.rsqrt(jnp.mean(y * y, axis=0, keepdims=True) + norm_epsilon)
            rs_out[j, g:g + 1, :] = rs
            y = y * rs * q_gain[:, 0:1]
            lo, hi = y[:HEAD_SIZE // 2], y[HEAD_SIZE // 2:]
            y = jnp.concatenate([lo * cos[...] - hi * sin[...], hi * cos[...] + lo * sin[...]], axis=0)
            q_out[lane(j * heads + g, HEAD_SIZE), :] = y.astype(bf16)
        for k, plan in FORWARD_PLAN[0]:
            pl.when(j == k)(partial(tick, *plan))
        return 0

    lax.fori_loop(0, KEY_VALUE_HEADS, q_tile, 0)
    begin_all(cot_spread)
    save(q_out)
    for q in across:
        q.wait_recv()
    for q in onward:
        q.start()
    tick(*FORWARD_PLAN[1])
    for q in klocal:
        q.wait()
    for q in sibling + onward:
        q.wait_recv()
    save(ks, vs)
    scale = HEAD_SIZE ** -0.5 * LOG2E

    def attend_head(j, _):
        kl = lane(j, HEAD_SIZE)
        kb = ks[:, :, :, kl].reshape(PROMPT_LENGTH, HEAD_SIZE)
        vb = vs[:, :, :, kl].reshape(PROMPT_LENGTH, HEAD_SIZE)
        for g in range(heads):
            ql = lane(j * heads + g, HEAD_SIZE)
            q = q_out[ql, :]
            p = jnp.exp2(mm(kb, q[:, :rows], 1, 0) * scale + past[...])
            total = jnp.sum(p, axis=0, keepdims=True)
            o = mm(vb, p.astype(bf16), 0, 0) / total
            attended[:rows, ql] = o.T.astype(bf16)
            lse_out[j, g:g + 1, :rows] = jnp.log2(total)
            p = jnp.exp2(mm(kb, q[:, rows:], 1, 0) * scale)
            r = jnp.exp2(mm(k_out[rows:, kl], q[:, rows:], 1, 0) * scale + inside[...])
            total = jnp.sum(p, axis=0, keepdims=True) + jnp.sum(r, axis=0, keepdims=True)
            o = (mm(vb, p.astype(bf16), 0, 0) + mm(v[rows:, kl], r.astype(bf16), 0, 0)) / total
            attended[rows:, ql] = o.T.astype(bf16)
            lse_out[j, g:g + 1, rows:] = jnp.log2(total)
        for k, plan in FORWARD_PLAN[2]:
            pl.when(j == k)(partial(tick, *plan))
        return 0

    lax.fori_loop(0, KEY_VALUE_HEADS, attend_head, 0)
    save(attended)
    wait_all(cot_spread)
    reorder(cot_in, False)
    begin_all(cot_collect)

    stats[...] = jnp.zeros_like(stats)
    for q in range(n_out):
        tick.until(q + 1)
        load(q).wait()

        def out_tile(j, _):
            cols = lane(q * (OB // 256) + j, 256)
            w = o_buf[q, :, :, :, :, :, lane(j, 256)].reshape(-1, 256)
            y = x[:, cols].astype(f32) + mm(attended[...], w, 1, 0)
            resid[:, cols] = y
            stats[1:2, :] += jnp.sum(valid[...] * y * y, axis=0, keepdims=True)
            return 0

        lax.fori_loop(0, OB // 256, out_tile, 0)

    def norm_rows(j, _):
        h2[block(j), :] = norm(resid[block(j), :], gain2)
        return 0

    lax.fori_loop(0, T // RB, norm_rows, 0)
    save(resid, h2)
    saved = lambda q: [pltpu.make_async_copy(g_st.at[q % 2], gate.at[:, pl.ds(q * GB, GB)], gos.at[q % 2, 0]),
                       pltpu.make_async_copy(u_st.at[q % 2], up.at[:, pl.ds(q * GB, GB)], gos.at[q % 2, 1])]
    for q in range(n_mlp):
        tick.until(n_out + 2 * q + 2)
        load(n_out + 2 * q).wait()
        load(n_out + 2 * q + 1).wait()
        if q >= 2:
            for s in saved(q - 2):
                s.wait()

        def mlp_tile(j, _):
            g = mm(h2[...], g_buf[q % 2, :, :, :, :, :, lane(j, 256)].reshape(-1, 256), 1, 0)
            u = mm(h2[...], u_buf[q % 2, :, :, :, :, :, lane(j, 256)].reshape(-1, 256), 1, 0)
            g_st[q % 2, :, lane(j, 256)] = g.astype(bf16)
            u_st[q % 2, :, lane(j, 256)] = u.astype(bf16)
            act[:, lane(q * (GB // 256) + j, 256)] = (g / (1.0 + jnp.exp(-g)) * u).astype(bf16)
            return 0

        lax.fori_loop(0, GB // 256, mlp_tile, 0)
        release()
        for s in saved(q):
            s.start()
    save(act)
    for q in range(n_out):
        tick.until(n_out + 2 * n_mlp + q + 1)
        load(n_out + 2 * n_mlp + q).wait()

        def down_tile(j, _):
            cols = lane(q * (OB // 256) + j, 256)
            w = d_buf[q, :, :, :, :, :, lane(j, 256)].reshape(-1, 256)
            y = resid[:, cols] + mm(act[...], w, 1, 0)
            mixed[:, cols] = y.astype(bf16)
            stats[0:1, :] += jnp.sum(valid[...] * y * y, axis=0, keepdims=True)
            return 0

        lax.fori_loop(0, OB // 256, down_tile, 0)
    save(mixed)
    for q in range(max(0, n_mlp - 2), n_mlp):
        for s in saved(q):
            s.wait()
    wait_all(cot_collect)
    for q in across + sibling + onward:
        q.wait_send()
    for r in rings:
        r.end()
    for q in saves.values():
        q.wait()


X_FIRST = 4
FORWARD_PLAN = (((1, (1,)), (3, (1,)), (5, (1,)), (7, (1,))), (1,), ((1, (1,)), (3, (1,)), (5, (1,)), (7, (1,))))


def forward(index, prompt, staged, cot, wk, wv, wq, shards, k_gain, q_gain, cos_r, sin_r, cos, sin, past, inside, valid, gain1, gain2, n, cid):
    rows, W = prompt.shape
    S = staged.shape[1]
    T = rows + S * CONTINUATION_LEN
    group = PROMPT_LENGTH // rows
    half, A = group // 2, n // 4
    halves = [s.reshape(2, s.shape[0] // 2, s.shape[1]) for s in shards]
    flat = staged.reshape((-1,) + staged.shape[2:])
    QW, KW, FW = wq.shape[1], wk.shape[1], shards[1].shape[1]
    D, V = pltpu.SemaphoreType.DMA, pltpu.VMEM
    shape = jax.ShapeDtypeStruct
    small = shape((KEY_VALUE_HEADS, 2, T), f32)
    keys = ((half, 2, rows, KW), bf16)
    kept = [((T, W), bf16), ((T, W), bf16), ((T, QW), bf16), ((QW, T), bf16), ((T, KW), f32), ((T, KW), bf16), ((T, KW), bf16), keys, keys,
            ((T, W), f32), ((T, W), bf16), ((T, FW), bf16), ((T, W), bf16)]
    out_shape = [shape((A, 2, 2) + s.shape, bf16) for s in halves] + [shape((S, n) + staged.shape[2:], bf16), shape((T, FW), bf16), shape((T, FW), bf16)]
    out_shape += [shape(*k) for k in kept] + [small, small, shape((8, 256), f32)]
    vm, hbm, sm = pl.BlockSpec(memory_space=pltpu.VMEM), pl.BlockSpec(memory_space=pl.ANY), pl.BlockSpec(memory_space=pltpu.SMEM)
    OB, GB = 512, 768
    n_out, n_mlp = W // OB, FW // GB
    m = 2 * n_out + 2 * n_mlp
    buf = lambda i, k, w: V((k, A, 2, 2) + halves[i].shape[:2] + (w,), bf16)
    res = pl.pallas_call(
        partial(forward_kernel, n, group),
        out_shape=out_shape,
        in_specs=[sm, vm, vm, hbm] + [hbm] * 7 + [vm] * 11,
        out_specs=[hbm] * 20 + [vm] * 3,
        scratch_shapes=[V(*k) for k in kept] + [V(wk.shape, bf16), V(wv.shape, bf16), V(wq.shape, bf16), V(staged.shape, bf16), V((S, n) + staged.shape[2:], bf16),
            V(staged.shape, bf16), buf(0, n_out, OB), buf(1, 2, GB), buf(2, 2, GB), buf(3, n_out, OB), V((2, T, GB), bf16), V((2, T, GB), bf16)]
        + [D((m, A - 1))] * 2 + [D((m, 3))] * 2 + [D((m,))] * 2 + [D((2, max(half - 1, 1)))] * 2 + [D((2, half))] * 2 + [D((2,))]
        + [D((3, n - 1))] * 2 + [D((3,)), D((2, 2)), D((13,)), D((3,))],
        compiler_params=pltpu.CompilerParams(collective_id=cid, has_side_effects=True, vmem_limit_bytes=63 << 20),
        name="forward",
    )(index, prompt, flat, cot, wk, wv, wq, *halves, k_gain, q_gain, cos_r, sin_r, cos, sin, past, inside, valid, gain1, gain2)
    res = list(res)
    for i, s in enumerate(shards):
        res[i] = res[i].reshape(-1, s.shape[1])
    for i in (14, 15):
        res[i] = res[i].reshape(PROMPT_LENGTH, KW)
    return res


PLAN = ((3, 5), (1, 3), (2, 8), (4, 5), (5, 8), (0, 1), (6, 8), (2, 8), (3, 3), (1, 5), (2, 8), (1, 3), (3, 8), (3, 1), (0, 6), (6, 2), (2, 4), (5, 4), (1, 2), (5, 3))


class Fold:
    def __init__(self, n, R, where, g, bufs, out, cols, sems, i):
        self.bufs, self.k, self.landing = bufs
        self.waited = set()
        self.g, self.out, self.cols, self.i, self.sems = g, out, cols, i, sems
        self.A, self.bits = n // 4, R.bit_length() - 1
        self.rep, self.a, self.b, self.c, self.h = where
        self.rh = self.bufs[0].shape[-2]
        self.k0 = fold_split(self.rh)

    b1 = property(lambda self: self.bufs[0].at[self.landing])
    b2y, b2x, b3, b4, s4, b5 = [property(lambda self, j=j: self.bufs[j].at[self.k]) for j in range(1, 7)]

    def device(self, da=0, db=0, dc=0, bit=None):
        rep, a, b, c = self.rep, self.a, self.b, self.c
        if bit is not None:
            rep = rep + (1 << bit) - 2 * (1 << bit) * ((rep // (1 << bit)) % 2)
        return (rep, (((a + da) % self.A) * 2 + (1 - b if db else b)) * 2 + (1 - c if dc else c))

    @property
    def ydev(self):
        return self.device(db=1)

    @property
    def xdev(self):
        return self.device(bit=0)

    @property
    def cdev(self):
        return self.device(dc=1)

    def zdev(self, d):
        return self.device(da=d)

    def flip(self, bit):
        return self.device(bit=bit)

    def hop(self, k):
        i, a, b, c, h, k0, rh = self.i, self.a, self.b, self.c, self.h, self.k0, self.rh
        s1s, s1r, s2s, s2r, s3s, s3r, s4s, s4r, s5s, s5r, _ = self.sems
        lo, hi = pl.ds(0, k0), pl.ds(k0, rh - k0)
        if k == 1:
            return [remote(self.g.at[:, :, 1 - c], self.b1, s1s.at[i], s1r.at[i], self.cdev)]
        if k == 2:
            q = [remote(self.b1.at[:, 1 - b, :, lo], self.b2y, s2s.at[i, 0], s2r.at[i, 0], self.ydev)]
            if k0 < rh:
                q.append(remote(self.b1.at[:, :, 1 - h, hi], self.b2x, s2s.at[i, 1], s2r.at[i, 1], self.xdev))
            return q
        if k == 3:
            q = [remote(self.b2y.at[:, 1 - h], self.b3.at[:, lo], s3s.at[i, 0], s3r.at[i, 0], self.xdev)]
            if k0 < rh:
                q.append(remote(self.b2x.at[:, 1 - b], self.b3.at[:, hi], s3s.at[i, 1], s3r.at[i, 1], self.ydev))
            return q
        if k == 4:
            return [remote(self.b3.at[(a + d) % self.A], self.b4.at[d - 1], s4s.at[i, d - 1], s4r.at[i, d - 1], self.zdev(d)) for d in range(1, self.A)]
        last = self.bits - 1
        return [remote(self.s4.at[last], self.b5.at[last], s5s.at[i, last], s5r.at[i, last], self.xdev)]

    def put(self, k):
        last = self.bits - 1
        half = self.h if k == 0 else 1 - self.h
        return pltpu.make_async_copy((self.s4 if k == 0 else self.b5).at[last], self.out.at[half, :, self.cols], self.sems[-1].at[self.i, k])

    def begin(self):
        for q in self.hop(1):
            q.start()

    def arrive(self, k):
        for q in self.hop(k):
            q.wait_recv()

    def go(self, k):
        for q in self.hop(k):
            q.start()

    def step(self, k):
        a, b, c, h, k0, rh = self.a, self.b, self.c, self.h, self.k0, self.rh
        self.arrive(k)
        lo, hi = pl.ds(0, k0), pl.ds(k0, rh - k0)
        if k == 1:
            for q in self.hop(1):
                q.wait_send()
            view = lambda ref: lambda j: ref.at[j // 4, (j // 2) % 2, j % 2]
            add_rows(self.A * 4, view(self.b1), view(self.b1), [lambda j: self.g.at[j // 4, (j // 2) % 2, c, j % 2]])
            return
        elif k == 2:
            view = lambda ref: lambda j: ref.at[j // 2, j % 2]
            add_rows(self.A * 2, view(self.b2y), view(self.b2y), [lambda j: self.b1.at[j // 2, b, j % 2, lo]])
            if k0 < rh:
                add_rows(self.A * 2, view(self.b2x), view(self.b2x), [lambda j: self.b1.at[j // 2, j % 2, h, hi]])
        elif k == 3:
            view = lambda part: lambda j: self.b3.at[j, part]
            add_rows(self.A, view(lo), view(lo), [lambda j: self.b2y.at[j, h]])
            if k0 < rh:
                add_rows(self.A, view(hi), view(hi), [lambda j: self.b2x.at[j, b]])
        elif k == 4:
            add_rows(1, lambda j: self.s4.at[0], lambda j: self.b3.at[a], [lambda j, d=d: self.b4.at[d] for d in range(self.A - 1)])
            s5s, s5r = self.sems[8:10]
            for r in range(self.bits - 1):
                q = remote(self.s4.at[r], self.b5.at[r], s5s.at[self.i, r], s5r.at[self.i, r], self.flip(r + 1))
                q.start()
                q.wait()
                add_rows(1, lambda j, r=r: self.s4.at[r + 1], lambda j, r=r: self.s4.at[r], [lambda j, r=r: self.b5.at[r]])
            self.put(0).start()
        else:
            self.put(1).start()
            return
        self.go(k + 1)

    def sent(self, k):
        if k not in self.waited:
            self.waited.add(k)
            for q in self.hop(k):
                q.wait_send()

    def end(self):
        for k in range(2, 6):
            self.sent(k)
        self.put(0).wait()
        self.put(1).wait()


def fold_split(rh):
    if (rh // 2) % 16 == 0:
        return rh // 2
    return rh // 32 * 16 if rh >= 32 else rh


def backward_kernel(n, R, group, UD, UF, UO, *refs):
    it = iter(refs)
    take = lambda count: [next(it) for _ in range(count)]
    index, mixed, dm, h2, act, gate, up, resid, wd, wg, wu, wo, attended, q_rot, lse, rs_q, ks, vs, k_rot, v, k_pre, wq, wk, wv, hidden, x = take(26)
    k_gain, q_gain, cos_r, sin_r, cos, sin, past, inside, valid, gain1, gain2, sums = take(12)
    outs = take(7)
    vec, d_prompt, mixed_out, grad_out = take(4)
    classes = [take(7) for _ in range(3)]
    r1, r2, mixed_in, turned, grad_src, grad_in, vb, vz, dres = take(9)
    fold_sems = take(11)
    lds, hs, gs, gr, fs, fr, a2s, a2r, a2l, vs_, vr_, free = take(12)
    A, T, W = n // 4, dm.shape[0], dm.shape[1]
    half, rows, KW = group // 2, r1.shape[2], k_rot.shape[1]
    FW, QW = act.shape[1], attended.shape[1]
    bits = R.bit_length() - 1
    rep, a, b, c = position(n)
    h = rep % 2
    rank = lambda a, b, c: (a * 2 + b) * 2 + c
    me = rank(a, b, c)
    first, slot = (me // group) * half, (me // 2) % half
    flip = lambda bit: (rep + (1 << bit) - 2 * (1 << bit) * ((rep // (1 << bit)) % 2), me)
    meet([(rep, (me + d) % n) for d in range(1, n)] + [flip(k) for k in range(bits)])

    lane = lambda j, w: pl.ds(pl.multiple_of(j * w, w), w)
    heads = QUERY_HEADS // KEY_VALUE_HEADS
    loads = iter(range(lds.shape[0]))

    def fetch(src, dst):
        q = pltpu.make_async_copy(src, dst, lds.at[next(loads)])
        q.start()
        return q

    S = turned.shape[1]

    trips = (a2s, a2r, a2l)
    spread_copies = lambda src, dst, k: slot_spread(n, src, dst, trips, k, (rep, me))
    collect_copies = lambda src, dst, k: slot_collect(n, src, dst, trips, k, (rep, me))

    def reorder(src, dst):
        def put(j, _):
            s = index[j]
            dst[j // S, j % S] = src[s // S, s % S]
            return 0

        lax.fori_loop(0, n * S, put, 0)

    mixed_spread = spread_copies(mixed, mixed_in, 0)
    grad_spread, grad_collect = spread_copies(grad_src, grad_in, 2), collect_copies(turned, grad_out, 3)

    units = []

    def unit(cls, k, g, out, cols, landing=None):
        units.append(Fold(n, R, (rep, a, b, c, h), g, (classes[cls], k, k if landing is None else landing), outs[out], cols, fold_sems, len(units)))
        return units[-1]

    done = [0] * 6

    def e1():
        units[done[0]].step(1)
        done[0] += 1

    def tick(count=1, lag=2):
        for _ in range(count):
            before = list(done)
            if done[1] < before[0]:
                units[done[1]].go(2)
                done[1] += 1
            for k in range(2, 6):
                if before[k - 1] - done[k] >= lag:
                    units[done[k]].step(k)
                    done[k] += 1

    n_down, n_ff, n_out = W // UD, FW // UF, W // UO
    V = pltpu.VMEM
    rh = lambda k: classes[k][0].shape[-2]
    AT, QT = FW // A, QW // A

    def down(act_c, act_t, g_down, dm_v):
        got = fetch(dm, dm_v)
        pieces = [fetch(act.at[:, pl.ds(0, AT)], act_c.at[0])]
        begin_all(mixed_spread)
        got.wait()
        for i in range(A):
            if i + 1 < A:
                pieces.append(fetch(act.at[:, pl.ds((i + 1) * AT, AT)], act_c.at[(i + 1) % 2]))
            pieces[i].wait()
            act_t[...] = act_c[i % 2].T

            def down_tile(j, _):
                y = mm(act_t[...], dm_v[:, lane(j, UD)], 1, 0).astype(bf16)
                g_down[j, i] = y.reshape(g_down.shape[2:])
                return 0

            lax.fori_loop(0, n_down, down_tile, 0)
        for u in range(n_down):
            unit(0, u, g_down.at[u], 0, pl.ds(u * UD, UD)).begin()
        for u in range(n_down):
            e1()

    pl.run_scoped(down, V((2, T, AT), bf16), V((AT, T), bf16), V((n_down, A, 2, 2, 2, rh(0), UD), bf16), V((T, W), bf16))
    tick(*PLAN[0])
    RB = 32
    block = lambda j: pl.ds(pl.multiple_of(j * RB, RB), RB)

    def norm_back(value, gain, grad):
        r = lax.rsqrt(jnp.mean(value * value, axis=-1, keepdims=True) + norm_epsilon)
        u = value * r
        t = grad * gain
        return r * (t - u * jnp.mean(t * u, axis=-1, keepdims=True)), jnp.sum(grad * u, axis=0, keepdims=True)

    def persistent(dq, dkr, dvl):
        def after_mlp(drl):
            pl.run_scoped(partial(mlp, drl), V((4, A, 2, 2, 2, rh(1), UF), bf16), V((2, UF, W), bf16), V((2, W, UF), bf16), V((2, W, UF), bf16), V((2, T, UF), bf16),
                          V((2, T, UF), bf16), V((T, UF), bf16), V((T, UF), bf16), V((W, T), bf16), V((T, W), bf16), V((T, W), bf16), V((T, W), f32))
            pl.run_scoped(partial(out_grad, drl), V((2, T, QT), bf16), V((QT, T), bf16), V((n_out, A, 2, 2, 2, rh(2), UO), bf16))
            wait_all(mixed_spread)
            reorder(mixed_in, turned)
            mixed_collect = collect_copies(turned, mixed_out, 1)
            begin_all(mixed_collect)
            pl.run_scoped(partial(attention, drl, dq, dkr, dvl), V((half, 2, rows, KW), bf16), V((half, 2, rows, KW), bf16), V((2, PROMPT_LENGTH, HEAD_SIZE), bf16),
                          V((2, PROMPT_LENGTH, HEAD_SIZE), bf16), V((2, heads * HEAD_SIZE, T), bf16), V((2, T, heads * HEAD_SIZE), bf16), V((2, heads * HEAD_SIZE, W), bf16),
                          V((T, KW), bf16), V((T, KW), bf16))
            wait_all(mixed_collect)

        pl.run_scoped(after_mlp, V((T, W), bf16))
        pl.run_scoped(partial(weights_back, dq, dkr, dvl), V((2, 256, QW), bf16), V((2, 256, KW), bf16), V((2, 256, KW), bf16), V((T, W), bf16), V((W, T), bf16),
                      V((T, KW), f32), V((T, KW), bf16), V((4, A, 2, 2, 2, rh(1), UF), bf16), V((T, W), f32))

    def mlp(drl, g_ff, wd_c, wg_c, wu_c, gate_c, up_c, dg_c, du_c, h2_t, h2_v, dm_v, dhid):
        got = [fetch(h2, h2_v), fetch(dm, dm_v)]

        def fetch_ff(q):
            cols, s = pl.ds(q * UF, UF), q % 2
            return [fetch(wd.at[cols], wd_c.at[s]), fetch(gate.at[:, cols], gate_c.at[s]), fetch(up.at[:, cols], up_c.at[s]),
                    fetch(wg.at[:, cols], wg_c.at[s]), fetch(wu.at[:, cols], wu_c.at[s])]

        ff = [fetch_ff(0)]
        got_resid = fetch(resid, dres)
        for f in got:
            f.wait()
        h2_t[...] = h2_v[...].T
        for q in range(n_ff):
            s = q % 2
            if q + 1 < n_ff:
                ff.append(fetch_ff(q + 1))
            for f in ff[q]:
                f.wait()

            def act_tile(j, _):
                cols = lane(j, 256)
                g, u = gate_c[s, :, cols].astype(f32), up_c[s, :, cols].astype(f32)
                da = mm(dm_v[...], wd_c[s, lane(j, 256), :], 1, 1)
                sg = 1.0 / (1.0 + jnp.exp(-g))
                du_c[:, cols] = (da * (g * sg)).astype(bf16)
                dg_c[:, cols] = (da * u * (sg * (1.0 + g * (1.0 - sg)))).astype(bf16)
                return 0

            lax.fori_loop(0, UF // 256, act_tile, 0)
            for k, d in enumerate((dg_c, du_c)):
                while done[0] < len(units) - 1:
                    e1()

                def ff_tile(j, _):
                    y = mm(h2_t[...], d[:, lane(j, 256)], 1, 0).astype(bf16)
                    g_ff[(2 * q + k) % 4, :, :, :, :, :, lane(j, 256)] = y.reshape(g_ff.shape[1:6] + (256,))
                    return 0

                lax.fori_loop(0, UF // 256, ff_tile, 0)
                unit(1, 2 * q + k, g_ff.at[(2 * q + k) % 4], 1 + k, pl.ds(q * UF, UF)).begin()

            def hid_tile(j, _):
                cols = lane(j, 256)
                y = mm(dg_c[...], wg_c[s, cols, :], 1, 1) + mm(du_c[...], wu_c[s, cols, :], 1, 1)
                dhid[:, cols] = y if q == 0 else dhid[:, cols] + y
                return 0

            lax.fori_loop(0, W // 256, hid_tile, 0)
            tick(*PLAN[1 + q])
        while done[0] < len(units):
            e1()
        got_resid.wait()

        def second_norm(j, total):
            d, gg = norm_back(dres[block(j), :], gain2[...], dhid[block(j), :])
            d = dm_v[block(j), :].astype(f32) + d
            dres[block(j), :] = d
            drl[block(j), :] = d.astype(bf16)
            return total + gg

        g2 = lax.fori_loop(0, T // RB, second_norm, jnp.zeros((1, W), f32))
        for k in range(W // 128):
            vec[W // 128 + k:W // 128 + k + 1, :] = g2[:, k * 128:(k + 1) * 128]

    def out_grad(drl, att_c, att_t, g_out):
        pieces = [fetch(attended.at[:, pl.ds(0, QT)], att_c.at[0])]
        for i in range(A):
            if i + 1 < A:
                pieces.append(fetch(attended.at[:, pl.ds((i + 1) * QT, QT)], att_c.at[(i + 1) % 2]))
            pieces[i].wait()
            att_t[...] = att_c[i % 2].T

            def out_tile(j, _):
                y = mm(att_t[...], drl[:, lane(j, UO)], 1, 0).astype(bf16)
                g_out[j, i] = y.reshape(g_out.shape[2:])
                return 0

            lax.fori_loop(0, n_out, out_tile, 0)
        for u in range(n_out):
            unit(2, u, g_out.at[u], 3, pl.ds(u * UO, UO)).begin()
        while done[0] < len(units):
            e1()
        tick(*PLAN[7])

    def attention(drl, dq, dkr, dvl, dk, dv, ks_c, vs_c, q_c, att_c, wo_c, kr_v, v_v):
        others = [fetch(k_rot, kr_v), fetch(v, v_v)]
        pair = lambda j: lane(j, heads * HEAD_SIZE)

        def head_copies(j):
            s = j % 2
            moves = [(ks.at[:, lane(j, HEAD_SIZE)], ks_c), (vs.at[:, lane(j, HEAD_SIZE)], vs_c), (q_rot.at[pair(j), :], q_c),
                     (attended.at[:, pair(j)], att_c), (wo.at[pair(j), :], wo_c)]
            return [pltpu.make_async_copy(src, dst.at[s], hs.at[s, k]) for k, (src, dst) in enumerate(moves)]

        for q in head_copies(jnp.int32(0)):
            q.start()
        for q in others:
            q.wait()
        scale = HEAD_SIZE ** -0.5
        plus = lambda p, q: q if p is None else p + q

        def head(j, gain_grad):
            @pl.when(j + 1 < KEY_VALUE_HEADS)
            def _():
                for q in head_copies(j + 1):
                    q.start()

            for q in head_copies(j):
                q.wait()
            at = j % 2
            kl = lane(j, HEAD_SIZE)
            kb, vb_ = ks_c[at], vs_c[at]
            dkp = dvp = dks = dvs = None
            do_pair = mm(drl[...], wo_c[at], 1, 1)
            out_pair = att_c[at].astype(f32)
            for g in range(heads):
                sl = slice(g * HEAD_SIZE, (g + 1) * HEAD_SIZE)
                q = q_c[at, sl, :]
                do = do_pair[:, sl].astype(bf16)
                delta = jnp.sum((do.astype(f32) * out_pair[:, sl]).T, axis=0, keepdims=True)
                log_total = lse[j, g:g + 1, :]
                parts = []
                for suffix in range(2):
                    part = slice(rows, None) if suffix else slice(0, rows)
                    qp, dop, lp, dp = q[:, part], do[part], log_total[:, part], delta[:, part]
                    pieces = [(kb, vb_, None if suffix else past[...])]
                    if suffix:
                        pieces.append((kr_v[rows:, kl], v_v[rows:, kl], inside[...]))
                    total = None
                    for i, (kk, vv, bias) in enumerate(pieces):
                        s = mm(kk, qp, 1, 0) * (scale * LOG2E) - lp
                        p = jnp.exp2(s if bias is None else s + bias)
                        ds = (p * (mm(vv, dop, 1, 1) - dp)).astype(bf16)
                        gv, gk = mm(p.astype(bf16), dop, 1, 0), mm(ds, qp, 1, 1)
                        total = plus(total, mm(kk, ds, 0, 0))
                        if i:
                            dks, dvs = plus(dks, gk), plus(dvs, gv)
                        else:
                            dkp, dvp = plus(dkp, gk), plus(dvp, gv)
                    parts.append(total)
                d = jnp.concatenate(parts, axis=1) * scale
                m = HEAD_SIZE // 2
                cs, sn = cos[...], sin[...]
                dy = jnp.concatenate([d[:m] * cs + d[m:] * sn, d[m:] * cs - d[:m] * sn], axis=0)
                qf = q.astype(f32)
                u = jnp.concatenate([qf[:m] * cs + qf[m:] * sn, qf[m:] * cs - qf[:m] * sn], axis=0) / q_gain[:, 0:1]
                gg = dy * u
                for t in range(T // 128):
                    gain_grad = gain_grad + gg[:, t * 128:(t + 1) * 128]
                dy = dy * q_gain[:, 0:1]
                dx = rs_q[j, g:g + 1, :] * (dy - u * jnp.mean(dy * u, axis=0, keepdims=True))
                dq[:, lane(j * heads + g, HEAD_SIZE)] = dx.T.astype(bf16)
            dk[:, :, :, kl] = (dkp * scale).astype(bf16).reshape(half, 2, rows, HEAD_SIZE)
            dv[:, :, :, kl] = dvp.astype(bf16).reshape(half, 2, rows, HEAD_SIZE)
            dkr[rows:, kl] = dks * scale
            dvl[rows:, kl] = dvs.astype(bf16)
            for k in range(KEY_VALUE_HEADS - 1):
                if PLAN[8 + k][0]:
                    pl.when(j == k)(partial(tick, *PLAN[8 + k]))
            return gain_grad

        gain_grad = lax.fori_loop(0, KEY_VALUE_HEADS, head, jnp.zeros((HEAD_SIZE, 128), f32))
        vec[2 * W // 128:2 * W // 128 + 1, :] = jnp.sum(gain_grad.T, axis=0, keepdims=True)
        grads = [dk, dv]
        home = lambda s, c: (rep, (first + s) * 2 + c)

        def to_sibling(i, d):
            return remote(grads[i].at[(slot + d) % half, 1 - c], r1.at[i, d], gs.at[i, d], gr.at[i, d], home(slot, 1 - c))

        order = list(range(1, half)) + [0]
        for d in order:
            for i in range(2):
                to_sibling(i, d).start()
        for d in order:
            for i in range(2):
                to_sibling(i, d).wait_recv()

                def one(j, _):
                    r1[i, d, block(j)] = (grads[i][(slot + d) % half, c, block(j)].astype(f32) + r1[i, d, block(j)].astype(f32)).astype(bf16)
                    return 0

                lax.fori_loop(0, rows // RB, one, 0)
                if d:
                    across(i, d).start()
        for d in order:
            for i in range(2):
                to_sibling(i, d).wait_send()
        tick(*PLAN[15])

    def across(i, d):
        return remote(r1.at[i, d], r2.at[i, d - 1], fs.at[i, d - 1], fr.at[i, d - 1], (rep, (first + (slot + d) % half) * 2 + c))

    def weights_back(dq, dkr, dvl, wq_c, wk_c, wv_c, hid_v, hid_t, kp_v, dkl, g_qkv, dhid):
        got = [fetch(hidden, hid_v), fetch(k_pre, kp_v)]
        tiles = W // 256
        fetch_q = lambda j: fetch(wq.at[pl.ds(j * 256, 256)], wq_c.at[j % 2])
        fetch_kv = lambda j, s: [fetch(wk.at[pl.ds(j * 256, 256)], wk_c.at[s]), fetch(wv.at[pl.ds(j * 256, 256)], wv_c.at[s])]
        q_tiles, kv_tiles = [fetch_q(0), fetch_q(1)], [fetch_kv(0, 0), fetch_kv(1, 1)]
        got[0].wait()
        hid_t[...] = hid_v[...].T
        got_x = fetch(x, hid_v)
        count = [0]
        first_ff = n_down
        while done[2] < first_ff + (QW + 2 * KW) // UF:
            tick()
        for f in units[first_ff:first_ff + (QW + 2 * KW) // UF]:
            f.sent(2)
        pl.semaphore_signal(free, inc=1, device_id=(rep, rank(a, b, 1 - c)), device_id_type=MESH)
        pl.semaphore_wait(free, 1)

        def grad_unit(d, out, cols):
            k = count[0]
            count[0] += 1
            start = cols * UF

            def tile(j, _):
                y = mm(hid_t[...], d[:, pl.ds(pl.multiple_of(start + j * 256, 256), 256)], 1, 0).astype(bf16)
                g_qkv[k % 4, :, :, :, :, :, lane(j, 256)] = y.reshape(g_qkv.shape[1:6] + (256,))
                return 0

            lax.fori_loop(0, UF // 256, tile, 0)
            unit(1, 2 * n_ff + k, g_qkv.at[k % 4], out, pl.ds(start, UF), k).begin()

        for u in range(QW // UF):
            grad_unit(dq, 4, u)
        for u in range(QW // UF):
            e1()
        tick(*PLAN[16])
        got[1].wait()

        def key_head(part, j, total):
            lanes = lane(j, HEAD_SIZE)
            y = kp_v[part, lanes]
            r = lax.rsqrt(jnp.mean(y * y, axis=-1, keepdims=True) + norm_epsilon)
            u = y * r
            dy = dkr[part, lanes]
            dy = dy * cos_r[part, :] - pltpu.roll(dy, HEAD_SIZE // 2, 1) * sin_r[part, :]
            total = total + jnp.sum(dy * u, axis=0, keepdims=True)
            dy = dy * k_gain[...]
            dkl[part, lanes] = (r * (dy - u * jnp.mean(dy * u, axis=-1, keepdims=True))).astype(bf16)
            return total

        def first_norm(j, carry):
            total, square = carry
            d, gg = norm_back(hid_v[block(j), :].astype(f32), gain1[...], dhid[block(j), :])
            d = dres[block(j), :] + d
            dres[block(j), :] = d
            return total + gg, square + jnp.sum(valid[block(j), :] * d * d, axis=0, keepdims=True)

        ours, theirs = pl.ds(rows, T - rows), pl.ds(0, rows)
        gk = lax.fori_loop(0, KEY_VALUE_HEADS, partial(key_head, ours), jnp.zeros((1, HEAD_SIZE), f32))
        for j in range(tiles):
            cols = pl.ds(j * 256, 256)
            q_tiles[j].wait()
            for f in kv_tiles[j]:
                f.wait()
            dhid[:, cols] = mm(dq[...], wq_c[j % 2], 1, 1)
            dhid[ours, cols] += mm(dkl[ours, :], wk_c[j % 2], 1, 1) + mm(dvl[ours, :], wv_c[j % 2], 1, 1)
            if j + 2 < tiles:
                q_tiles.append(fetch_q(j + 2))
            kv_tiles.append(fetch_kv((j + 2) % tiles, j % 2))
        got_x.wait()
        zero = jnp.zeros((1, W), f32)
        g1, square = lax.fori_loop(rows // RB, T // RB, first_norm, (zero, zero))
        width = CONTINUATION_LEN // n
        step = max(width, 8)

        def pack(j, _):
            y = dres[pl.ds(pl.multiple_of(rows + j * step, step), step), :].astype(bf16)
            for k in range(step // width):
                i = j * (step // width) + k
                grad_src[i // n, i % n] = y[k * width:(k + 1) * width]
            return 0

        lax.fori_loop(0, S * CONTINUATION_LEN // step, pack, 0)
        begin_all(grad_spread)
        tick(*PLAN[17])
        for i in range(2):
            for d in range(1, half):
                across(i, d).wait_recv()

        def own_keys(j, _):
            t, u = r1[0, 0, block(j)].astype(f32), r1[1, 0, block(j)].astype(f32)
            for d in range(1, half):
                t, u = t + r2[0, d - 1, block(j)].astype(f32), u + r2[1, d - 1, block(j)].astype(f32)
            dkr[block(j), :] = t
            dvl[block(j), :] = u.astype(bf16)
            return 0

        lax.fori_loop(0, rows // RB, own_keys, 0)
        for u in range(KW // UF):
            grad_unit(dvl, 6, u)
        gk = lax.fori_loop(0, KEY_VALUE_HEADS, partial(key_head, theirs), gk)
        vec[2 * W // 128 + 1:2 * W // 128 + 2, :] = gk
        for u in range(KW // UF):
            grad_unit(dkl, 5, u)
        while done[0] < len(units):
            e1()
        tick(*PLAN[18])
        wait_all(grad_spread)
        reorder(grad_in, turned)
        begin_all(grad_collect)
        for j in range(tiles):
            cols, s = pl.ds(j * 256, 256), (tiles + j) % 2
            for f in kv_tiles[tiles + j]:
                f.wait()
            dhid[theirs, cols] += mm(dkl[theirs, :], wk_c[s], 1, 1) + mm(dvl[theirs, :], wv_c[s], 1, 1)
            if j + 2 < tiles:
                kv_tiles.append(fetch_kv(j + 2, s))
        tick(*PLAN[19])
        g1, square = lax.fori_loop(0, rows // RB, first_norm, (g1, square))
        for k in range(W // 128):
            vec[k:k + 1, :] = g1[:, k * 128:(k + 1) * 128]
        place = lax.broadcasted_iota(jnp.int32, (1, 128), 1)
        row = jnp.zeros((1, 128), f32)
        whole = lambda y: jnp.sum(jnp.sum(y, axis=0, keepdims=True), axis=1, keepdims=True)
        for k, y in enumerate((sums[0:1, :], sums[1:2, :], square, valid[...])):
            row = jnp.where(place == k, whole(y), row)
        vec[2 * W // 128 + 2:2 * W // 128 + 3, :] = row
        vec[2 * W // 128 + 3:, :] = jnp.zeros((vec.shape[0] - 2 * W // 128 - 3, 128), f32)

    pl.run_scoped(persistent, V((T, QW), bf16), V((T, KW), f32), V((T, KW), bf16))
    for i in range(2):
        for d in range(1, half):
            across(i, d).wait_send()

    prompt_out = fetch(dres.at[pl.ds(0, rows)], d_prompt)
    tick(2, 1)
    rounds = [(rep, rank(a, b, 1 - c)), (rep, rank(a, 1 - b, c))] + [flip(k) for k in range(bits)]
    vb[0] = vec[...]
    for k, to in enumerate(rounds):
        q = remote(vb.at[2 * k], vb.at[2 * k + 1], vs_.at[k], vr_.at[k], to)
        q.start()
        q.wait()
        vb[2 * k + 2] = vb[2 * k] + vb[2 * k + 1]
        tick(2, 1)
    last, nr = 2 * len(rounds), len(rounds)
    zs = [remote(vb.at[last], vz.at[a], vs_.at[nr + d - 1], vr_.at[nr + d - 1], (rep, rank((a + d) % A, b, c))) for d in range(1, A)]
    for q in zs:
        q.start()
    vz[a] = vb[last]
    for q in zs:
        q.wait()
    total = vz[0]
    for k in range(1, A):
        total = total + vz[k]
    vec[...] = total
    while done[5] < len(units):
        tick(lag=1)
    wait_all(grad_collect)
    prompt_out.wait()
    for f in units:
        f.end()


def backward(index, mixed, dm, h2, act, gate, up, resid, wd, wg, wu, wo, attended, q_rot, lse, rs_q, ks, vs, k_rot, v, k_pre, wq, wk, wv, hidden, x,
             k_gain, q_gain, cos_r, sin_r, cos, sin, past, inside, valid, gain1, gain2, sums, rows, n, R, cid):
    group = PROMPT_LENGTH // rows
    half, A, (T, W), bits = group // 2, n // 4, dm.shape, R.bit_length() - 1
    FW, QW, KW = act.shape[1], attended.shape[1], k_rot.shape[1]
    UD, UF, UO = 256, 512, 512
    S = mixed.shape[0]
    V, D = pltpu.VMEM, pltpu.SemaphoreType.DMA
    shape = jax.ShapeDtypeStruct
    vm, hbm, sm = pl.BlockSpec(memory_space=pltpu.VMEM), pl.BlockSpec(memory_space=pl.ANY), pl.BlockSpec(memory_space=pltpu.SMEM)
    rh = lambda w: w.shape[0] // (2 * n)
    out_shape = [shape((2, rh(w), w.shape[1]), bf16) for w in (wd, wg, wu, wo, wq, wk, wv)]
    vec_rows = 2 * W // 128 + 8
    out_shape += [shape((vec_rows, 128), f32), shape((rows, W), f32), shape(mixed.shape, bf16), shape(mixed.shape, bf16)]
    scratch = []
    for count, r, w in ((W // UD, rh(wd), UD), (2 * (FW // UF) + (QW + 2 * KW) // UF, rh(wg), UF), (W // UO, rh(wo), UO)):
        k0 = fold_split(r)
        k1 = max(r - k0, 8)
        landing = 2 * (FW // UF) if w == UF and r == rh(wg) else count
        scratch += [V((landing, A, 2, 2, r, w), bf16), V((count, A, 2, k0, w), bf16), V((count, A, 2, k1, w) if k0 < r else (1, 1, 1, 8, 128), bf16), V((count, A, r, w), bf16),
                    V((count, A - 1, r, w), bf16), V((count, bits, r, w), bf16), V((count, bits, r, w), bf16)]
    m = W // UD + 2 * (FW // UF) + (QW + 2 * KW) // UF + W // UO
    turned = (n, S) + mixed.shape[2:]
    kv = (2, half, rows, KW)
    scratch += [V(kv, bf16), V((2, max(half - 1, 1), rows, KW), bf16), V(turned, bf16), V(turned, bf16), V(mixed.shape, bf16), V(turned, bf16),
                V((2 * (2 + bits) + 1, vec_rows, 128), f32), V((A, vec_rows, 128), f32), V((T, W), f32)]
    scratch += [D((m,)), D((m,)), D((m, 2)), D((m, 2)), D((m, 2)), D((m, 2)), D((m, A - 1)), D((m, A - 1)), D((m, bits)), D((m, bits)), D((m, 2))]
    scratch += [D((2 * A + 5 * (FW // UF) + 32,)), D((2, 5)), D((2, half)), D((2, half)), D((2, max(half - 1, 1))), D((2, max(half - 1, 1))), D((4, n - 1)), D((4, n - 1)), D((4,)),
                D((2 + bits + A - 1,)), D((2 + bits + A - 1,)), pltpu.SemaphoreType.REGULAR]
    hbm_in = [mixed, dm, h2, act, gate, up, resid, wd, wg, wu, wo, attended, q_rot, lse, rs_q, ks, vs, k_rot, v, k_pre, wq, wk, wv, hidden, x]
    in_vmem = {13, 14}
    res = pl.pallas_call(
        partial(backward_kernel, n, R, group, UD, UF, UO),
        out_shape=out_shape,
        in_specs=[sm] + [vm if k in in_vmem else hbm for k in range(len(hbm_in))] + [vm] * 12,
        out_specs=[hbm] * 7 + [vm] + [hbm] * 3,
        scratch_shapes=scratch,
        compiler_params=pltpu.CompilerParams(collective_id=cid, has_side_effects=True, vmem_limit_bytes=63 << 20),
        name="backward",
    )(index, *hbm_in, k_gain, q_gain, cos_r, sin_r, cos, sin, past, inside, valid, gain1, gain2, sums)
    return [r.reshape(-1, r.shape[-1]) for r in res[:7]], res[7], res[8], res[9], res[10]


def per_device(
    prompt_rows,
    suffix_rows,
    assignment,
    lengths,
    attention_gain,
    query_weight,
    key_matrix,
    value_matrix,
    query_gain,
    key_norm_gain,
    out_weight,
    mlp_gain,
    gate_weight,
    up_weight,
    down_weight,
    prompt_cotangent,
    suffix_cotangent,
):
    n, R = lax.axis_size("fsdp"), lax.axis_size("rep")
    rank = lax.axis_index("fsdp")
    rows = prompt_rows.shape[0]
    suffix = suffix_rows.shape[0]
    S = suffix // CONTINUATION_LEN
    total = rows + suffix
    width = MODEL_WIDTH

    pad = lambda v: jnp.pad(v.astype(f32).reshape(-1), (0, 128 - v.size))
    tile = jnp.stack([pad(v) for v in (attention_gain, mlp_gain, query_gain, key_norm_gain, assignment, lengths)])
    tile = jnp.pad(tile, ((0, 2), (0, 0)))
    cut = lambda v: v.reshape(S, n, CONTINUATION_LEN // n, width)
    w_key, w_value, w_query, tiles, staged = gather(key_matrix, value_matrix, query_weight, tile, cut(suffix_rows), n, 0)
    gain_first = tiles[:, 0, : attention_gain.size].reshape(-1)
    gain_second = tiles[:, 1, : mlp_gain.size].reshape(-1)
    query_scale = tiles[:, 2, : query_gain.size].reshape(-1)
    key_scale = tiles[:, 3, : key_norm_gain.size].reshape(-1)

    owner = tiles[:, 4, :S].reshape(-1).astype(jnp.int32) // CONT
    slot_count = n * S
    ids = jnp.arange(slot_count, dtype=jnp.int32)
    ahead = (owner[None, :] < owner[:, None]) | ((owner[None, :] == owner[:, None]) & (ids[None, :] < ids[:, None]))
    place = jnp.sum(ahead.astype(jnp.int32), axis=1)
    hits = place[None, :] == ids[:, None]
    order = jnp.sum(jnp.where(hits, ids[None, :], 0), axis=1)
    slot_lengths = jnp.sum(jnp.where(hits, tiles[:, 5, :S].reshape(-1).astype(jnp.int32)[None, :], 0), axis=1)
    own_lengths = lax.dynamic_slice_in_dim(slot_lengths, rank * S, S)

    prompt_place = (rank * rows) % PROMPT_LENGTH + jnp.arange(rows, dtype=jnp.int32)
    suffix_place = jnp.arange(suffix, dtype=jnp.int32) % CONTINUATION_LEN
    suffix_slot = jnp.arange(suffix, dtype=jnp.int32) // CONTINUATION_LEN
    length_rows = jnp.repeat(own_lengths, CONTINUATION_LEN)
    suffix_valid = suffix_place < length_rows
    valid_rows = jnp.concatenate([jnp.ones((rows,), f32), suffix_valid.astype(f32)])
    token_positions = jnp.concatenate([prompt_place, PROMPT_LENGTH + suffix_place]).astype(f32)
    half = HEAD_SIZE // 2
    inverse = rope_theta ** (jnp.arange(half, dtype=f32) * (-2.0 / HEAD_SIZE))
    angles_t = inverse[:, None] * token_positions[None, :]
    cos_t, sin_t = jnp.cos(angles_t), jnp.sin(angles_t)
    cos_r, sin_r = cos_t.T, sin_t.T
    cos_rows = jnp.concatenate([cos_r, cos_r], axis=1)
    sin_rows = jnp.concatenate([-sin_r, sin_r], axis=1)
    past = jnp.where(jnp.arange(PROMPT_LENGTH, dtype=jnp.int32)[:, None] <= prompt_place[None, :], 0.0, masked_score).astype(f32)
    inside = jnp.where(
        (suffix_slot[:, None] == suffix_slot[None, :]) & (suffix_place[:, None] <= suffix_place[None, :]) & suffix_valid[:, None], 0.0, masked_score
    ).astype(f32)

    key_gain_row = key_scale.reshape(1, HEAD_SIZE)
    query_gain_col = jnp.broadcast_to(query_scale[:, None], (HEAD_SIZE, 128))
    (
        w_out, w_gate, w_up, w_down, moved_cotangent, gate_low, up_low, rows_low, hidden, attended, query_rot, key_pre, key_rot, values,
        prompt_keys, prompt_values, residual, hidden_two, act, mixed_low, lse, query_rs, sums,
    ) = forward(
        order, prompt_rows, staged, cut(suffix_cotangent), w_key, w_value, w_query, [out_weight, gate_weight, up_weight, down_weight], key_gain_row,
        query_gain_col, cos_rows, sin_rows, cos_t, sin_t, past, inside, valid_rows[:, None], gain_first[None, :], gain_second[None, :], n, 2,
    )
    moved_cotangent = moved_cotangent.reshape(suffix, width)
    d_mixed_low = jnp.concatenate([prompt_cotangent, moved_cotangent], 0) * valid_rows[:, None].astype(bf16)
    shards, vec_sum, prompt_grad, suffix_mixed, suffix_grad = backward(
        place, cut(mixed_low[rows:]), d_mixed_low, hidden_two, act, gate_low, up_low, residual, w_down, w_gate, w_up, w_out, attended, query_rot, lse, query_rs,
        prompt_keys, prompt_values, key_rot, values, key_pre, w_query, w_key, w_value, hidden, rows_low, key_gain_row, query_gain_col,
        cos_rows, sin_rows, cos_t, sin_t, past, inside, valid_rows[:, None], gain_first[None, :], gain_second[None, :], sums, rows, n, R, 3,
    )
    suffix_mixed, suffix_grad = suffix_mixed.reshape(suffix, width), suffix_grad.reshape(suffix, width)
    g_down, g_gate, g_up, g_out, g_query, g_key, g_value = [g.astype(f32) for g in shards]
    flat = vec_sum.reshape(-1)

    def mine(first, size, part):
        return lax.dynamic_slice_in_dim(flat[first : first + size], rank * part, part)

    g_first = mine(0, width, attention_gain.size)
    g_second = mine(width, width, mlp_gain.size)
    g_query_gain = mine(2 * width, HEAD_SIZE, query_gain.size)
    g_key_gain = mine(2 * width + HEAD_SIZE, HEAD_SIZE, key_norm_gain.size)
    stat_sums = flat[2 * width + 2 * HEAD_SIZE : 2 * width + 2 * HEAD_SIZE + 4]
    token_norms = jnp.sqrt(stat_sums[:3] / (stat_sums[3] * width))
    return (
        mixed_low[:rows],
        suffix_mixed,
        prompt_grad,
        suffix_grad.astype(f32),
        g_first,
        g_query,
        g_key,
        g_value,
        g_query_gain,
        g_key_gain,
        g_out,
        g_second,
        g_gate,
        g_up,
        g_down,
        token_norms,
    )


def solution(mesh):
    placed = (
        P(("rep", "fsdp"), None),
        P(("rep", "fsdp"), None),
        P("rep", "fsdp"),
        P("rep", "fsdp"),
        P("fsdp"),
        P("fsdp", None),
        P("fsdp", None),
        P("fsdp", None),
        P("fsdp"),
        P("fsdp"),
        P("fsdp", None),
        P("fsdp"),
        P("fsdp", None),
        P("fsdp", None),
        P("fsdp", None),
        P(("rep", "fsdp"), None),
        P(("rep", "fsdp"), None),
    )
    return jax.shard_map(
        per_device,
        mesh=mesh,
        in_specs=placed,
        out_specs=(
            P(("rep", "fsdp"), None),
            P(("rep", "fsdp"), None),
            P(("rep", "fsdp"), None),
            P(("rep", "fsdp"), None),
            P("fsdp"),
            P("fsdp", None),
            P("fsdp", None),
            P("fsdp", None),
            P("fsdp"),
            P("fsdp"),
            P("fsdp", None),
            P("fsdp"),
            P("fsdp", None),
            P("fsdp", None),
            P("fsdp", None),
            P(),
        ),
        check_vma=False,
    )
```

time: 604 us -> 521 us (0.86)
  Pallas kernels: 552 us -> 477 us
    pallas_call x1, Pallas kernels: 272 us -> 229 us  [backward(): pl.pallas_call(partial(backward_kernel, n, R, group, UD, UF, UO), out_sha...]
    pallas_call x2 -> x1, Pallas kernels: 103 us -> 70.2 us  [gather(): pl.pallas_call(partial(gather_kernel, n, CB), out_shape=[shape((A, 2, 2)...]
where the time goes in v1:
time: 521 us; the launch traced here: 516 us
  Pallas kernels  477 us (92%)
  other arithmetic  22 us (4%)
  local copies, waits for them, and re-layouts  15.6 us (3%)
    pallas_call x1, Pallas kernels, backward(): pl.pallas_call(partial(backward_kernel, n, R, group, UD, UF, UO), out_sha...  229 us
    pallas_call x1, Pallas kernels, forward(): pl.pallas_call(partial(forward_kernel, n, group), out_shape=out_shape, in...  177 us
    pallas_call x1, Pallas kernels, gather(): pl.pallas_call(partial(gather_kernel, n, CB), out_shape=[shape((A, 2, 2)...  70.2 us

profile of v1, /device:TPU:0, one launch (start us, length us, event | category | flops | bytes accessed | tf_op | source)
XLA Modules:
  0.0 516.1 jit_solution(3518794347753980416)
XLA Ops:
  0.6 0.7 bitcast_convert_fusion.10
  1.3 0.7 bitcast_convert_fusion.8
  3.9 70.2 %gather.1 = (bf16[4,2,2,2,32,2048]{5,4,3,2,1,0:T(8,128)(2,1)}, bf16[4,2,2,2,32,1024]{5,4,3,2,1,0:T(8,128)(2,1)}, bf16[4,2,2,2,32,1024]{5,4,3,2,1,0:T(8,128)(2,1)...) custom-call(bf16[2,32,2048]{2,1,0:T(8,128)(2,1)} %bitcast.101, bf16[2,32,1024]{2,1,0:T(8,128)(2,1)} %bitcast.102, ...), custom_call_target="tpu_custom_call" | custom-call | tf_op jit(solution)/shard_map/gather/pallas_call | solution.py:195
  74.1 1.0 convert_reduce_fusion.1
  76.1 1.0 slice_reduce_fusion.2
  77.8 0.7 broadcast_in_dim.42.refs_12_.refs_27_
  78.5 1.0 fusion.1
  79.5 0.8 pad_maximum_fusion.refs_13_.refs_28_
  80.3 0.8 pad_maximum_fusion.1.refs_14_.refs_29_
  81.2 1.2 multiply_sine_fusion.1
  82.4 1.1 fusion.refs_17_.refs_32_
  83.6 0.9 and_select_fusion.refs_18_.refs_33_
  84.5 0.9 copy.35.refs_19_.refs_34_
  85.4 1.0 slice_reduce_fusion
  87.7 177.4 %forward.1 = (bf16[4,2,2,2,64,1024]{5,4,3,2,1,0:T(8,128)(2,1)}, bf16[4,2,2,2,32,3072]{5,4,3,2,1,0:T(8,128)(2,1)}, bf16[4,2,2,2,32,3072]{5,4,3,2,1,0:T(8,128)(2,1...) custom-call(s32[32]{0:T(128)} %get-tuple-element.101.refs_0_, ...), custom_call_target="tpu_custom_call" | custom-call | tf_op jit(solution)/shard_map/forward/pallas_call | solution.py:499
  265.1 2.3 fusion.7
  267.5 1.2 maximum_multiply_fusion.refs_2_
  268.7 229.3 %backward.1 = (bf16[2,96,1024]{2,1,0:T(8,128)(2,1)}, bf16[2,32,3072]{2,1,0:T(8,128)(2,1)}, bf16[2,32,3072]{2,1,0:T(8,128)(2,1)}, bf16[2,64,1024]{2,1,0:T(8,128)(...) custom-call(s32[32]{0:T(128)} %copy-done.10, ...), custom_call_target="tpu_custom_call" | custom-call | tf_op jit(solution)/shard_map/backward/pallas_call | solution.py:1165
  498.0 2.2 bitcast_convert_fusion
  500.2 0.7 slice_bitcast_fusion
  501.5 1.8 bitcast_convert_fusion.5
  503.3 0.7 bitcast_convert_fusion.7
  504.0 0.7 bitcast_convert_fusion.6
  504.8 0.8 fusion.8
  506.7 0.9 bitcast_convert_fusion.4
  508.1 1.0 bitcast_convert_fusion.3
  509.1 1.0 bitcast_convert_fusion.2
  510.0 1.0 bitcast_convert_fusion.1
  511.0 1.3 slice.70
  513.0 1.2 fusion.6
  514.2 0.8 copy.39
  515.0 1.0 copy.40
  (47 shorter events, 7.5 us)
Async XLA Ops:
  75.5 10.9 %copy-start.10 = (s32[32]{0:T(128)}, s32[32]{0:T(128)S(1)}, u32[]{:S(2)}) copy-start(s32[32]{0:T(128)S(1)} %convert_reduce_fusion.refs_0_) | copy-start | bytes 388
  265.1 2.3 copy-start.2
  265.1 2.3 copy-start.3
  497.9 5.3 %copy-start.9 = (bf16[2,32,1024]{2,1,0:T(8,128)(2,1)S(1)}, bf16[2,32,1024]{2,1,0:T(8,128)(2,1)}, u32[]{:S(2)}) copy-start(bf16[2,32,1024]{2,1,0:T(8,128)(2,1)} %get-tuple-element.88) | copy-start | bytes 393220
  498.0 6.1 %copy-start.8 = (bf16[2,32,1024]{2,1,0:T(8,128)(2,1)S(1)}, bf16[2,32,1024]{2,1,0:T(8,128)(2,1)}, u32[]{:S(2)}) copy-start(bf16[2,32,1024]{2,1,0:T(8,128)(2,1)} %get-tuple-element.89) | copy-start | bytes 393220
  498.0 8.7 %copy-start.7 = (bf16[2,64,1024]{2,1,0:T(8,128)(2,1)S(1)}, bf16[2,64,1024]{2,1,0:T(8,128)(2,1)}, u32[]{:S(2)}) copy-start(bf16[2,64,1024]{2,1,0:T(8,128)(2,1)} %get-tuple-element.90) | copy-start | bytes 786436
  498.0 10.2 %copy-start.6 = (bf16[2,32,3072]{2,1,0:T(8,128)(2,1)S(1)}, bf16[2,32,3072]{2,1,0:T(8,128)(2,1)}, u32[]{:S(2)}) copy-start(bf16[2,32,3072]{2,1,0:T(8,128)(2,1)} %get-tuple-element.91) | copy-start | bytes 1179652
  500.2 8.9 %copy-start.5 = (bf16[2,32,3072]{2,1,0:T(8,128)(2,1)S(1)}, bf16[2,32,3072]{2,1,0:T(8,128)(2,1)}, u32[]{:S(2)}) copy-start(bf16[2,32,3072]{2,1,0:T(8,128)(2,1)} %get-tuple-element.92) | copy-start | bytes 1179652
  503.3 6.8 %copy-start.4 = (bf16[2,96,1024]{2,1,0:T(8,128)(2,1)S(1)}, bf16[2,96,1024]{2,1,0:T(8,128)(2,1)}, u32[]{:S(2)}) copy-start(bf16[2,96,1024]{2,1,0:T(8,128)(2,1)} %get-tuple-element.93) | copy-start | bytes 1179652
  506.7 7.5 %copy-start.1 = (bf16[2,16,8,1024]{3,2,1,0:T(8,128)(2,1)S(1)}, bf16[2,16,8,1024]{3,2,1,0:T(8,128)(2,1)}, u32[]{:S(2)}) copy-start(bf16[2,16,8,1024]{3,2,1,0:T(8,128)(2,1)} %get-tuple-element.83) | copy-start | bytes 1572868
  508.1 6.8 %copy-start = (f32[256,1024]{1,0:T(8,128)S(1)}, f32[256,1024]{1,0:T(8,128)}, u32[]{:S(2)}) copy-start(f32[256,1024]{1,0:T(8,128)} %get-tuple-element.143) | copy-start | bytes 3145732

commit v2 on v1

--- a/solution.py
+++ b/solution.py
@@ -105,11 +105,20 @@
 
 class Ticker:
     def __init__(self, rings, arrived=lambda i: None):
-        self.rings, self.arrived, self.done = rings, arrived, [0] * 5
+        self.rings, self.arrived, self.done, self.noted = rings, arrived, [0] * 5, None
+
+    def run(self, f):
+        f() if self.noted is None else self.noted.append(f)
+
+    def note(self, f):
+        self.noted = []
+        f()
+        noted, self.noted = self.noted, None
+        return noted
 
     def begin(self, count):
-        for r in self.rings[self.done[0]:self.done[0] + count]:
-            r.begin()
+        for r in self.rings[self.done[0]:self.done[0] + max(count, 0)]:
+            self.run(r.begin)
             self.done[0] += 1
 
     def __call__(self, count=1, lag=1):
@@ -118,7 +127,7 @@
             for k in range(1, 5):
                 i = self.done[k]
                 if i < len(self.rings) and before[k - 1] - i >= lag:
-                    self.rings[i].step(k - 1)
+                    self.run(partial(self.rings[i].step, k - 1))
                     self.done[k] += 1
                     if k == 1:
                         self.begin(self.done[1] + ALONG - self.done[0])
@@ -127,7 +136,10 @@
 
     def until(self, count):
         while self.done[4] < count:
-            self()
+            before = list(self.done)
+            self(1, 2)
+            if before == self.done:
+                self()
 
 
 ALONG = 2
@@ -239,7 +251,7 @@
         blocks += [(sg, wg, pl.ds(q * GB, GB), g_buf.at[q % 2]), (su, wu, pl.ds(q * GB, GB), u_buf.at[q % 2])]
     blocks += [(sd, wd, pl.ds(q * OB, OB), d_buf.at[q]) for q in range(n_out)]
     m = len(blocks)
-    rings = [Ring(n, own, full, cols, (zs, zr, ss, sr, ls), i, i < X_FIRST) for i, (own, full, cols, _) in enumerate(blocks)]
+    rings = [Ring(n, own, full, cols, (zs, zr, ss, sr, ls), i, i % 2 == 0) for i, (own, full, cols, _) in enumerate(blocks)]
 
     def load(i):
         _, full, cols, buf = blocks[i]
@@ -250,7 +262,7 @@
     def arrived(i):
         q = (i - n_out) // 2 if n_out <= i < n_out + 2 * n_mlp else 0
         if q < used[0] + 2:
-            load(i).start()
+            tick.run(lambda: load(i).start())
         else:
             late.append(i)
 
@@ -258,7 +270,7 @@
         used[0] += 1
         now, late[:] = [i for i in late if (i - n_out) // 2 < used[0] + 2], [i for i in late if (i - n_out) // 2 >= used[0] + 2]
         for i in now:
-            load(i).start()
+            tick.run(lambda i=i: load(i).start())
 
     tick = Ticker(rings, arrived)
     S = ordered.shape[1]
@@ -401,19 +413,27 @@
     begin_all(cot_collect)
 
     stats[...] = jnp.zeros_like(stats)
-    for q in range(n_out):
-        tick.until(q + 1)
-        load(q).wait()
-
-        def out_tile(j, _):
-            cols = lane(q * (OB // 256) + j, 256)
-            w = o_buf[q, :, :, :, :, :, lane(j, 256)].reshape(-1, 256)
-            y = x[:, cols].astype(f32) + mm(attended[...], w, 1, 0)
-            resid[:, cols] = y
-            stats[1:2, :] += jnp.sum(valid[...] * y * y, axis=0, keepdims=True)
-            return 0
-
-        lax.fori_loop(0, OB // 256, out_tile, 0)
+
+    def at_block(q, noted):
+        for k, fs_ in enumerate(noted):
+            if fs_:
+                pl.when(q == k)(lambda fs_=fs_: [f() for f in fs_] and None)
+
+    def arrived_block(q, first, full, width, buf):
+        pltpu.make_async_copy(full.at[:, :, :, :, :, lane(q, width)], buf, lds.at[first]).wait()
+
+    before_out = [tick.note(partial(tick.until, k + 1)) for k in range(n_out)]
+
+    def out_block(q, _):
+        at_block(q, before_out)
+        arrived_block(q, q, wo, OB, o_buf.at[q])
+        cols = lane(q, OB)
+        y = x[:, cols].astype(f32) + mm(attended[...], o_buf[q].reshape(-1, OB), 1, 0)
+        resid[:, cols] = y
+        stats[1:2, :] += jnp.sum(valid[...] * y * y, axis=0, keepdims=True)
+        return 0
+
+    lax.fori_loop(0, n_out, out_block, 0)
 
     def norm_rows(j, _):
         h2[block(j), :] = norm(resid[block(j), :], gain2)
@@ -421,13 +441,20 @@
 
     lax.fori_loop(0, T // RB, norm_rows, 0)
     save(resid, h2)
-    saved = lambda q: [pltpu.make_async_copy(g_st.at[q % 2], gate.at[:, pl.ds(q * GB, GB)], gos.at[q % 2, 0]),
-                       pltpu.make_async_copy(u_st.at[q % 2], up.at[:, pl.ds(q * GB, GB)], gos.at[q % 2, 1])]
-    for q in range(n_mlp):
-        tick.until(n_out + 2 * q + 2)
-        load(n_out + 2 * q).wait()
-        load(n_out + 2 * q + 1).wait()
-        if q >= 2:
+    saved = lambda q: [pltpu.make_async_copy(g_st.at[q % 2], gate.at[:, lane(q, GB)], gos.at[q % 2, 0]),
+                       pltpu.make_async_copy(u_st.at[q % 2], up.at[:, lane(q, GB)], gos.at[q % 2, 1])]
+    before_mlp, after_mlp = [], []
+    for k in range(n_mlp):
+        before_mlp.append(tick.note(partial(tick.until, n_out + 2 * k + 2)))
+        after_mlp.append(tick.note(release))
+
+    def mlp_block(q, _):
+        at_block(q, before_mlp)
+        arrived_block(q, n_out + 2 * q, wg, GB, g_buf.at[q % 2])
+        arrived_block(q, n_out + 2 * q + 1, wu, GB, u_buf.at[q % 2])
+
+        @pl.when(q >= 2)
+        def _():
             for s in saved(q - 2):
                 s.wait()
 
@@ -440,26 +467,28 @@
             return 0
 
         lax.fori_loop(0, GB // 256, mlp_tile, 0)
-        release()
+        at_block(q, after_mlp)
         for s in saved(q):
             s.start()
+        return 0
+
+    lax.fori_loop(0, n_mlp, mlp_block, 0)
     save(act)
-    for q in range(n_out):
-        tick.until(n_out + 2 * n_mlp + q + 1)
-        load(n_out + 2 * n_mlp + q).wait()
-
-        def down_tile(j, _):
-            cols = lane(q * (OB // 256) + j, 256)
-            w = d_buf[q, :, :, :, :, :, lane(j, 256)].reshape(-1, 256)
-            y = resid[:, cols] + mm(act[...], w, 1, 0)
-            mixed[:, cols] = y.astype(bf16)
-            stats[0:1, :] += jnp.sum(valid[...] * y * y, axis=0, keepdims=True)
-            return 0
-
-        lax.fori_loop(0, OB // 256, down_tile, 0)
+    before_down = [tick.note(partial(tick.until, n_out + 2 * n_mlp + k + 1)) for k in range(n_out)]
+
+    def down_block(q, _):
+        at_block(q, before_down)
+        arrived_block(q, n_out + 2 * n_mlp + q, wd, OB, d_buf.at[q])
+        cols = lane(q, OB)
+        y = resid[:, cols] + mm(act[...], d_buf[q].reshape(-1, OB), 1, 0)
+        mixed[:, cols] = y.astype(bf16)
+        stats[0:1, :] += jnp.sum(valid[...] * y * y, axis=0, keepdims=True)
+        return 0
+
+    lax.fori_loop(0, n_out, down_block, 0)
     save(mixed)
     for q in range(max(0, n_mlp - 2), n_mlp):
-        for s in saved(q):
+        for s in saved(jnp.int32(q)):
             s.wait()
     wait_all(cot_collect)
     for q in across + sibling + onward:
@@ -470,8 +499,7 @@
         q.wait()
 
 
-X_FIRST = 4
-FORWARD_PLAN = (((1, (1,)), (3, (1,)), (5, (1,)), (7, (1,))), (1,), ((1, (1,)), (3, (1,)), (5, (1,)), (7, (1,))))
+FORWARD_PLAN = (tuple((j, (1, 2)) for j in (1, 3, 5, 7)), (2, 2), tuple((j, (1, 2)) for j in range(8)))
 
 
 def forward(index, prompt, staged, cot, wk, wv, wq, shards, k_gain, q_gain, cos_r, sin_r, cos, sin, past, inside, valid, gain1, gain2, n, cid):
@@ -492,7 +520,7 @@
     out_shape = [shape((A, 2, 2) + s.shape, bf16) for s in halves] + [shape((S, n) + staged.shape[2:], bf16), shape((T, FW), bf16), shape((T, FW), bf16)]
     out_shape += [shape(*k) for k in kept] + [small, small, shape((8, 256), f32)]
     vm, hbm, sm = pl.BlockSpec(memory_space=pltpu.VMEM), pl.BlockSpec(memory_space=pl.ANY), pl.BlockSpec(memory_space=pltpu.SMEM)
-    OB, GB = 512, 768
+    OB, GB = 256, 512
     n_out, n_mlp = W // OB, FW // GB
     m = 2 * n_out + 2 * n_mlp
     buf = lambda i, k, w: V((k, A, 2, 2) + halves[i].shape[:2] + (w,), bf16)
@@ -704,19 +732,38 @@
 
     done = [0] * 6
 
-    def e1():
-        units[done[0]].step(1)
-        done[0] += 1
+    noted = [None]
+
+    def run(f):
+        f() if noted[0] is None else noted[0].append(f)
+
+    def note(f):
+        noted[0] = []
+        f()
+        fs_, noted[0] = noted[0], None
+        return fs_
+
+    def at_block(q, lists):
+        for k, fs_ in enumerate(lists):
+            if fs_:
+                pl.when(q == k)(lambda fs_=fs_: [f() for f in fs_] and None)
+
+    def e1(upto=None):
+        while done[0] < (done[0] + 1 if upto is None else upto):
+            run(partial(units[done[0]].step, 1))
+            done[0] += 1
+            if upto is None:
+                break
 
     def tick(count=1, lag=2):
         for _ in range(count):
             before = list(done)
             if done[1] < before[0]:
-                units[done[1]].go(2)
+                run(partial(units[done[1]].go, 2))
                 done[1] += 1
             for k in range(2, 6):
                 if before[k - 1] - done[k] >= lag:
-                    units[done[k]].step(k)
+                    run(partial(units[done[k]].step, k))
                     done[k] += 1
 
     n_down, n_ff, n_out = W // UD, FW // UF, W // UO
@@ -779,20 +826,34 @@
         got = [fetch(h2, h2_v), fetch(dm, dm_v)]
 
         def fetch_ff(q):
-            cols, s = pl.ds(q * UF, UF), q % 2
-            return [fetch(wd.at[cols], wd_c.at[s]), fetch(gate.at[:, cols], gate_c.at[s]), fetch(up.at[:, cols], up_c.at[s]),
-                    fetch(wg.at[:, cols], wg_c.at[s]), fetch(wu.at[:, cols], wu_c.at[s])]
-
-        ff = [fetch_ff(0)]
+            cols, s = lane(q, UF), q % 2
+            moves = ((wd.at[cols], wd_c), (gate.at[:, cols], gate_c), (up.at[:, cols], up_c), (wg.at[:, cols], wg_c), (wu.at[:, cols], wu_c))
+            return [pltpu.make_async_copy(src, dst.at[s], hs.at[s, k]) for k, (src, dst) in enumerate(moves)]
+
+        for f in fetch_ff(jnp.int32(0)):
+            f.start()
         got_resid = fetch(resid, dres)
         for f in got:
             f.wait()
         h2_t[...] = h2_v[...].T
+        dhid[...] = jnp.zeros_like(dhid)
+        free_slot, begun, after = ([], []), ([], []), []
         for q in range(n_ff):
+            for k in range(2):
+                free_slot[k].append(note(lambda: e1(len(units) - 1)))
+                unit(1, 2 * q + k, g_ff.at[(2 * q + k) % 4], 1 + k, pl.ds(q * UF, UF))
+                begun[k].append([units[-1].begin])
+            after.append(note(partial(tick, *PLAN[1 + q])))
+
+        def ff_block(q, _):
             s = q % 2
-            if q + 1 < n_ff:
-                ff.append(fetch_ff(q + 1))
-            for f in ff[q]:
+
+            @pl.when(q + 1 < n_ff)
+            def _():
+                for f in fetch_ff(q + 1):
+                    f.start()
+
+            for f in fetch_ff(q):
                 f.wait()
 
             def act_tile(j, _):
@@ -806,8 +867,7 @@
 
             lax.fori_loop(0, UF // 256, act_tile, 0)
             for k, d in enumerate((dg_c, du_c)):
-                while done[0] < len(units) - 1:
-                    e1()
+                at_block(q, free_slot[k])
 
                 def ff_tile(j, _):
                     y = mm(h2_t[...], d[:, lane(j, 256)], 1, 0).astype(bf16)
@@ -815,16 +875,18 @@
                     return 0
 
                 lax.fori_loop(0, UF // 256, ff_tile, 0)
-                unit(1, 2 * q + k, g_ff.at[(2 * q + k) % 4], 1 + k, pl.ds(q * UF, UF)).begin()
+                at_block(q, begun[k])
 
             def hid_tile(j, _):
                 cols = lane(j, 256)
-                y = mm(dg_c[...], wg_c[s, cols, :], 1, 1) + mm(du_c[...], wu_c[s, cols, :], 1, 1)
-                dhid[:, cols] = y if q == 0 else dhid[:, cols] + y
+                dhid[:, cols] += mm(dg_c[...], wg_c[s, cols, :], 1, 1) + mm(du_c[...], wu_c[s, cols, :], 1, 1)
                 return 0
 
             lax.fori_loop(0, W // 256, hid_tile, 0)
-            tick(*PLAN[1 + q])
+            at_block(q, after)
+            return 0
+
+        lax.fori_loop(0, n_ff, ff_block, 0)
         while done[0] < len(units):
             e1()
         got_resid.wait()
@@ -986,21 +1048,27 @@
         pl.semaphore_signal(free, inc=1, device_id=(rep, rank(a, b, 1 - c)), device_id_type=MESH)
         pl.semaphore_wait(free, 1)
 
-        def grad_unit(d, out, cols):
-            k = count[0]
-            count[0] += 1
-            start = cols * UF
-
-            def tile(j, _):
-                y = mm(hid_t[...], d[:, pl.ds(pl.multiple_of(start + j * 256, 256), 256)], 1, 0).astype(bf16)
-                g_qkv[k % 4, :, :, :, :, :, lane(j, 256)] = y.reshape(g_qkv.shape[1:6] + (256,))
+        def grad_units(d, out, width):
+            base, begun = count[0], []
+            for u in range(width // UF):
+                unit(1, 2 * n_ff + base + u, g_qkv.at[(base + u) % 4], out, pl.ds(u * UF, UF), base + u)
+                begun.append([units[-1].begin])
+            count[0] += width // UF
+
+            def tile(t, _):
+                u, j = t // (UF // 256), t % (UF // 256)
+                y = mm(hid_t[...], d[:, lane(t, 256)], 1, 0).astype(bf16)
+                g_qkv[(base + u) % 4, :, :, :, :, :, lane(j, 256)] = y.reshape(g_qkv.shape[1:6] + (256,))
+
+                @pl.when(j == UF // 256 - 1)
+                def _():
+                    at_block(u, begun)
+
                 return 0
 
-            lax.fori_loop(0, UF // 256, tile, 0)
-            unit(1, 2 * n_ff + k, g_qkv.at[k % 4], out, pl.ds(start, UF), k).begin()
-
-        for u in range(QW // UF):
-            grad_unit(dq, 4, u)
+            lax.fori_loop(0, width // 256, tile, 0)
+
+        grad_units(dq, 4, QW)
         for u in range(QW // UF):
             e1()
         tick(*PLAN[16])
@@ -1066,12 +1134,10 @@
             return 0
 
         lax.fori_loop(0, rows // RB, own_keys, 0)
-        for u in range(KW // UF):
-            grad_unit(dvl, 6, u)
+        grad_units(dvl, 6, KW)
         gk = lax.fori_loop(0, KEY_VALUE_HEADS, partial(key_head, theirs), gk)
         vec[2 * W // 128 + 1:2 * W // 128 + 2, :] = gk
-        for u in range(KW // UF):
-            grad_unit(dkl, 5, u)
+        grad_units(dkl, 5, KW)
         while done[0] < len(units):
             e1()
         tick(*PLAN[18])

time: 521 us -> 500 us (0.960)
  Pallas kernels: 477 us -> 456 us
    pallas_call x1, Pallas kernels: 177 us -> 157 us  [forward(): pl.pallas_call(partial(forward_kernel, n, group), out_shape=out_shape, in...]
where the time goes in v2:
time: 500 us; the launch traced here: 496 us
  Pallas kernels  456 us (91%)
  other arithmetic  22 us (4%)
  local copies, waits for them, and re-layouts  15.6 us (3%)
    pallas_call x1, Pallas kernels, backward(): pl.pallas_call(partial(backward_kernel, n, R, group, UD, UF, UO), out_sha...  228 us
    pallas_call x1, Pallas kernels, forward(): pl.pallas_call(partial(forward_kernel, n, group), out_shape=out_shape, in...  157 us
    pallas_call x1, Pallas kernels, gather(): pl.pallas_call(partial(gather_kernel, n, CB), out_shape=[shape((A, 2, 2)...  70.6 us

profile of v2, /device:TPU:0, one launch (start us, length us, event | category | flops | bytes accessed | tf_op | source)
XLA Modules:
  0.0 495.5 jit_solution(5977141352950474735)
XLA Ops:
  0.6 0.7 bitcast_convert_fusion.10
  1.3 0.7 bitcast_convert_fusion.8
  3.9 70.6 %gather.1 = (bf16[4,2,2,2,32,2048]{5,4,3,2,1,0:T(8,128)(2,1)}, bf16[4,2,2,2,32,1024]{5,4,3,2,1,0:T(8,128)(2,1)}, bf16[4,2,2,2,32,1024]{5,4,3,2,1,0:T(8,128)(2,1)...) custom-call(bf16[2,32,2048]{2,1,0:T(8,128)(2,1)} %bitcast.101, bf16[2,32,1024]{2,1,0:T(8,128)(2,1)} %bitcast.102, ...), custom_call_target="tpu_custom_call" | custom-call | tf_op jit(solution)/shard_map/gather/pallas_call | solution.py:207
  74.6 1.0 convert_reduce_fusion.1
  76.6 1.0 slice_reduce_fusion.2
  78.2 0.7 broadcast_in_dim.42.refs_12_.refs_27_
  79.0 1.0 fusion.1
  80.0 0.8 pad_maximum_fusion.refs_13_.refs_28_
  80.8 0.8 pad_maximum_fusion.1.refs_14_.refs_29_
  81.7 1.2 multiply_sine_fusion.1
  82.9 1.1 fusion.refs_17_.refs_32_
  84.1 0.9 and_select_fusion.refs_18_.refs_33_
  85.0 0.9 copy.35.refs_19_.refs_34_
  85.9 1.0 slice_reduce_fusion
  88.2 157.3 %forward.1 = (bf16[4,2,2,2,64,1024]{5,4,3,2,1,0:T(8,128)(2,1)}, bf16[4,2,2,2,32,3072]{5,4,3,2,1,0:T(8,128)(2,1)}, bf16[4,2,2,2,32,3072]{5,4,3,2,1,0:T(8,128)(2,1...) custom-call(s32[32]{0:T(128)} %get-tuple-element.101.refs_0_, ...), custom_call_target="tpu_custom_call" | custom-call | tf_op jit(solution)/shard_map/forward/pallas_call | solution.py:527
  245.5 2.3 fusion.7
  247.8 1.2 maximum_multiply_fusion.refs_2_
  249.0 228.1 %backward.1 = (bf16[2,96,1024]{2,1,0:T(8,128)(2,1)}, bf16[2,32,3072]{2,1,0:T(8,128)(2,1)}, bf16[2,32,3072]{2,1,0:T(8,128)(2,1)}, bf16[2,64,1024]{2,1,0:T(8,128)(...) custom-call(s32[32]{0:T(128)} %copy-done.10, ...), custom_call_target="tpu_custom_call" | custom-call | tf_op jit(solution)/shard_map/backward/pallas_call | solution.py:1231
  477.1 2.2 bitcast_convert_fusion
  479.3 0.7 slice_bitcast_fusion
  480.6 1.8 bitcast_convert_fusion.5
  482.4 0.7 bitcast_convert_fusion.7
  483.2 0.7 bitcast_convert_fusion.6
  483.9 0.8 fusion.8
  485.8 0.9 bitcast_convert_fusion.4
  487.3 1.0 bitcast_convert_fusion.3
  488.2 1.0 bitcast_convert_fusion.2
  489.2 1.0 bitcast_convert_fusion.1
  490.2 1.3 slice.70
  492.1 1.2 fusion.6
  493.3 0.8 copy.39
  494.1 1.0 copy.40
  (47 shorter events, 7.5 us)
Async XLA Ops:
  75.9 10.9 %copy-start.10 = (s32[32]{0:T(128)}, s32[32]{0:T(128)S(1)}, u32[]{:S(2)}) copy-start(s32[32]{0:T(128)S(1)} %convert_reduce_fusion.refs_0_) | copy-start | bytes 388
  245.5 2.3 copy-start.2
  245.5 2.3 copy-start.3
  477.1 5.3 %copy-start.9 = (bf16[2,32,1024]{2,1,0:T(8,128)(2,1)S(1)}, bf16[2,32,1024]{2,1,0:T(8,128)(2,1)}, u32[]{:S(2)}) copy-start(bf16[2,32,1024]{2,1,0:T(8,128)(2,1)} %get-tuple-element.88) | copy-start | bytes 393220
  477.1 6.1 %copy-start.8 = (bf16[2,32,1024]{2,1,0:T(8,128)(2,1)S(1)}, bf16[2,32,1024]{2,1,0:T(8,128)(2,1)}, u32[]{:S(2)}) copy-start(bf16[2,32,1024]{2,1,0:T(8,128)(2,1)} %get-tuple-element.89) | copy-start | bytes 393220
  477.1 8.7 %copy-start.7 = (bf16[2,64,1024]{2,1,0:T(8,128)(2,1)S(1)}, bf16[2,64,1024]{2,1,0:T(8,128)(2,1)}, u32[]{:S(2)}) copy-start(bf16[2,64,1024]{2,1,0:T(8,128)(2,1)} %get-tuple-element.90) | copy-start | bytes 786436
  477.1 10.2 %copy-start.6 = (bf16[2,32,3072]{2,1,0:T(8,128)(2,1)S(1)}, bf16[2,32,3072]{2,1,0:T(8,128)(2,1)}, u32[]{:S(2)}) copy-start(bf16[2,32,3072]{2,1,0:T(8,128)(2,1)} %get-tuple-element.91) | copy-start | bytes 1179652
  479.3 8.9 %copy-start.5 = (bf16[2,32,3072]{2,1,0:T(8,128)(2,1)S(1)}, bf16[2,32,3072]{2,1,0:T(8,128)(2,1)}, u32[]{:S(2)}) copy-start(bf16[2,32,3072]{2,1,0:T(8,128)(2,1)} %get-tuple-element.92) | copy-start | bytes 1179652
  482.4 6.8 %copy-start.4 = (bf16[2,96,1024]{2,1,0:T(8,128)(2,1)S(1)}, bf16[2,96,1024]{2,1,0:T(8,128)(2,1)}, u32[]{:S(2)}) copy-start(bf16[2,96,1024]{2,1,0:T(8,128)(2,1)} %get-tuple-element.93) | copy-start | bytes 1179652
  485.8 7.5 %copy-start.1 = (bf16[2,16,8,1024]{3,2,1,0:T(8,128)(2,1)S(1)}, bf16[2,16,8,1024]{3,2,1,0:T(8,128)(2,1)}, u32[]{:S(2)}) copy-start(bf16[2,16,8,1024]{3,2,1,0:T(8,128)(2,1)} %get-tuple-element.83) | copy-start | bytes 1572868
  487.3 6.8 %copy-start = (f32[256,1024]{1,0:T(8,128)S(1)}, f32[256,1024]{1,0:T(8,128)}, u32[]{:S(2)}) copy-start(f32[256,1024]{1,0:T(8,128)} %get-tuple-element.143) | copy-start | bytes 3145732

commit v3 on v2

--- a/solution.py
+++ b/solution.py
@@ -544,7 +544,7 @@
     return res
 
 
-PLAN = ((3, 5), (1, 3), (2, 8), (4, 5), (5, 8), (0, 1), (6, 8), (2, 8), (3, 3), (1, 5), (2, 8), (1, 3), (3, 8), (3, 1), (0, 6), (6, 2), (2, 4), (5, 4), (1, 2), (5, 3))
+PLAN = ((3, 8), (1, 8), (2, 3), (2, 3), (5, 5), (2, 4), (4, 5), (1, 3), (6, 8), (1, 1), (2, 8), (2, 3), (6, 8), (3, 1), (0, 2), (3, 1), (2, 6), (1, 1), (3, 2), (6, 6))
 
 
 class Fold:

time: 500 us -> 489 us (0.978)
  Pallas kernels: 456 us -> 445 us
    pallas_call x1, Pallas kernels: 228 us -> 217 us  [backward(): pl.pallas_call(partial(backward_kernel, n, R, group, UD, UF, UO), out_sha...]
where the time goes in v3:
time: 489 us; the launch traced here: 485 us
  Pallas kernels  445 us (91%)
  other arithmetic  22 us (4%)
  local copies, waits for them, and re-layouts  15.6 us (3%)
    pallas_call x1, Pallas kernels, backward(): pl.pallas_call(partial(backward_kernel, n, R, group, UD, UF, UO), out_sha...  217 us
    pallas_call x1, Pallas kernels, forward(): pl.pallas_call(partial(forward_kernel, n, group), out_shape=out_shape, in...  157 us
    pallas_call x1, Pallas kernels, gather(): pl.pallas_call(partial(gather_kernel, n, CB), out_shape=[shape((A, 2, 2)...  70.6 us

profile of v3, /device:TPU:0, one launch (start us, length us, event | category | flops | bytes accessed | tf_op | source)
XLA Modules:
  0.0 484.6 jit_solution(16219960704083616139)
XLA Ops:
  0.6 0.7 bitcast_convert_fusion.10
  1.3 0.7 bitcast_convert_fusion.8
  3.9 70.6 %gather.1 = (bf16[4,2,2,2,32,2048]{5,4,3,2,1,0:T(8,128)(2,1)}, bf16[4,2,2,2,32,1024]{5,4,3,2,1,0:T(8,128)(2,1)}, bf16[4,2,2,2,32,1024]{5,4,3,2,1,0:T(8,128)(2,1)...) custom-call(bf16[2,32,2048]{2,1,0:T(8,128)(2,1)} %bitcast.101, bf16[2,32,1024]{2,1,0:T(8,128)(2,1)} %bitcast.102, ...), custom_call_target="tpu_custom_call" | custom-call | tf_op jit(solution)/shard_map/gather/pallas_call | solution.py:207
  74.6 1.0 convert_reduce_fusion.1
  76.6 1.0 slice_reduce_fusion.2
  78.2 0.7 broadcast_in_dim.42.refs_12_.refs_27_
  79.0 1.0 fusion.1
  80.0 0.8 pad_maximum_fusion.refs_13_.refs_28_
  80.8 0.8 pad_maximum_fusion.1.refs_14_.refs_29_
  81.7 1.2 multiply_sine_fusion.1
  82.9 1.1 fusion.refs_17_.refs_32_
  84.1 0.9 and_select_fusion.refs_18_.refs_33_
  85.0 0.9 copy.35.refs_19_.refs_34_
  85.9 1.0 slice_reduce_fusion
  88.2 157.3 %forward.1 = (bf16[4,2,2,2,64,1024]{5,4,3,2,1,0:T(8,128)(2,1)}, bf16[4,2,2,2,32,3072]{5,4,3,2,1,0:T(8,128)(2,1)}, bf16[4,2,2,2,32,3072]{5,4,3,2,1,0:T(8,128)(2,1...) custom-call(s32[32]{0:T(128)} %get-tuple-element.101.refs_0_, ...), custom_call_target="tpu_custom_call" | custom-call | tf_op jit(solution)/shard_map/forward/pallas_call | solution.py:527
  245.5 2.3 fusion.7
  247.8 1.2 maximum_multiply_fusion.refs_2_
  249.0 217.1 %backward.1 = (bf16[2,96,1024]{2,1,0:T(8,128)(2,1)}, bf16[2,32,3072]{2,1,0:T(8,128)(2,1)}, bf16[2,32,3072]{2,1,0:T(8,128)(2,1)}, bf16[2,64,1024]{2,1,0:T(8,128)(...) custom-call(s32[32]{0:T(128)} %copy-done.10, ...), custom_call_target="tpu_custom_call" | custom-call | tf_op jit(solution)/shard_map/backward/pallas_call | solution.py:1231
  466.2 2.2 bitcast_convert_fusion
  468.4 0.7 slice_bitcast_fusion
  469.7 1.8 bitcast_convert_fusion.5
  471.5 0.7 bitcast_convert_fusion.7
  472.2 0.7 bitcast_convert_fusion.6
  472.9 0.8 fusion.8
  474.9 0.9 bitcast_convert_fusion.4
  476.3 1.0 bitcast_convert_fusion.3
  477.3 1.0 bitcast_convert_fusion.2
  478.2 1.0 bitcast_convert_fusion.1
  479.2 1.3 slice.70
  481.1 1.2 fusion.6
  482.4 0.8 copy.39
  483.1 1.0 copy.40
  (47 shorter events, 7.5 us)
Async XLA Ops:
  75.9 10.9 %copy-start.10 = (s32[32]{0:T(128)}, s32[32]{0:T(128)S(1)}, u32[]{:S(2)}) copy-start(s32[32]{0:T(128)S(1)} %convert_reduce_fusion.refs_0_) | copy-start | bytes 388
  245.5 2.3 copy-start.2
  245.5 2.3 copy-start.3
  466.1 5.3 %copy-start.9 = (bf16[2,32,1024]{2,1,0:T(8,128)(2,1)S(1)}, bf16[2,32,1024]{2,1,0:T(8,128)(2,1)}, u32[]{:S(2)}) copy-start(bf16[2,32,1024]{2,1,0:T(8,128)(2,1)} %get-tuple-element.88) | copy-start | bytes 393220
  466.1 6.1 %copy-start.8 = (bf16[2,32,1024]{2,1,0:T(8,128)(2,1)S(1)}, bf16[2,32,1024]{2,1,0:T(8,128)(2,1)}, u32[]{:S(2)}) copy-start(bf16[2,32,1024]{2,1,0:T(8,128)(2,1)} %get-tuple-element.89) | copy-start | bytes 393220
  466.1 8.7 %copy-start.7 = (bf16[2,64,1024]{2,1,0:T(8,128)(2,1)S(1)}, bf16[2,64,1024]{2,1,0:T(8,128)(2,1)}, u32[]{:S(2)}) copy-start(bf16[2,64,1024]{2,1,0:T(8,128)(2,1)} %get-tuple-element.90) | copy-start | bytes 786436
  466.2 10.2 %copy-start.6 = (bf16[2,32,3072]{2,1,0:T(8,128)(2,1)S(1)}, bf16[2,32,3072]{2,1,0:T(8,128)(2,1)}, u32[]{:S(2)}) copy-start(bf16[2,32,3072]{2,1,0:T(8,128)(2,1)} %get-tuple-element.91) | copy-start | bytes 1179652
  468.4 8.9 %copy-start.5 = (bf16[2,32,3072]{2,1,0:T(8,128)(2,1)S(1)}, bf16[2,32,3072]{2,1,0:T(8,128)(2,1)}, u32[]{:S(2)}) copy-start(bf16[2,32,3072]{2,1,0:T(8,128)(2,1)} %get-tuple-element.92) | copy-start | bytes 1179652
  471.5 6.8 %copy-start.4 = (bf16[2,96,1024]{2,1,0:T(8,128)(2,1)S(1)}, bf16[2,96,1024]{2,1,0:T(8,128)(2,1)}, u32[]{:S(2)}) copy-start(bf16[2,96,1024]{2,1,0:T(8,128)(2,1)} %get-tuple-element.93) | copy-start | bytes 1179652
  474.9 7.5 %copy-start.1 = (bf16[2,16,8,1024]{3,2,1,0:T(8,128)(2,1)S(1)}, bf16[2,16,8,1024]{3,2,1,0:T(8,128)(2,1)}, u32[]{:S(2)}) copy-start(bf16[2,16,8,1024]{3,2,1,0:T(8,128)(2,1)} %get-tuple-element.83) | copy-start | bytes 1572868
  476.3 6.8 %copy-start = (f32[256,1024]{1,0:T(8,128)S(1)}, f32[256,1024]{1,0:T(8,128)}, u32[]{:S(2)}) copy-start(f32[256,1024]{1,0:T(8,128)} %get-tuple-element.143) | copy-start | bytes 3145732

commit v4 on v3

--- a/solution.py
+++ b/solution.py
@@ -773,13 +773,14 @@
 
     def down(act_c, act_t, g_down, dm_v):
         got = fetch(dm, dm_v)
-        pieces = [fetch(act.at[:, pl.ds(0, AT)], act_c.at[0])]
+        piece = lambda i: pltpu.make_async_copy(act.at[:, lane(i, AT)], act_c.at[i % 2], hs.at[i % 2, 0])
+        piece(jnp.int32(0)).start()
         begin_all(mixed_spread)
         got.wait()
-        for i in range(A):
-            if i + 1 < A:
-                pieces.append(fetch(act.at[:, pl.ds((i + 1) * AT, AT)], act_c.at[(i + 1) % 2]))
-            pieces[i].wait()
+
+        def down_part(i, _):
+            pl.when(i + 1 < A)(lambda: piece(i + 1).start())
+            piece(i).wait()
             act_t[...] = act_c[i % 2].T
 
             def down_tile(j, _):
@@ -787,7 +788,9 @@
                 g_down[j, i] = y.reshape(g_down.shape[2:])
                 return 0
 
-            lax.fori_loop(0, n_down, down_tile, 0)
+            return lax.fori_loop(0, n_down, down_tile, 0)
+
+        lax.fori_loop(0, A, down_part, 0)
         for u in range(n_down):
             unit(0, u, g_down.at[u], 0, pl.ds(u * UD, UD)).begin()
         for u in range(n_down):
@@ -903,11 +906,12 @@
             vec[W // 128 + k:W // 128 + k + 1, :] = g2[:, k * 128:(k + 1) * 128]
 
     def out_grad(drl, att_c, att_t, g_out):
-        pieces = [fetch(attended.at[:, pl.ds(0, QT)], att_c.at[0])]
-        for i in range(A):
-            if i + 1 < A:
-                pieces.append(fetch(attended.at[:, pl.ds((i + 1) * QT, QT)], att_c.at[(i + 1) % 2]))
-            pieces[i].wait()
+        piece = lambda i: pltpu.make_async_copy(attended.at[:, lane(i, QT)], att_c.at[i % 2], hs.at[i % 2, 0])
+        piece(jnp.int32(0)).start()
+
+        def out_part(i, _):
+            pl.when(i + 1 < A)(lambda: piece(i + 1).start())
+            piece(i).wait()
             att_t[...] = att_c[i % 2].T
 
             def out_tile(j, _):
@@ -915,7 +919,9 @@
                 g_out[j, i] = y.reshape(g_out.shape[2:])
                 return 0
 
-            lax.fori_loop(0, n_out, out_tile, 0)
+            return lax.fori_loop(0, n_out, out_tile, 0)
+
+        lax.fori_loop(0, A, out_part, 0)
         for u in range(n_out):
             unit(2, u, g_out.at[u], 3, pl.ds(u * UO, UO)).begin()
         while done[0] < len(units):

time: 489 us -> 485 us (level)
  no operation moved by 1% of the time
where the time goes in v4:
time: 485 us; the launch traced here: 484 us
  Pallas kernels  445 us (92%)
  other arithmetic  22 us (5%)
  local copies, waits for them, and re-layouts  15.6 us (3%)
    pallas_call x1, Pallas kernels, backward(): pl.pallas_call(partial(backward_kernel, n, R, group, UD, UF, UO), out_sha...  217 us
    pallas_call x1, Pallas kernels, forward(): pl.pallas_call(partial(forward_kernel, n, group), out_shape=out_shape, in...  157 us
    pallas_call x1, Pallas kernels, gather(): pl.pallas_call(partial(gather_kernel, n, CB), out_shape=[shape((A, 2, 2)...  70.6 us

profile of v4, /device:TPU:0, one launch (start us, length us, event | category | flops | bytes accessed | tf_op | source)
XLA Modules:
  0.0 484.1 jit_solution(17405063877434571991)
XLA Ops:
  0.6 0.7 bitcast_convert_fusion.10
  1.3 0.7 bitcast_convert_fusion.8
  3.9 70.6 %gather.1 = (bf16[4,2,2,2,32,2048]{5,4,3,2,1,0:T(8,128)(2,1)}, bf16[4,2,2,2,32,1024]{5,4,3,2,1,0:T(8,128)(2,1)}, bf16[4,2,2,2,32,1024]{5,4,3,2,1,0:T(8,128)(2,1)...) custom-call(bf16[2,32,2048]{2,1,0:T(8,128)(2,1)} %bitcast.101, bf16[2,32,1024]{2,1,0:T(8,128)(2,1)} %bitcast.102, ...), custom_call_target="tpu_custom_call" | custom-call | tf_op jit(solution)/shard_map/gather/pallas_call | solution.py:207
  74.6 1.0 convert_reduce_fusion.1
  76.6 1.0 slice_reduce_fusion.2
  78.2 0.7 broadcast_in_dim.42.refs_12_.refs_27_
  79.0 1.0 fusion.1
  80.0 0.8 pad_maximum_fusion.refs_13_.refs_28_
  80.8 0.8 pad_maximum_fusion.1.refs_14_.refs_29_
  81.7 1.2 multiply_sine_fusion.1
  82.9 1.1 fusion.refs_17_.refs_32_
  84.1 0.9 and_select_fusion.refs_18_.refs_33_
  85.0 0.9 copy.35.refs_19_.refs_34_
  85.9 1.0 slice_reduce_fusion
  88.2 157.1 %forward.1 = (bf16[4,2,2,2,64,1024]{5,4,3,2,1,0:T(8,128)(2,1)}, bf16[4,2,2,2,32,3072]{5,4,3,2,1,0:T(8,128)(2,1)}, bf16[4,2,2,2,32,3072]{5,4,3,2,1,0:T(8,128)(2,1...) custom-call(s32[32]{0:T(128)} %get-tuple-element.101.refs_0_, ...), custom_call_target="tpu_custom_call" | custom-call | tf_op jit(solution)/shard_map/forward/pallas_call | solution.py:527
  245.3 2.3 fusion.7
  247.6 1.2 maximum_multiply_fusion.refs_2_
  248.8 217.2 %backward.1 = (bf16[2,96,1024]{2,1,0:T(8,128)(2,1)}, bf16[2,32,3072]{2,1,0:T(8,128)(2,1)}, bf16[2,32,3072]{2,1,0:T(8,128)(2,1)}, bf16[2,64,1024]{2,1,0:T(8,128)(...) custom-call(s32[32]{0:T(128)} %copy-done.10, ...), custom_call_target="tpu_custom_call" | custom-call | tf_op jit(solution)/shard_map/backward/pallas_call | solution.py:1237
  466.1 2.2 bitcast_convert_fusion
  468.3 0.7 slice_bitcast_fusion
  469.6 1.8 bitcast_convert_fusion.5
  471.4 0.7 bitcast_convert_fusion.7
  472.1 0.7 bitcast_convert_fusion.6
  472.9 0.8 fusion.8
  474.8 0.9 bitcast_convert_fusion.4
  476.2 1.0 bitcast_convert_fusion.3
  477.2 1.0 bitcast_convert_fusion.2
  478.2 1.0 bitcast_convert_fusion.1
  479.2 1.3 slice.70
  481.1 1.2 fusion.6
  482.3 0.8 copy.39
  483.1 1.0 copy.40
  (47 shorter events, 7.5 us)
Async XLA Ops:
  75.9 10.9 %copy-start.10 = (s32[32]{0:T(128)}, s32[32]{0:T(128)S(1)}, u32[]{:S(2)}) copy-start(s32[32]{0:T(128)S(1)} %convert_reduce_fusion.refs_0_) | copy-start | bytes 388
  245.2 2.3 copy-start.2
  245.3 2.3 copy-start.3
  466.1 5.3 %copy-start.9 = (bf16[2,32,1024]{2,1,0:T(8,128)(2,1)S(1)}, bf16[2,32,1024]{2,1,0:T(8,128)(2,1)}, u32[]{:S(2)}) copy-start(bf16[2,32,1024]{2,1,0:T(8,128)(2,1)} %get-tuple-element.88) | copy-start | bytes 393220
  466.1 6.1 %copy-start.8 = (bf16[2,32,1024]{2,1,0:T(8,128)(2,1)S(1)}, bf16[2,32,1024]{2,1,0:T(8,128)(2,1)}, u32[]{:S(2)}) copy-start(bf16[2,32,1024]{2,1,0:T(8,128)(2,1)} %get-tuple-element.89) | copy-start | bytes 393220
  466.1 8.7 %copy-start.7 = (bf16[2,64,1024]{2,1,0:T(8,128)(2,1)S(1)}, bf16[2,64,1024]{2,1,0:T(8,128)(2,1)}, u32[]{:S(2)}) copy-start(bf16[2,64,1024]{2,1,0:T(8,128)(2,1)} %get-tuple-element.90) | copy-start | bytes 786436
  466.1 10.2 %copy-start.6 = (bf16[2,32,3072]{2,1,0:T(8,128)(2,1)S(1)}, bf16[2,32,3072]{2,1,0:T(8,128)(2,1)}, u32[]{:S(2)}) copy-start(bf16[2,32,3072]{2,1,0:T(8,128)(2,1)} %get-tuple-element.91) | copy-start | bytes 1179652
  468.3 8.9 %copy-start.5 = (bf16[2,32,3072]{2,1,0:T(8,128)(2,1)S(1)}, bf16[2,32,3072]{2,1,0:T(8,128)(2,1)}, u32[]{:S(2)}) copy-start(bf16[2,32,3072]{2,1,0:T(8,128)(2,1)} %get-tuple-element.92) | copy-start | bytes 1179652
  471.4 6.8 %copy-start.4 = (bf16[2,96,1024]{2,1,0:T(8,128)(2,1)S(1)}, bf16[2,96,1024]{2,1,0:T(8,128)(2,1)}, u32[]{:S(2)}) copy-start(bf16[2,96,1024]{2,1,0:T(8,128)(2,1)} %get-tuple-element.93) | copy-start | bytes 1179652
  474.8 7.5 %copy-start.1 = (bf16[2,16,8,1024]{3,2,1,0:T(8,128)(2,1)S(1)}, bf16[2,16,8,1024]{3,2,1,0:T(8,128)(2,1)}, u32[]{:S(2)}) copy-start(bf16[2,16,8,1024]{3,2,1,0:T(8,128)(2,1)} %get-tuple-element.83) | copy-start | bytes 1572868
  476.2 6.8 %copy-start = (f32[256,1024]{1,0:T(8,128)S(1)}, f32[256,1024]{1,0:T(8,128)}, u32[]{:S(2)}) copy-start(f32[256,1024]{1,0:T(8,128)} %get-tuple-element.143) | copy-start | bytes 3145732
